TPU v7x, 128 devices: a whole 4x4x4 slice. The times are simulated.
128 devices in a mesh: row: 16 (over y_hi, x, core), col: 8 (over y_lo, z).
Axes of the slice: x: 4, y: 4 (y_hi: 2, y_lo: 2; y = y_hi * 2 + y_lo), z: 4, core: 2. Of those that a mesh axis runs over, the one named last changes fastest.
Arguments:
- window_rows: bfloat16 [2048, 65536], P('row', 'col'), may hold values from -6 to 6
- omega_cols: bfloat16 [512, 2048], P(None, 'row'), may hold values from -0.125 to 0.125
- psi_rows: bfloat16 [65536, 1024], P(('col', 'row')), may hold values from -0.09375 to 0.09375
- upsilon_rows: bfloat16 [65536, 2048], P(('col', 'row')), may hold values from -0.09375 to 0.09375
- phi_cols: bfloat16 [2048, 2048], P(None, 'row'), may hold values from -0.125 to 0.125
- range_old: float32 [512, 65536], P(None, ('col', 'row')), may hold values from -6 to 6
- core_old: float32 [2048, 2048], P('row', 'col'), may hold values from -6 to 6
Outputs:
- range_sketch: float32 [512, 65536], P(None, ('col', 'row'))
- corange_sketch: float32 [2048, 1024], P('row', 'col')
- core_sketch: float32 [2048, 2048], P('row', 'col')
All inputs are finite; a program needn't handle non-finite values.
Results may differ from a plain program's by a relative error of at most 0.0022.
Values may be sent and summed in bfloat16 or wider, within the bound.
No kernel may reach another device: no remote copies, remote signals or barrier semaphores. Data moves between devices by JAX's collectives and lax.ppermute only.
A program may use at most 128 MiB of HBM per device.

v0:
```python
import jax
import jax.numpy as jnp
from jax import lax
from jax.sharding import Mesh, PartitionSpec as P


PLANE = ("yh", "x")
TILE = ("yh", "x", "yl")
WIRE = jnp.float16
NEAR = 64.0
FAR = 16.0


def shift(value, axis, by):
    n = lax.axis_size(axis)
    return lax.ppermute(value, axis, [(i, (i + by) % n) for i in range(n)])


def swap(value):
    return lax.ppermute(value, "k", [(0, 1), (1, 0)])


def dot(a, b):
    return jnp.dot(a, b, preferred_element_type=jnp.float32)


def after(value, *others):
    return lax.optimization_barrier((value,) + others)[0]


def body(window_rows, omega_cols, psi_rows, upsilon_rows, phi_cols, range_old, core_old):
    k = lax.axis_index("k")
    z = lax.axis_index("z")
    rows, cols = window_rows.shape
    own = cols // 16
    psi_other = swap(psi_rows)
    ups_other = swap(upsilon_rows)

    pieces = jnp.stack([window_rows[:, i * 2 * own : (i + 1) * 2 * own] for i in range(8)])
    relaid = lax.all_to_all(pieces, PLANE, 0, 0, tiled=True).reshape(8 * rows, 2 * own)

    def both(mine, theirs):
        return jnp.concatenate([jnp.where(k == 0, mine, theirs), jnp.where(k == 0, theirs, mine)], axis=0)

    wide = upsilon_rows.shape[1] // 8

    def part(at):
        start = (z + at) % 4 * wide
        cut = [
            jnp.concatenate(
                [lax.dynamic_slice_in_dim(u, start + yl * 4 * wide, wide, 1) for yl in range(2)], axis=1
            )
            for u in (upsilon_rows, ups_other)
        ]
        return both(*cut)

    b = [part(at) for at in range(4)]
    psi = both(psi_rows, psi_other)
    held = lax.optimization_barrier((relaid, psi) + tuple(b))
    relaid, psi, b = held[0], held[1], held[2:]
    sent = []
    for at in (2, 1, 3):
        share = (NEAR * dot(relaid, b[at])).astype(WIRE)
        sent.append(shift(share, "z", at))

    co = (NEAR * dot(relaid, psi)).astype(WIRE)
    co = lax.all_to_all(co.reshape(16, rows // 2, -1), TILE, 0, 0, tiled=True)
    mine = lax.optimization_barrier(dot(relaid, b[0]))
    co = jnp.sum(co.astype(jnp.float32), axis=0) * (1.0 / NEAR)

    small = jnp.concatenate(
        [jnp.broadcast_to(omega_cols[None], (8,) + omega_cols.shape), phi_cols.reshape(8, -1, phi_cols.shape[1])], axis=1
    )
    small = lax.all_to_all(after(small, co), PLANE, 0, 0, tiled=True)
    split = omega_cols.shape[0]
    omega = jnp.moveaxis(small[:, :split], 0, 1).reshape(split, -1)
    phi = jnp.moveaxis(small[:, split:], 0, 1).reshape(-1, 8 * phi_cols.shape[1])

    kept = lax.dynamic_slice_in_dim(relaid, k * own, own, 1)
    given = lax.dynamic_slice_in_dim(relaid, (1 - k) * own, own, 1)
    range_sketch = range_old + dot(omega, kept) + swap(dot(omega, given))

    narrow = co.shape[1] // 8
    co = jnp.stack([co[:, i * narrow : (i + 1) * narrow] for i in range(8)])
    co = lax.all_to_all(co, ("yl", "z"), 0, 0, tiled=True)
    co = co.reshape(2, 4, rows // 2, narrow)
    corange_sketch = jnp.concatenate([jnp.sum(co[0], axis=0), jnp.sum(co[1], axis=0)], axis=0)

    held = lax.optimization_barrier((mine, range_sketch, corange_sketch) + tuple(sent))
    mine, range_sketch, corange_sketch = held[:3]
    total = mine + (1.0 / NEAR) * sum(s.astype(jnp.float32) for s in held[3:])
    sk = (FAR * total).astype(WIRE).reshape(16, rows // 2, 2 * wide)
    sk = lax.all_to_all(sk, TILE, 0, 0, tiled=True)
    sk = (jnp.sum(sk.astype(jnp.float32), axis=0) * (1.0 / FAR)).astype(jnp.bfloat16)
    sk = jnp.stack([sk[:, :wide], sk[:, wide:]])
    sk = jnp.broadcast_to(sk[None], (8,) + sk.shape).reshape(16, rows // 2, wide)
    sk = lax.all_to_all(sk, TILE, 0, 0, tiled=True)
    term = dot(phi, sk.reshape(8 * rows, wide))
    here = lax.dynamic_slice_in_dim(term, k * rows, rows, 0)
    there = lax.dynamic_slice_in_dim(term, (1 - k) * rows, rows, 0)
    core_sketch = core_old + here + swap(there)
    return (range_sketch, corange_sketch, core_sketch)


def solution(mesh):
    fine = Mesh(mesh.devices.reshape(2, 4, 2, 2, 4), ("yh", "x", "k", "yl", "z"))
    row = ("yh", "x", "k")
    col = ("yl", "z")
    placed = (
        P(row, col),
        P(None, row),
        P(col + row, None),
        P(col + row, None),
        P(None, row),
        P(None, col + row),
        P(row, col),
    )
    return jax.shard_map(
        body,
        mesh=fine,
        in_specs=placed,
        out_specs=(P(None, col + row), P(row, col), P(row, col)),
        check_vma=False,
    )
```

profile of v0, /device:TPU:1, one launch (start us, length us, event | category | flops | bytes accessed | tf_op | source)
XLA Modules:
  0.0 180.0 jit_solution(10116990056530036011)
XLA Ops:
  0.6 1.5 collective-permute-start.1
  2.1 0.1 collective-permute-start
  2.2 1.7 bitcast_dynamic-update-slice_fusion.7
  3.9 1.7 bitcast_dynamic-update-slice_fusion.6
  5.6 1.7 bitcast_dynamic-update-slice_fusion.5
  7.2 1.7 bitcast_dynamic-update-slice_fusion.4
  8.9 1.7 bitcast_dynamic-update-slice_fusion.3
  10.6 1.7 bitcast_dynamic-update-slice_fusion.2
  12.2 1.7 bitcast_dynamic-update-slice_fusion.1
  13.9 1.7 bitcast_dynamic-update-slice_fusion
  15.5 6.8 %all-to-all-start = ((bf16[8,128,1024]{2,1,0:T(8,128)(2,1)}), bf16[8,128,1024]{2,1,0:T(8,128)(2,1)S(1)}, u32[]{:S(2)}, u32[]{:S(2)}) async-start(bf16[8,128,1024]{2,1,0:T(8,128)(2,1)} %bitcast_dynamic-update-slice_fusion), calls=%async_computation | async-start | bytes 4194304 | tf_op jit(solution)/shard_map/all_to_all | solution.py:40
  22.3 1.8 constant_dynamic-slice_fusion.4
  24.2 0.1 broadcast_select_fusion.1
  24.3 1.5 pad_maximum_fusion
  25.8 1.7 constant_dynamic-slice_fusion.2
  27.5 0.5 broadcast_select_fusion.3
  27.9 1.0 pad_maximum_fusion.5
  29.0 1.1 pad_maximum_fusion.4
  30.0 0.4 broadcast_select_fusion.7
  30.5 1.1 pad_maximum_fusion.3
  31.6 1.1 pad_maximum_fusion.2
  32.7 18.2 %all-to-all-done = bf16[8,128,1024]{2,1,0:T(8,128)(2,1)S(1)} async-done(((bf16[8,128,1024]{2,1,0:T(8,128)(2,1)}), bf16[8,128,1024]{2,1,0:T(8,128)(2,1)S(1)}, u32[]{:S(2)}, u32[]{:S(2)}) %all-to-all-start) | async-done | bytes 2097184 | tf_op jit(solution)/shard_map/all_to_all | solution.py:40
  50.9 6.0 %multiply_convert_fusion = f16[1024,1024]{1,0:T(8,128)(2,1)} fusion(bf16[1024,1024]{1,0:T(8,128)(2,1)S(1)} %bitcast.80, bf16[1024,1024]{1,0:T(8,128)(2,1)} %pad_maximum_fusion), kind=kOutput, calls=%fused_computation.1 | convolution fusion | flops 2149580800 | bytes 6291456 | tf_op jit(solution)/shard_map/dot_general | solution.py:24
  56.9 6.3 %all-to-all-start.1 = ((f16[16,64,1024]{2,1,0:T(8,128)(2,1)}), f16[16,64,1024]{2,1,0:T(8,128)(2,1)S(1)}, u32[]{:S(2)}, u32[]{:S(2)}) async-start(f16[16,64,1024]{2,1,0:T(8,128)(2,1)} %bitcast.88), calls=%async_computation.1 | async-start | bytes 4194304 | tf_op jit(solution)/shard_map/all_to_all | solution.py:67
  63.2 0.1 copy.13
  63.3 0.2 copy.14
  63.7 1.3 pad_maximum_fusion.1
  64.9 0.8 copy-done.1
  65.7 0.3 copy-done.6
  66.0 2.2 %multiply_convert_fusion.2 = f16[1024,512]{1,0:T(8,128)(2,1)} fusion(bf16[1024,1024]{1,0:T(8,128)(2,1)S(1)} %bitcast.84, bf16[1024,512]{1,0:T(8,128)(2,1)S(1)} %copy-done.6), kind=kOutput, calls=%fused_computation.5 | convolution fusion | flops 1074790400 | bytes 4194304 | tf_op jit(solution)/shard_map/dot_general | solution.py:24
  68.2 3.8 %collective-permute-start.5 = (f16[1024,512]{1,0:T(8,128)(2,1)}, f16[1024,512]{1,0:T(8,128)(2,1)}, u32[]{:S(2)}, u32[]{:S(2)}) collective-permute-start(f16[1024,512]{1,0:T(8,128)(2,1)} %multiply_convert_fusion.2), channel_id=1, source_target_pairs={{0,3},{1,0},{2,1},{3,2},{4,7},{5,4},{6,5},{7,6},{8,11},{9,8},{10,9... | collective-permute-start | bytes 3145736 | tf_op jit(solution)/shard_map/ppermute | solution.py:16
  72.0 2.2 %multiply_convert_fusion.3 = f16[1024,512]{1,0:T(8,128)(2,1)} fusion(bf16[1024,1024]{1,0:T(8,128)(2,1)S(1)} %bitcast.85, bf16[1024,512]{1,0:T(8,128)(2,1)S(1)} %copy-done.7), kind=kOutput, calls=%fused_computation.6 | convolution fusion | flops 1074790400 | bytes 4194304 | tf_op jit(solution)/shard_map/dot_general | solution.py:24
  74.2 16.5 %all-to-all-done.1 = f16[16,64,1024]{2,1,0:T(8,128)(2,1)S(1)} async-done(((f16[16,64,1024]{2,1,0:T(8,128)(2,1)}), f16[16,64,1024]{2,1,0:T(8,128)(2,1)S(1)}, u32[]{:S(2)}, u32[]{:S(2)}) %all-to-all-start.1) | async-done | bytes 2097184 | tf_op jit(solution)/shard_map/all_to_all | solution.py:67
  90.7 0.5 convert_reduce_fusion
  91.2 4.6 %all-to-all-start.2 = ((bf16[8,768,128]{1,2,0:T(8,128)(2,1)}), bf16[8,768,128]{1,2,0:T(8,128)(2,1)S(1)}, u32[]{:S(2)}, u32[]{:S(2)}) async-start(bf16[8,768,128]{1,2,0:T(8,128)(2,1)} %pad_maximum_fusion.1), calls=%async_computation.2 | async-start | bytes 3145728 | tf_op jit(solution)/shard_map/all_to_all | solution.py:74
  95.8 3.8 %multiply_convert_fusion.4 = f16[1024,512]{1,0:T(8,128)(2,1)} fusion(bf16[1024,1024]{1,0:T(8,128)(2,1)} %bitcast.81, bf16[1024,512]{1,0:T(8,128)(2,1)S(1)} %copy-done.5), kind=kOutput, calls=%fused_computation.7 | convolution fusion | flops 1074790400 | bytes 4194304 | tf_op jit(solution)/shard_map/dot_general | solution.py:24
  99.6 3.6 %collective-permute-start.3 = (f16[1024,512]{1,0:T(8,128)(2,1)}, f16[1024,512]{1,0:T(8,128)(2,1)}, u32[]{:S(2)}, u32[]{:S(2)}) collective-permute-start(f16[1024,512]{1,0:T(8,128)(2,1)} %multiply_convert_fusion.4), channel_id=1, source_target_pairs={{0,2},{1,3},{2,0},{3,1},{4,6},{5,7},{6,4},{7,5},{8,10},{9,11},{10,... | collective-permute-start | bytes 3145736 | tf_op jit(solution)/shard_map/ppermute | solution.py:16
  103.2 0.6 constant_dynamic-update-slice_fusion.7
  103.8 0.6 constant_dynamic-update-slice_fusion.6
  104.5 0.6 constant_dynamic-update-slice_fusion.5
  105.1 0.6 constant_dynamic-update-slice_fusion.4
  105.7 0.6 constant_dynamic-update-slice_fusion.3
  106.3 0.6 constant_dynamic-update-slice_fusion.2
  106.9 11.9 %all-to-all-done.2 = bf16[8,768,128]{1,2,0:T(8,128)(2,1)S(1)} async-done(((bf16[8,768,128]{1,2,0:T(8,128)(2,1)}), bf16[8,768,128]{1,2,0:T(8,128)(2,1)S(1)}, u32[]{:S(2)}, u32[]{:S(2)}) %all-to-all-start.2) | async-done | bytes 1572896 | tf_op jit(solution)/shard_map/all_to_all | solution.py:74
  118.9 1.5 copy-done.2
  120.4 1.7 fusion.1
  122.1 0.8 collective-permute-start.2
  122.9 0.6 constant_dynamic-update-slice_fusion.1
  123.5 0.6 constant_dynamic-update-slice_fusion
  124.1 5.0 %all-to-all-start.3 = ((f32[8,64,128]{2,1,0:T(8,128)}), f32[8,64,128]{2,1,0:T(8,128)S(1)}, u32[]{:S(2)}, u32[]{:S(2)}) async-start(f32[8,64,128]{2,1,0:T(8,128)} %constant_dynamic-update-slice_fusion), calls=%async_computation.3 | async-start | bytes 524288 | tf_op jit(solution)/shard_map/all_to_all | solution.py:85
  129.1 4.4 %fusion.6 = f32[1024,512]{1,0:T(8,128)} fusion(bf16[1024,1024]{1,0:T(8,128)(2,1)} %bitcast.82, bf16[1024,512]{1,0:T(8,128)(2,1)} %pad_maximum_fusion.2), kind=kOutput, calls=%fused_computation.88 | convolution fusion | flops 1073741824 | bytes 5242880 | tf_op jit(solution)/shard_map/dot_general | solution.py:24
  133.5 1.7 all-to-all-done.3
  135.3 0.6 pad_maximum_fusion.14
  135.9 3.7 %fusion = f32[512,512]{1,0:T(8,128)} fusion(f32[512,512]{1,0:T(8,128)} %collective-permute-done.2, f32[512,512]{1,0:T(8,128)} %param.12, bf16[512,1024]{0,1:T(8,128)(2,1)S(1)} %bitcast.79, bf16[1024,1024]{1,0:T(8,128)(2,1)} %bitcast.83, s32[]{:T(128)S(6)} %select_n.135), kind=kOutput, calls=%fused_computation.10 | convolution fusion | flops 537395200 | bytes 5242884 | tf_op jit(solution)/shard_map/dot_general | solution.py:24
  139.6 2.6 %multiply_convert_fusion.1 = f16[1024,512]{1,0:T(8,128)(2,1)S(1)} fusion(f32[1024,512]{1,0:T(8,128)S(1)} %copy-done.3, f16[1024,512]{1,0:T(8,128)(2,1)} %collective-permute-done.5, f16[1024,512]{1,0:T(8,128)(2,1)} %collective-permute-done.4, f16[1024,512]{1,0:T(8,128)(2,1)} %collective-permute-done.3), kind=kLoop, calls=%fused_computation.4 | loop fusion | flops 4718592 | bytes 6291456 | tf_op jit(solution)/shard_map/convert_element_type | solution.py:92
  142.3 18.4 %all_to_all.30 = f16[16,64,512]{2,1,0:T(8,128)(2,1)S(1)} all-to-all(f16[16,64,512]{2,1,0:T(8,128)(2,1)S(1)} %bitcast.87), channel_id=1, replica_groups=mesh['yh'=2,'x'=4,'k'=2,'yl'=2,'z'=4] {'yh','x','yl'}, dimensions={0} | all-to-all | bytes 2097152 | tf_op jit(solution)/shard_map/all_to_all | solution.py:93
  160.7 0.1 convert_reduce_fusion.1
  160.9 0.9 broadcast_in_dim.5
  161.7 3.6 %all-to-all-start.5 = ((bf16[16,64,256]{2,1,0:T(8,128)(2,1)}), bf16[16,64,256]{2,1,0:T(8,128)(2,1)S(1)}, u32[]{:S(2)}, u32[]{:S(2)}) async-start(bf16[16,64,256]{2,1,0:T(8,128)(2,1)} %bitcast.27), calls=%async_computation.5 | async-start | bytes 1048576 | tf_op jit(solution)/shard_map/all_to_all | solution.py:97
  165.3 9.2 %all-to-all-done.5 = bf16[16,64,256]{2,1,0:T(8,128)(2,1)S(1)} async-done(((bf16[16,64,256]{2,1,0:T(8,128)(2,1)}), bf16[16,64,256]{2,1,0:T(8,128)(2,1)S(1)}, u32[]{:S(2)}, u32[]{:S(2)}) %all-to-all-start.5) | async-done | bytes 524320 | tf_op jit(solution)/shard_map/all_to_all | solution.py:97
  174.6 0.3 fusion.7
  174.9 3.4 %collective-permute-start.6 = (f32[128,256]{1,0:T(8,128)S(1)}, f32[128,256]{1,0:T(8,128)S(1)}, u32[]{:S(2)}, u32[]{:S(2)}) collective-permute-start(f32[128,256]{1,0:T(8,128)S(1)} %constant_dynamic-slice_fusion), channel_id=1, source_target_pairs={{0,8},{8,0},{1,9},{9,1},{2,10},{10,2},{3,11},{11,3},{4,12},{12,4},... | collective-permute-start | bytes 393224 | tf_op jit(solution)/shard_map/ppermute | solution.py:20
  178.4 1.0 collective-permute-done.6
  179.4 0.7 add_add_fusion
  (35 shorter events, 0.4 us)
Async XLA Ops:
  0.6 25.2 %collective-permute-start.1 = (bf16[512,2048]{1,0:T(8,128)(2,1)}, bf16[512,2048]{1,0:T(8,128)(2,1)}, u32[]{:S(2)}, u32[]{:S(2)}) collective-permute-start(bf16[512,2048]{1,0:T(8,128)(2,1)} %param.10), channel_id=1, source_target_pairs={{0,8},{8,0},{1,9},{9,1},{2,10},{10,2},{3,11},{11,3},{4,12},{12,4},... | collective-permute-start | bytes 6291464 | tf_op jit(solution)/shard_map/ppermute | solution.py:20
  2.1 22.0 %collective-permute-start = (bf16[512,1024]{1,0:T(8,128)(2,1)}, bf16[512,1024]{1,0:T(8,128)(2,1)S(1)}, u32[]{:S(2)}, u32[]{:S(2)}) collective-permute-start(bf16[512,1024]{1,0:T(8,128)(2,1)} %param.9), channel_id=1, source_target_pairs={{0,8},{8,0},{1,9},{9,1},{2,10},{10,2},{3,11},{11,3},{4,12},{12,4},... | collective-permute-start | bytes 3145736 | tf_op jit(solution)/shard_map/ppermute | solution.py:20
  15.5 35.4 %all-to-all-start = ((bf16[8,128,1024]{2,1,0:T(8,128)(2,1)}), bf16[8,128,1024]{2,1,0:T(8,128)(2,1)S(1)}, u32[]{:S(2)}, u32[]{:S(2)}) async-start(bf16[8,128,1024]{2,1,0:T(8,128)(2,1)} %bitcast_dynamic-update-slice_fusion), calls=%async_computation | async-start | bytes 4194304 | tf_op jit(solution)/shard_map/all_to_all | solution.py:40
  22.3 1.9 %copy-start.4 = (bf16[512,1024]{1,0:T(8,128)(2,1)S(1)}, bf16[512,1024]{1,0:T(8,128)(2,1)}, u32[]{:S(2)}) copy-start(bf16[512,1024]{1,0:T(8,128)(2,1)} %param.9) | copy-start | bytes 3145732
  50.9 6.0 %copy-start = (bf16[8,128,1024]{2,1,0:T(8,128)(2,1)}, bf16[8,128,1024]{2,1,0:T(8,128)(2,1)S(1)}, u32[]{:S(2)}) copy-start(bf16[8,128,1024]{2,1,0:T(8,128)(2,1)S(1)} %all-to-all-done) | copy-start | bytes 6291460
  56.9 6.3 %copy-start.10 = (bf16[512,128]{1,0:T(8,128)(2,1)S(1)}, bf16[512,128]{1,0:T(8,128)(2,1)}, u32[]{:S(2)}) copy-start(bf16[512,128]{1,0:T(8,128)(2,1)} %param.8) | copy-start | bytes 393220
  56.9 6.4 %copy-start.8 = (bf16[2048,128]{1,0:T(8,128)(2,1)S(1)}, bf16[2048,128]{1,0:T(8,128)(2,1)}, u32[]{:S(2)}) copy-start(bf16[2048,128]{1,0:T(8,128)(2,1)} %param.11) | copy-start | bytes 1572868
  56.9 33.8 %all-to-all-start.1 = ((f16[16,64,1024]{2,1,0:T(8,128)(2,1)}), f16[16,64,1024]{2,1,0:T(8,128)(2,1)S(1)}, u32[]{:S(2)}, u32[]{:S(2)}) async-start(f16[16,64,1024]{2,1,0:T(8,128)(2,1)} %bitcast.88), calls=%async_computation.1 | async-start | bytes 4194304 | tf_op jit(solution)/shard_map/all_to_all | solution.py:67
  63.6 2.2 %copy-start.1 = (bf16[8,128,1024]{2,1,0:T(8,128)(2,1)S(1)}, bf16[8,128,1024]{2,1,0:T(8,128)(2,1)}, u32[]{:S(2)}) copy-start(bf16[8,128,1024]{2,1,0:T(8,128)(2,1)} %copy-done) | copy-start | bytes 6291460
  63.6 2.4 %copy-start.6 = (bf16[1024,512]{1,0:T(8,128)(2,1)S(1)}, bf16[1024,512]{1,0:T(8,128)(2,1)}, u32[]{:S(2)}) copy-start(bf16[1024,512]{1,0:T(8,128)(2,1)} %pad_maximum_fusion.5) | copy-start | bytes 3145732
  66.0 6.0 %copy-start.7 = (bf16[1024,512]{1,0:T(8,128)(2,1)S(1)}, bf16[1024,512]{1,0:T(8,128)(2,1)}, u32[]{:S(2)}) copy-start(bf16[1024,512]{1,0:T(8,128)(2,1)} %pad_maximum_fusion.3) | copy-start | bytes 3145732
  68.2 71.4 %collective-permute-start.5 = (f16[1024,512]{1,0:T(8,128)(2,1)}, f16[1024,512]{1,0:T(8,128)(2,1)}, u32[]{:S(2)}, u32[]{:S(2)}) collective-permute-start(f16[1024,512]{1,0:T(8,128)(2,1)} %multiply_convert_fusion.2), channel_id=1, source_target_pairs={{0,3},{1,0},{2,1},{3,2},{4,7},{5,4},{6,5},{7,6},{8,11},{9,8},{10,9... | collective-permute-start | bytes 3145736 | tf_op jit(solution)/shard_map/ppermute | solution.py:16
  74.2 65.4 %collective-permute-start.4 = (f16[1024,512]{1,0:T(8,128)(2,1)}, f16[1024,512]{1,0:T(8,128)(2,1)}, u32[]{:S(2)}, u32[]{:S(2)}) collective-permute-start(f16[1024,512]{1,0:T(8,128)(2,1)} %multiply_convert_fusion.3), channel_id=1, source_target_pairs={{0,1},{1,2},{2,3},{3,0},{4,5},{5,6},{6,7},{7,4},{8,9},{9,10},{10,1... | collective-permute-start | bytes 3145736 | tf_op jit(solution)/shard_map/ppermute | solution.py:16
  91.2 4.6 %copy-start.5 = (bf16[1024,512]{1,0:T(8,128)(2,1)S(1)}, bf16[1024,512]{1,0:T(8,128)(2,1)}, u32[]{:S(2)}) copy-start(bf16[1024,512]{1,0:T(8,128)(2,1)} %pad_maximum_fusion.4) | copy-start | bytes 3145732
  91.2 27.6 %all-to-all-start.2 = ((bf16[8,768,128]{1,2,0:T(8,128)(2,1)}), bf16[8,768,128]{1,2,0:T(8,128)(2,1)S(1)}, u32[]{:S(2)}, u32[]{:S(2)}) async-start(bf16[8,768,128]{1,2,0:T(8,128)(2,1)} %pad_maximum_fusion.1), calls=%async_computation.2 | async-start | bytes 3145728 | tf_op jit(solution)/shard_map/all_to_all | solution.py:74
  99.6 40.0 %collective-permute-start.3 = (f16[1024,512]{1,0:T(8,128)(2,1)}, f16[1024,512]{1,0:T(8,128)(2,1)}, u32[]{:S(2)}, u32[]{:S(2)}) collective-permute-start(f16[1024,512]{1,0:T(8,128)(2,1)} %multiply_convert_fusion.4), channel_id=1, source_target_pairs={{0,2},{1,3},{2,0},{3,1},{4,6},{5,7},{6,4},{7,5},{8,10},{9,11},{10,... | collective-permute-start | bytes 3145736 | tf_op jit(solution)/shard_map/ppermute | solution.py:16
  118.8 1.6 copy-start.2
  122.1 13.8 %collective-permute-start.2 = (f32[512,512]{1,0:T(8,128)}, f32[512,512]{1,0:T(8,128)}, u32[]{:S(2)}, u32[]{:S(2)}) collective-permute-start(f32[512,512]{1,0:T(8,128)} %fusion.1), channel_id=1, source_target_pairs={{0,8},{8,0},{1,9},{9,1},{2,10},{10,2},{3,11},{11,3},{4,12},{12,4},... | collective-permute-start | bytes 3145736 | tf_op jit(solution)/shard_map/ppermute | solution.py:20
  124.1 11.2 %all-to-all-start.3 = ((f32[8,64,128]{2,1,0:T(8,128)}), f32[8,64,128]{2,1,0:T(8,128)S(1)}, u32[]{:S(2)}, u32[]{:S(2)}) async-start(f32[8,64,128]{2,1,0:T(8,128)} %constant_dynamic-update-slice_fusion), calls=%async_computation.3 | async-start | bytes 524288 | tf_op jit(solution)/shard_map/all_to_all | solution.py:85
  135.9 3.7 %copy-start.3 = (f32[1024,512]{1,0:T(8,128)S(1)}, f32[1024,512]{1,0:T(8,128)}, u32[]{:S(2)}) copy-start(f32[1024,512]{1,0:T(8,128)} %fusion.6) | copy-start | bytes 6291460
  160.8 18.5 %copy-start.9 = (f32[128,256]{1,0:T(8,128)S(1)}, f32[128,256]{1,0:T(8,128)}, u32[]{:S(2)}) copy-start(f32[128,256]{1,0:T(8,128)} %param.13) | copy-start | bytes 393220
  161.7 12.8 %all-to-all-start.5 = ((bf16[16,64,256]{2,1,0:T(8,128)(2,1)}), bf16[16,64,256]{2,1,0:T(8,128)(2,1)S(1)}, u32[]{:S(2)}, u32[]{:S(2)}) async-start(bf16[16,64,256]{2,1,0:T(8,128)(2,1)} %bitcast.27), calls=%async_computation.5 | async-start | bytes 1048576 | tf_op jit(solution)/shard_map/all_to_all | solution.py:97
  174.9 4.4 %collective-permute-start.6 = (f32[128,256]{1,0:T(8,128)S(1)}, f32[128,256]{1,0:T(8,128)S(1)}, u32[]{:S(2)}, u32[]{:S(2)}) collective-permute-start(f32[128,256]{1,0:T(8,128)S(1)} %constant_dynamic-slice_fusion), channel_id=1, source_target_pairs={{0,8},{8,0},{1,9},{9,1},{2,10},{10,2},{3,11},{11,3},{4,12},{12,4},... | collective-permute-start | bytes 393224 | tf_op jit(solution)/shard_map/ppermute | solution.py:20
where the time goes:
time: 181 us; the launch traced here: 180 us
  waiting for transfers between devices  58.5 us (32%)
  starting transfers between devices  39.4 us (22%)
  local copies, waits for them, and re-layouts  25.7 us (14%)
  matrix products  24.5 us (14%)
  blocking collectives  18.4 us (10%)
  other arithmetic  12.7 us (7%)
    dot_general x8, matrix products, dot(): return jnp.dot(a, b, preferred_element_type=jnp.float32)  24.5 us
    unnamed x37, local copies, waits for them, and re-layouts  18.7 us
    all_to_all x1, blocking collectives, body(): sk = lax.all_to_all(sk, TILE, 0, 0, tiled=True)  18.4 us
    all_to_all x1, waiting for transfers between devices, body(): lax.all_to_all(pieces, PLANE, 0, 0, tiled=True).reshape(8 * rows, 2 * own)  18.2 us
    all_to_all x1, waiting for transfers between devices, body(): co = lax.all_to_all(co.reshape(16, rows // 2, -1), TILE, 0, 0, tiled=True)  16.5 us
    all_to_all x1, waiting for transfers between devices, body(): small = lax.all_to_all(after(small, co), PLANE, 0, 0, tiled=True)  11.9 us
    all_to_all x1, waiting for transfers between devices, body(): sk = lax.all_to_all(sk, TILE, 0, 0, tiled=True)  9.21 us
    ppermute x3, starting transfers between devices, shift(): return lax.ppermute(value, axis, [(i, (i + by) % n) for i in range(n)])  7.36 us
  transfers between devices with their start and end apart: 12, of which 6 were waited for; matrix products, arithmetic and copies ran while one was open for 28% of the time, Pallas kernels for 0%

commit v1 on v0

v1 whole, which is shorter than its diff:
```python
import jax
import jax.numpy as jnp
from jax import lax
from jax.experimental import pallas as pl
from jax.sharding import Mesh, PartitionSpec as P


PLANE = ("yh", "x")
TILE = ("yh", "x", "yl")
WIRE = jnp.float16
NEAR = 64.0
FAR = 16.0


def shift(value, axis, by):
    n = lax.axis_size(axis)
    return lax.ppermute(value, axis, [(i, (i + by) % n) for i in range(n)])


def swap(value, axis="k"):
    return lax.ppermute(value, axis, [(0, 1), (1, 0)])


def dot(a, b):
    return jnp.dot(a, b, preferred_element_type=jnp.float32)


def tied(*values):
    return lax.optimization_barrier(values)


def cut_columns(value, count):
    rows, cols = value.shape
    wide = cols // count

    def move(src, dst):
        dst[0] = src[...]

    return pl.pallas_call(
        move,
        grid=(count,),
        in_specs=[pl.BlockSpec((rows, wide), lambda i: (0, i))],
        out_specs=pl.BlockSpec((1, rows, wide), lambda i: (i, 0, 0)),
        out_shape=jax.ShapeDtypeStruct((count, rows, wide), value.dtype),
    )(value)


def exchange(value, axes):
    return lax.all_to_all(value, axes, 0, 0, tiled=True)


def body(window_rows, omega_cols, psi_rows, upsilon_rows, phi_cols, range_old, core_old):
    k = lax.axis_index("k")
    z = lax.axis_index("z")
    yl = lax.axis_index("yl")
    rows, cols = window_rows.shape
    own = cols // 16
    ups_other = swap(upsilon_rows)
    psi_other = swap(psi_rows)

    relaid = exchange(cut_columns(window_rows, 8), PLANE).reshape(8 * rows, 2 * own)

    def both(mine, theirs):
        return jnp.concatenate([jnp.where(k == 0, mine, theirs), jnp.where(k == 0, theirs, mine)], axis=0)

    def pick(value, at, wide):
        start = (z + at) % 4 * wide
        return jnp.concatenate(
            [lax.dynamic_slice_in_dim(value, start + half * 4 * wide, wide, 1) for half in range(2)], axis=1
        )

    wide = upsilon_rows.shape[1] // 8
    b = [both(pick(upsilon_rows, at, wide), pick(ups_other, at, wide)) for at in range(4)]
    psi = both(psi_rows, psi_other)
    split = omega_cols.shape[0]
    small = jnp.concatenate(
        [jnp.broadcast_to(omega_cols[None], (8,) + omega_cols.shape), phi_cols.reshape(8, -1, phi_cols.shape[1])], axis=1
    )
    relaid, psi, small, *b = tied(relaid, psi, small, *b)

    small = exchange(small, PLANE)
    sent = []
    for at in (2, 1, 3):
        share = (NEAR * dot(relaid, b[at])).astype(WIRE)
        sent.append(shift(share, "z", at))

    co = (NEAR * dot(relaid, psi)).astype(WIRE)
    co, small = tied(co, small)
    co = exchange(co.reshape(16, rows // 2, -1), TILE)
    mine = dot(relaid, b[0])
    co = jnp.sum(co.astype(jnp.float32), axis=0) * (1.0 / NEAR)

    mine, co, *sent = tied(mine, co, *sent)
    total = mine + (1.0 / NEAR) * sum(s.astype(jnp.float32) for s in sent)
    sk = (FAR * total).astype(WIRE).reshape(16, rows // 2, 2 * wide)
    sk = exchange(sk, TILE)

    omega = jnp.moveaxis(small[:, :split], 0, 1).reshape(split, -1)
    phi = jnp.moveaxis(small[:, split:], 0, 1).reshape(-1, 8 * phi_cols.shape[1])
    kept = lax.dynamic_slice_in_dim(relaid, k * own, own, 1)
    given = lax.dynamic_slice_in_dim(relaid, (1 - k) * own, own, 1)
    range_given = dot(omega, given)
    range_kept = dot(omega, kept)
    range_sketch = range_old + range_kept + swap(range_given)

    narrow = co.shape[1] // 8
    others = [shift(pick(co, at, narrow), "z", at) for at in (2, 1, 3)]
    co = pick(co, 0, narrow) + others[0] + others[1] + others[2]
    co_kept = lax.dynamic_slice_in_dim(co, yl * narrow, narrow, 1)
    co_other = swap(lax.dynamic_slice_in_dim(co, (1 - yl) * narrow, narrow, 1), "yl")
    corange_sketch = jnp.concatenate(
        [jnp.where(yl == 0, co_kept, co_other), jnp.where(yl == 0, co_other, co_kept)], axis=0
    )

    sk = (jnp.sum(sk.astype(jnp.float32), axis=0) * (1.0 / FAR)).astype(jnp.bfloat16)
    sk = jnp.stack([sk[:, :wide], sk[:, wide:]])
    sk = jnp.broadcast_to(sk[None], (8,) + sk.shape).reshape(16, rows // 2, wide)
    sk = exchange(sk, TILE)
    term = dot(phi, sk.reshape(8 * rows, wide))
    here = lax.dynamic_slice_in_dim(term, k * rows, rows, 0)
    there = lax.dynamic_slice_in_dim(term, (1 - k) * rows, rows, 0)
    core_sketch = core_old + here + swap(there)
    return (range_sketch, corange_sketch, core_sketch)


def solution(mesh):
    fine = Mesh(mesh.devices.reshape(2, 4, 2, 2, 4), ("yh", "x", "k", "yl", "z"))
    row = ("yh", "x", "k")
    col = ("yl", "z")
    placed = (
        P(row, col),
        P(None, row),
        P(col + row, None),
        P(col + row, None),
        P(None, row),
        P(None, col + row),
        P(row, col),
    )
    return jax.shard_map(
        body,
        mesh=fine,
        in_specs=placed,
        out_specs=(P(None, col + row), P(row, col), P(row, col)),
        check_vma=False,
    )
```

time: 181 us -> 186 us (1.028)
  waiting for transfers between devices: 58.5 us -> 84.5 us
  blocking collectives: 18.4 us -> 0 us
  local copies, waits for them, and re-layouts: 25.7 us -> 9.12 us
  starting transfers between devices: 39.4 us -> 46 us
  Pallas kernels: 0 us -> 5.63 us
  other arithmetic: 12.7 us -> 15.9 us
    ppermute x3 -> x6, waiting for transfers between devices: 0.01 us -> 27.4 us  [shift(): return lax.ppermute(value, axis, [(i, (i + by) % n) for i in range(n)])]
    all_to_all x1 -> x0, blocking collectives: 18.4 us -> none  [body(): sk = lax.all_to_all(sk, TILE, 0, 0, tiled=True)]
    unnamed x37 -> x29, local copies, waits for them, and re-layouts: 18.7 us -> 5.89 us
    pallas_call x0 -> x1, Pallas kernels: none -> 5.63 us  [cut_columns(): pl.pallas_call(move, grid=(count,), in_specs=[pl.BlockSpec((rows, wide),...]
    ppermute x3 -> x6, starting transfers between devices: 7.36 us -> 10.8 us  [shift(): return lax.ppermute(value, axis, [(i, (i + by) % n) for i in range(n)])]
    ppermute x4 -> x5, starting transfers between devices: 5.79 us -> 8.24 us  [swap(): return lax.ppermute(value, axis, [(0, 1), (1, 0)])]
    another operation x2 -> x0, local copies, waits for them, and re-layouts: 2.26 us -> none  [the longest x1 1.66 us: body(): jnp.stack([window_rows[:, i * 2 * own:(i + 1) * 2 * own] for i in range(8)])]
  transfers between devices with their start and end apart: 12 -> 16, of which waited for: 6 -> 8; matrix products, arithmetic and copies ran while one was open for 28% -> 20% of each run, Pallas kernels for 0% -> 3%
where the time goes in v1:
time: 186 us; the launch traced here: 185 us
  waiting for transfers between devices  84.5 us (45%)
  starting transfers between devices  46 us (25%)
  matrix products  22.7 us (12%)
  other arithmetic  15.9 us (9%)
  local copies, waits for them, and re-layouts  9.12 us (5%)
  Pallas kernels  5.63 us (3%)
    all_to_all x5, waiting for transfers between devices, exchange(): return lax.all_to_all(value, axes, 0, 0, tiled=True)  56.8 us
    ppermute x6, waiting for transfers between devices, shift(): return lax.ppermute(value, axis, [(i, (i + by) % n) for i in range(n)])  27.4 us
    all_to_all x5, starting transfers between devices, exchange(): return lax.all_to_all(value, axes, 0, 0, tiled=True)  27 us
    dot_general x8, matrix products, dot(): return jnp.dot(a, b, preferred_element_type=jnp.float32)  22.7 us
    ppermute x6, starting transfers between devices, shift(): return lax.ppermute(value, axis, [(i, (i + by) % n) for i in range(n)])  10.8 us
    ppermute x5, starting transfers between devices, swap(): return lax.ppermute(value, axis, [(0, 1), (1, 0)])  8.24 us
    unnamed x29, local copies, waits for them, and re-layouts  5.89 us
    pallas_call x1, Pallas kernels, cut_columns(): pl.pallas_call(move, grid=(count,), in_specs=[pl.BlockSpec((rows, wide),...  5.63 us
  transfers between devices with their start and end apart: 16, of which 8 were waited for; matrix products, arithmetic and copies ran while one was open for 20% of the time, Pallas kernels for 3%

profile of v1, /device:TPU:1, one launch (start us, length us, event | category | flops | bytes accessed | tf_op | source)
XLA Modules:
  0.0 184.8 jit_solution(8173301515950871916)
XLA Ops:
  0.6 1.5 collective-permute-start.1
  2.1 0.1 collective-permute-start
  2.2 5.6 %shard_map.94 = bf16[8,128,1024]{2,1,0:T(8,128)(2,1)} custom-call(bf16[128,8192]{1,0:T(8,128)(2,1)} %src.1), custom_call_target="tpu_custom_call" | custom-call | tf_op jit(solution)/shard_map/pallas_call | solution.py:39
  7.8 6.9 %all-to-all-start = ((bf16[8,128,1024]{2,1,0:T(8,128)(2,1)}), bf16[8,128,1024]{2,1,0:T(8,128)(2,1)S(1)}, u32[]{:S(2)}, u32[]{:S(2)}) async-start(bf16[8,128,1024]{2,1,0:T(8,128)(2,1)} %shard_map.94), calls=%async_computation | async-start | bytes 4194304 | tf_op jit(solution)/shard_map/all_to_all | solution.py:49
  14.7 0.1 copy.11
  14.9 0.2 copy.12
  15.1 0.0 copy-start.7
  15.1 0.1 broadcast_in_dim.4
  15.2 1.3 pad_maximum_fusion.1
  16.5 0.8 copy-done.7
  17.3 0.3 constant_dynamic-slice_fusion.13
  17.6 0.0 collective-permute-done
  17.6 0.9 copy-done.8
  18.5 1.4 broadcast_select_fusion.1
  19.9 1.6 pad_maximum_fusion
  21.4 1.7 constant_dynamic-slice_fusion.11
  23.1 0.5 broadcast_select_fusion.7
  23.6 0.1 pad_maximum_fusion.3
  23.7 0.5 broadcast_select_fusion.3
  24.1 1.1 pad_maximum_fusion.5
  25.2 1.0 pad_maximum_fusion.4
  26.2 1.0 pad_maximum_fusion.2
  27.2 16.1 %all-to-all-done = bf16[8,128,1024]{2,1,0:T(8,128)(2,1)S(1)} async-done(((bf16[8,128,1024]{2,1,0:T(8,128)(2,1)}), bf16[8,128,1024]{2,1,0:T(8,128)(2,1)S(1)}, u32[]{:S(2)}, u32[]{:S(2)}) %all-to-all-start) | async-done | bytes 2097184 | tf_op jit(solution)/shard_map/all_to_all | solution.py:49
  43.3 1.4 copy-done.2
  44.7 6.0 %all-to-all-start.1 = ((bf16[8,768,128]{1,2,0:T(8,128)(2,1)}), bf16[8,768,128]{1,2,0:T(8,128)(2,1)S(1)}, u32[]{:S(2)}, u32[]{:S(2)}) async-start(bf16[8,768,128]{1,2,0:T(8,128)(2,1)} %pad_maximum_fusion.1), calls=%async_computation.1 | async-start | bytes 3145728 | tf_op jit(solution)/shard_map/all_to_all | solution.py:49
  50.7 5.9 %multiply_convert_fusion = f16[1024,1024]{1,0:T(8,128)(2,1)} fusion(bf16[1024,1024]{1,0:T(8,128)(2,1)} %bitcast.33, bf16[1024,1024]{1,0:T(8,128)(2,1)} %pad_maximum_fusion), kind=kOutput, calls=%fused_computation.1 | convolution fusion | flops 2149580800 | bytes 6291456 | tf_op jit(solution)/shard_map/dot_general | solution.py:25
  56.6 17.1 %all-to-all-done.1 = bf16[8,768,128]{1,2,0:T(8,128)(2,1)S(1)} async-done(((bf16[8,768,128]{1,2,0:T(8,128)(2,1)}), bf16[8,768,128]{1,2,0:T(8,128)(2,1)S(1)}, u32[]{:S(2)}, u32[]{:S(2)}) %all-to-all-start.1) | async-done | bytes 1572896 | tf_op jit(solution)/shard_map/all_to_all | solution.py:49
  73.7 1.2 copy-done
  74.9 3.7 %all-to-all-start.2 = ((f16[16,64,1024]{2,1,0:T(8,128)(2,1)}), f16[16,64,1024]{2,1,0:T(8,128)(2,1)S(1)}, u32[]{:S(2)}, u32[]{:S(2)}) async-start(f16[16,64,1024]{2,1,0:T(8,128)(2,1)} %bitcast.40), calls=%async_computation.2 | async-start | bytes 4194304 | tf_op jit(solution)/shard_map/all_to_all | solution.py:49
  78.6 4.3 %multiply_convert_fusion.2 = f16[1024,512]{1,0:T(8,128)(2,1)} fusion(bf16[1024,1024]{1,0:T(8,128)(2,1)} %bitcast.34, bf16[1024,512]{1,0:T(8,128)(2,1)} %pad_maximum_fusion.5), kind=kOutput, calls=%fused_computation.5 | convolution fusion | flops 1074790400 | bytes 4194304 | tf_op jit(solution)/shard_map/dot_general | solution.py:25
  82.9 2.3 %multiply_convert_fusion.3 = f16[1024,512]{1,0:T(8,128)(2,1)} fusion(bf16[1024,1024]{1,0:T(8,128)(2,1)S(1)} %bitcast.36, bf16[1024,512]{1,0:T(8,128)(2,1)S(1)} %pad_maximum_fusion.3), kind=kOutput, calls=%fused_computation.6 | convolution fusion | flops 1074790400 | bytes 4194304 | tf_op jit(solution)/shard_map/dot_general | solution.py:25
  85.2 2.2 %multiply_convert_fusion.4 = f16[1024,512]{1,0:T(8,128)(2,1)} fusion(bf16[1024,1024]{1,0:T(8,128)(2,1)S(1)} %bitcast.37, bf16[1024,512]{1,0:T(8,128)(2,1)S(1)} %copy-done.10), kind=kOutput, calls=%fused_computation.7 | convolution fusion | flops 1074790400 | bytes 4194304 | tf_op jit(solution)/shard_map/dot_general | solution.py:25
  87.4 3.6 %collective-permute-start.3 = (f16[1024,512]{1,0:T(8,128)(2,1)}, f16[1024,512]{1,0:T(8,128)(2,1)}, u32[]{:S(2)}, u32[]{:S(2)}) collective-permute-start(f16[1024,512]{1,0:T(8,128)(2,1)} %multiply_convert_fusion.4), channel_id=1, source_target_pairs={{0,2},{1,3},{2,0},{3,1},{4,6},{5,7},{6,4},{7,5},{8,10},{9,11},{10,... | collective-permute-start | bytes 3145736 | tf_op jit(solution)/shard_map/ppermute | solution.py:17
  91.0 0.7 collective-permute-start.4
  91.8 1.9 %collective-permute-start.5 = (f16[1024,512]{1,0:T(8,128)(2,1)}, f16[1024,512]{1,0:T(8,128)(2,1)}, u32[]{:S(2)}, u32[]{:S(2)}) collective-permute-start(f16[1024,512]{1,0:T(8,128)(2,1)} %multiply_convert_fusion.2), channel_id=1, source_target_pairs={{0,3},{1,0},{2,1},{3,2},{4,7},{5,4},{6,5},{7,6},{8,11},{9,8},{10,9... | collective-permute-start | bytes 3145736 | tf_op jit(solution)/shard_map/ppermute | solution.py:17
  93.7 2.6 %fusion.8 = f32[1024,512]{1,0:T(8,128)} fusion(bf16[1024,1024]{1,0:T(8,128)(2,1)S(1)} %bitcast.38, bf16[1024,512]{1,0:T(8,128)(2,1)S(1)} %copy-done.9), kind=kOutput, calls=%fused_computation.79 | convolution fusion | flops 1073741824 | bytes 5242880 | tf_op jit(solution)/shard_map/dot_general | solution.py:25
  96.3 13.2 %all-to-all-done.2 = f16[16,64,1024]{2,1,0:T(8,128)(2,1)S(1)} async-done(((f16[16,64,1024]{2,1,0:T(8,128)(2,1)}), f16[16,64,1024]{2,1,0:T(8,128)(2,1)S(1)}, u32[]{:S(2)}, u32[]{:S(2)}) %all-to-all-start.2) | async-done | bytes 2097184 | tf_op jit(solution)/shard_map/all_to_all | solution.py:49
  109.6 0.5 convert_reduce_fusion
  110.1 4.0 %collective-permute-done.3 = f16[1024,512]{1,0:T(8,128)(2,1)} collective-permute-done((f16[1024,512]{1,0:T(8,128)(2,1)}, f16[1024,512]{1,0:T(8,128)(2,1)}, u32[]{:S(2)}, u32[]{:S(2)}) %collective-permute-start.3) | collective-permute-done | bytes 1048608 | tf_op jit(solution)/shard_map/ppermute | solution.py:17
  114.1 23.3 %collective-permute-done.4 = f16[1024,512]{1,0:T(8,128)(2,1)} collective-permute-done((f16[1024,512]{1,0:T(8,128)(2,1)}, f16[1024,512]{1,0:T(8,128)(2,1)}, u32[]{:S(2)}, u32[]{:S(2)}) %collective-permute-start.4) | collective-permute-done | bytes 1048608 | tf_op jit(solution)/shard_map/ppermute | solution.py:17
  137.4 3.7 %multiply_convert_fusion.1 = f16[1024,512]{1,0:T(8,128)(2,1)} fusion(f32[1024,512]{1,0:T(8,128)S(1)} %copy-done.6, f16[1024,512]{1,0:T(8,128)(2,1)} %collective-permute-done.5, f16[1024,512]{1,0:T(8,128)(2,1)} %collective-permute-done.4, f16[1024,512]{1,0:T(8,128)(2,1)} %collective-permute-done.3), kind=kLoop, calls=%fused_computation.4 | loop fusion | flops 4718592 | bytes 6291456 | tf_op jit(solution)/shard_map/convert_element_type | solution.py:95
  141.1 6.8 %all-to-all-start.3 = ((f16[16,64,512]{2,1,0:T(8,128)(2,1)}), f16[16,64,512]{2,1,0:T(8,128)(2,1)}, u32[]{:S(2)}, u32[]{:S(2)}) async-start(f16[16,64,512]{2,1,0:T(8,128)(2,1)} %bitcast.8), calls=%async_computation.3 | async-start | bytes 2097152 | tf_op jit(solution)/shard_map/all_to_all | solution.py:49
  148.0 0.1 slice.12
  148.1 1.5 copy-done.4
  149.6 1.7 fusion.1
  151.3 1.6 collective-permute-start.2
  152.9 1.8 collective-permute-start.6
  154.8 1.2 collective-permute-start.7
  155.9 0.6 pad_maximum_fusion.16
  156.6 1.5 collective-permute-start.8
  158.1 5.8 %all-to-all-done.3 = f16[16,64,512]{2,1,0:T(8,128)(2,1)} async-done(((f16[16,64,512]{2,1,0:T(8,128)(2,1)}), f16[16,64,512]{2,1,0:T(8,128)(2,1)}, u32[]{:S(2)}, u32[]{:S(2)}) %all-to-all-start.3) | async-done | bytes 1048608 | tf_op jit(solution)/shard_map/all_to_all | solution.py:49
  163.9 1.4 convert_reduce_fusion.1
  165.3 0.8 broadcast_in_dim.5
  166.1 3.6 %all-to-all-start.4 = ((bf16[16,64,256]{2,1,0:T(8,128)(2,1)}), bf16[16,64,256]{2,1,0:T(8,128)(2,1)S(1)}, u32[]{:S(2)}, u32[]{:S(2)}) async-start(bf16[16,64,256]{2,1,0:T(8,128)(2,1)} %bitcast.11), calls=%async_computation.4 | async-start | bytes 1048576 | tf_op jit(solution)/shard_map/all_to_all | solution.py:49
  169.7 0.0 slice-start
  169.7 0.0 collective-permute-done.2
  169.7 3.3 %fusion = f32[512,512]{1,0:T(8,128)} fusion(f32[512,512]{1,0:T(8,128)} %collective-permute-done.2, f32[512,512]{1,0:T(8,128)S(1)} %copy-done.5, bf16[512,1024]{0,1:T(8,128)(2,1)S(1)} %bitcast.31, bf16[1024,1024]{1,0:T(8,128)(2,1)} %bitcast.35, s32[]{:T(128)S(6)} %select_n.193), kind=kOutput, calls=%fused_computation.10 | convolution fusion | flops 537395200 | bytes 5242884 | tf_op jit(solution)/shard_map/dot_general | solution.py:25
  173.1 1.3 collective-permute-start.9
  174.4 4.5 %all-to-all-done.4 = bf16[16,64,256]{2,1,0:T(8,128)(2,1)S(1)} async-done(((bf16[16,64,256]{2,1,0:T(8,128)(2,1)}), bf16[16,64,256]{2,1,0:T(8,128)(2,1)S(1)}, u32[]{:S(2)}, u32[]{:S(2)}) %all-to-all-start.4) | async-done | bytes 524320 | tf_op jit(solution)/shard_map/all_to_all | solution.py:49
  179.0 0.3 fusion.9
  179.3 3.8 %collective-permute-start.10 = (f32[128,256]{1,0:T(8,128)S(1)}, f32[128,256]{1,0:T(8,128)S(1)}, u32[]{:S(2)}, u32[]{:S(2)}) collective-permute-start(f32[128,256]{1,0:T(8,128)S(1)} %constant_dynamic-slice_fusion), channel_id=1, source_target_pairs={{0,8},{8,0},{1,9},{9,1},{2,10},{10,2},{3,11},{11,3},{4,12},{12,4},... | collective-permute-start | bytes 393224 | tf_op jit(solution)/shard_map/ppermute | solution.py:21
  183.2 0.6 pad_maximum_fusion.17
  183.8 0.3 collective-permute-done.10
  184.1 0.7 add_add_fusion
  (40 shorter events, 0.2 us)
Async XLA Ops:
  0.6 20.8 %collective-permute-start.1 = (bf16[512,2048]{1,0:T(8,128)(2,1)}, bf16[512,2048]{1,0:T(8,128)(2,1)}, u32[]{:S(2)}, u32[]{:S(2)}) collective-permute-start(bf16[512,2048]{1,0:T(8,128)(2,1)} %param.10), channel_id=1, source_target_pairs={{0,8},{8,0},{1,9},{9,1},{2,10},{10,2},{3,11},{11,3},{4,12},{12,4},... | collective-permute-start | bytes 6291464 | tf_op jit(solution)/shard_map/ppermute | solution.py:21
  2.1 15.5 %collective-permute-start = (bf16[512,1024]{1,0:T(8,128)(2,1)}, bf16[512,1024]{1,0:T(8,128)(2,1)}, u32[]{:S(2)}, u32[]{:S(2)}) collective-permute-start(bf16[512,1024]{1,0:T(8,128)(2,1)} %param.9), channel_id=1, source_target_pairs={{0,8},{8,0},{1,9},{9,1},{2,10},{10,2},{3,11},{11,3},{4,12},{12,4},... | collective-permute-start | bytes 3145736 | tf_op jit(solution)/shard_map/ppermute | solution.py:21
  7.8 6.9 %copy-start.13 = (bf16[512,128]{1,0:T(8,128)(2,1)S(1)}, bf16[512,128]{1,0:T(8,128)(2,1)}, u32[]{:S(2)}) copy-start(bf16[512,128]{1,0:T(8,128)(2,1)} %param.8) | copy-start | bytes 393220
  7.8 7.0 %copy-start.11 = (bf16[2048,128]{1,0:T(8,128)(2,1)S(1)}, bf16[2048,128]{1,0:T(8,128)(2,1)}, u32[]{:S(2)}) copy-start(bf16[2048,128]{1,0:T(8,128)(2,1)} %param.11) | copy-start | bytes 1572868
  7.8 35.5 %all-to-all-start = ((bf16[8,128,1024]{2,1,0:T(8,128)(2,1)}), bf16[8,128,1024]{2,1,0:T(8,128)(2,1)S(1)}, u32[]{:S(2)}, u32[]{:S(2)}) async-start(bf16[8,128,1024]{2,1,0:T(8,128)(2,1)} %shard_map.94), calls=%async_computation | async-start | bytes 4194304 | tf_op jit(solution)/shard_map/all_to_all | solution.py:49
  15.1 2.2 %copy-start.7 = (bf16[512,2048]{1,0:T(8,128)(2,1)S(1)}, bf16[512,2048]{1,0:T(8,128)(2,1)}, u32[]{:S(2)}) copy-start(bf16[512,2048]{1,0:T(8,128)(2,1)} %param.10) | copy-start | bytes 6291460
  17.3 1.2 copy-start.8
  43.3 1.4 copy-start.2
  44.7 29.0 %all-to-all-start.1 = ((bf16[8,768,128]{1,2,0:T(8,128)(2,1)}), bf16[8,768,128]{1,2,0:T(8,128)(2,1)S(1)}, u32[]{:S(2)}, u32[]{:S(2)}) async-start(bf16[8,768,128]{1,2,0:T(8,128)(2,1)} %pad_maximum_fusion.1), calls=%async_computation.1 | async-start | bytes 3145728 | tf_op jit(solution)/shard_map/all_to_all | solution.py:49
  73.7 1.2 copy-start
  74.9 34.7 %all-to-all-start.2 = ((f16[16,64,1024]{2,1,0:T(8,128)(2,1)}), f16[16,64,1024]{2,1,0:T(8,128)(2,1)S(1)}, u32[]{:S(2)}, u32[]{:S(2)}) async-start(f16[16,64,1024]{2,1,0:T(8,128)(2,1)} %bitcast.40), calls=%async_computation.2 | async-start | bytes 4194304 | tf_op jit(solution)/shard_map/all_to_all | solution.py:49
  78.6 4.3 %copy-start.3 = (bf16[8,128,1024]{2,1,0:T(8,128)(2,1)S(1)}, bf16[8,128,1024]{2,1,0:T(8,128)(2,1)}, u32[]{:S(2)}) copy-start(bf16[8,128,1024]{2,1,0:T(8,128)(2,1)} %copy-done.2) | copy-start | bytes 6291460
  82.9 2.3 %copy-start.10 = (bf16[1024,512]{1,0:T(8,128)(2,1)S(1)}, bf16[1024,512]{1,0:T(8,128)(2,1)}, u32[]{:S(2)}) copy-start(bf16[1024,512]{1,0:T(8,128)(2,1)} %pad_maximum_fusion.4) | copy-start | bytes 3145732
  85.2 8.5 %copy-start.9 = (bf16[1024,512]{1,0:T(8,128)(2,1)S(1)}, bf16[1024,512]{1,0:T(8,128)(2,1)}, u32[]{:S(2)}) copy-start(bf16[1024,512]{1,0:T(8,128)(2,1)} %pad_maximum_fusion.2) | copy-start | bytes 3145732
  87.4 26.7 %collective-permute-start.3 = (f16[1024,512]{1,0:T(8,128)(2,1)}, f16[1024,512]{1,0:T(8,128)(2,1)}, u32[]{:S(2)}, u32[]{:S(2)}) collective-permute-start(f16[1024,512]{1,0:T(8,128)(2,1)} %multiply_convert_fusion.4), channel_id=1, source_target_pairs={{0,2},{1,3},{2,0},{3,1},{4,6},{5,7},{6,4},{7,5},{8,10},{9,11},{10,... | collective-permute-start | bytes 3145736 | tf_op jit(solution)/shard_map/ppermute | solution.py:17
  91.0 46.4 %collective-permute-start.4 = (f16[1024,512]{1,0:T(8,128)(2,1)}, f16[1024,512]{1,0:T(8,128)(2,1)}, u32[]{:S(2)}, u32[]{:S(2)}) collective-permute-start(f16[1024,512]{1,0:T(8,128)(2,1)} %multiply_convert_fusion.3), channel_id=1, source_target_pairs={{0,1},{1,2},{2,3},{3,0},{4,5},{5,6},{6,7},{7,4},{8,9},{9,10},{10,1... | collective-permute-start | bytes 3145736 | tf_op jit(solution)/shard_map/ppermute | solution.py:17
  91.8 45.7 %collective-permute-start.5 = (f16[1024,512]{1,0:T(8,128)(2,1)}, f16[1024,512]{1,0:T(8,128)(2,1)}, u32[]{:S(2)}, u32[]{:S(2)}) collective-permute-start(f16[1024,512]{1,0:T(8,128)(2,1)} %multiply_convert_fusion.2), channel_id=1, source_target_pairs={{0,3},{1,0},{2,1},{3,2},{4,7},{5,4},{6,5},{7,6},{8,11},{9,8},{10,9... | collective-permute-start | bytes 3145736 | tf_op jit(solution)/shard_map/ppermute | solution.py:17
  109.6 27.9 %copy-start.6 = (f32[1024,512]{1,0:T(8,128)S(1)}, f32[1024,512]{1,0:T(8,128)}, u32[]{:S(2)}) copy-start(f32[1024,512]{1,0:T(8,128)} %fusion.8) | copy-start | bytes 6291460
  141.1 6.9 %copy-start.1 = (bf16[8,768,128]{1,2,0:T(8,128)(2,1)S(1)}, bf16[8,768,128]{1,2,0:T(8,128)(2,1)}, u32[]{:S(2)}) copy-start(bf16[8,768,128]{1,2,0:T(8,128)(2,1)} %copy-done) | copy-start | bytes 4718596
  141.1 22.7 %all-to-all-start.3 = ((f16[16,64,512]{2,1,0:T(8,128)(2,1)}), f16[16,64,512]{2,1,0:T(8,128)(2,1)}, u32[]{:S(2)}, u32[]{:S(2)}) async-start(f16[16,64,512]{2,1,0:T(8,128)(2,1)} %bitcast.8), calls=%async_computation.3 | async-start | bytes 2097152 | tf_op jit(solution)/shard_map/all_to_all | solution.py:49
  148.0 1.6 copy-start.4
  151.3 18.4 %copy-start.5 = (f32[512,512]{1,0:T(8,128)S(1)}, f32[512,512]{1,0:T(8,128)}, u32[]{:S(2)}) copy-start(f32[512,512]{1,0:T(8,128)} %param.12) | copy-start | bytes 3145732
  151.3 18.4 %collective-permute-start.2 = (f32[512,512]{1,0:T(8,128)}, f32[512,512]{1,0:T(8,128)}, u32[]{:S(2)}, u32[]{:S(2)}) collective-permute-start(f32[512,512]{1,0:T(8,128)} %fusion.1), channel_id=1, source_target_pairs={{0,8},{8,0},{1,9},{9,1},{2,10},{10,2},{3,11},{11,3},{4,12},{12,4},... | collective-permute-start | bytes 3145736 | tf_op jit(solution)/shard_map/ppermute | solution.py:21
  152.9 20.1 %collective-permute-start.6 = (f32[64,256]{1,0:T(8,128)S(1)}, f32[64,256]{1,0:T(8,128)S(1)}, u32[]{:S(2)}, u32[]{:S(2)}) collective-permute-start(f32[64,256]{1,0:T(8,128)S(1)} %pad_maximum_fusion.14), channel_id=1, source_target_pairs={{0,2},{1,3},{2,0},{3,1},{4,6},{5,7},{6,4},{7,5},{8,10},{9,11},{10,... | collective-permute-start | bytes 196616 | tf_op jit(solution)/shard_map/ppermute | solution.py:17
  154.8 18.3 %collective-permute-start.7 = (f32[64,256]{1,0:T(8,128)S(1)}, f32[64,256]{1,0:T(8,128)S(1)}, u32[]{:S(2)}, u32[]{:S(2)}) collective-permute-start(f32[64,256]{1,0:T(8,128)S(1)} %pad_maximum_fusion.15), channel_id=1, source_target_pairs={{0,1},{1,2},{2,3},{3,0},{4,5},{5,6},{6,7},{7,4},{8,9},{9,10},{10,1... | collective-permute-start | bytes 196616 | tf_op jit(solution)/shard_map/ppermute | solution.py:17
  156.6 16.5 %collective-permute-start.8 = (f32[64,256]{1,0:T(8,128)}, f32[64,256]{1,0:T(8,128)S(1)}, u32[]{:S(2)}, u32[]{:S(2)}) collective-permute-start(f32[64,256]{1,0:T(8,128)} %pad_maximum_fusion.16), channel_id=1, source_target_pairs={{0,3},{1,0},{2,1},{3,2},{4,7},{5,4},{6,5},{7,6},{8,11},{9,8},{10,9... | collective-permute-start | bytes 196616 | tf_op jit(solution)/shard_map/ppermute | solution.py:17
  166.1 12.8 %all-to-all-start.4 = ((bf16[16,64,256]{2,1,0:T(8,128)(2,1)}), bf16[16,64,256]{2,1,0:T(8,128)(2,1)S(1)}, u32[]{:S(2)}, u32[]{:S(2)}) async-start(bf16[16,64,256]{2,1,0:T(8,128)(2,1)} %bitcast.11), calls=%async_computation.4 | async-start | bytes 1048576 | tf_op jit(solution)/shard_map/all_to_all | solution.py:49
  169.7 9.3 %slice-start = ((bf16[8,768,128]{1,2,0:T(8,128)(2,1)}), bf16[8,256,128]{1,2,0:T(8,128)(2,1)S(1)}, s32[]{:S(2)}) async-start(bf16[8,768,128]{1,2,0:T(8,128)(2,1)} %copy-done), calls=%async_computation.5 | async-start | bytes 1048576 | tf_op jit(solution)/shard_map/slice | solution.py:99
  173.0 11.1 %copy-start.12 = (f32[128,256]{1,0:T(8,128)S(1)}, f32[128,256]{1,0:T(8,128)}, u32[]{:S(2)}) copy-start(f32[128,256]{1,0:T(8,128)} %param.13) | copy-start | bytes 393220
  173.1 10.0 %collective-permute-start.9 = (f32[64,128]{1,0:T(8,128)S(1)}, f32[64,128]{1,0:T(8,128)S(1)}, u32[]{:S(2)}, u32[]{:S(2)}) collective-permute-start(f32[64,128]{1,0:T(8,128)S(1)} %constant_dynamic-slice_fusion.1), channel_id=1, source_target_pairs={{0,4},{4,0},{1,5},{5,1},{2,6},{6,2},{3,7},{7,3},{8,12},{12,8},{9,1... | collective-permute-start | bytes 98312 | tf_op jit(solution)/shard_map/ppermute | solution.py:21
  179.3 4.8 %collective-permute-start.10 = (f32[128,256]{1,0:T(8,128)S(1)}, f32[128,256]{1,0:T(8,128)S(1)}, u32[]{:S(2)}, u32[]{:S(2)}) collective-permute-start(f32[128,256]{1,0:T(8,128)S(1)} %constant_dynamic-slice_fusion), channel_id=1, source_target_pairs={{0,8},{8,0},{1,9},{9,1},{2,10},{10,2},{3,11},{11,3},{4,12},{12,4},... | collective-permute-start | bytes 393224 | tf_op jit(solution)/shard_map/ppermute | solution.py:21

commit v2 on v1

v2 whole, which is shorter than its diff:
```python
import jax
import jax.numpy as jnp
from jax import lax
from jax.experimental import pallas as pl
from jax.experimental.pallas import tpu as pltpu
from jax.sharding import Mesh, PartitionSpec as P


PLANE = ("yh", "x")
TILE = ("yh", "x", "yl")
WIRE = jnp.float16
NEAR = 64.0
FAR = 16.0


def shift(value, axis, by):
    n = lax.axis_size(axis)
    return lax.ppermute(value, axis, [(i, (i + by) % n) for i in range(n)])


def swap(value, axis="k"):
    return lax.ppermute(value, axis, [(0, 1), (1, 0)])


def dot(a, b):
    return jnp.dot(a, b, preferred_element_type=jnp.float32)


def tied(*values):
    return lax.optimization_barrier(values)


def arrange(window_rows, upsilon_rows, omega_cols, phi_cols, k, z):
    rows, cols = window_rows.shape
    own = cols // 16
    deep, width = upsilon_rows.shape
    wide = width // 8
    split, thin = omega_cols.shape
    tall = phi_cols.shape[0] // 8

    def move(where, window, upsilon, omega, phi, pieces, first, second, third, fourth, small, sems):
        picks = (first, second, third, fourth)
        k, z = where[0], where[1]
        copies = []

        def copy(src, dst):
            copies.append(pltpu.make_async_copy(src, dst, sems.at[len(copies)]))
            copies[-1].start()

        for i in range(8):
            for half in range(2):
                start = pl.multiple_of(2 * i * own + (k + half) % 2 * own, own)
                copy(window.at[:, pl.ds(start, own)], pieces.at[i, :, pl.ds(half * own, own)])
        for at in range(4):
            for half in range(2):
                start = pl.multiple_of((z + at) % 4 * wide + half * 4 * wide, wide)
                copy(upsilon.at[:, pl.ds(start, wide)], picks[at].at[:, pl.ds(half * wide, wide)])
        for i in range(8):
            copy(omega, small.at[i, pl.ds(0, split), :])
            copy(phi.at[pl.ds(i * tall, tall), :], small.at[i, pl.ds(split, tall), :])
        for one in copies:
            one.wait()

    kind = window_rows.dtype
    anywhere = pl.BlockSpec(memory_space=pl.ANY)
    return pl.pallas_call(
        move,
        in_specs=[pl.BlockSpec(memory_space=pltpu.SMEM)] + [anywhere] * 4,
        out_specs=[anywhere] * 6,
        out_shape=[
            jax.ShapeDtypeStruct((8, rows, 2 * own), kind),
            *[jax.ShapeDtypeStruct((deep, 2 * wide), kind)] * 4,
            jax.ShapeDtypeStruct((8, split + tall, thin), kind),
        ],
        scratch_shapes=[pltpu.SemaphoreType.DMA((40,))],
    )(jnp.stack([k, z]).astype(jnp.int32), window_rows, upsilon_rows, omega_cols, phi_cols)


def exchange(value, axes):
    return lax.all_to_all(value, axes, 0, 0, tiled=True)


def body(window_rows, omega_cols, psi_rows, upsilon_rows, phi_cols, range_old, core_old):
    k = lax.axis_index("k")
    z = lax.axis_index("z")
    yl = lax.axis_index("yl")
    rows, cols = window_rows.shape
    own = cols // 16
    wide = upsilon_rows.shape[1] // 8
    split = omega_cols.shape[0]

    pieces, *picks, small = arrange(window_rows, upsilon_rows, omega_cols, phi_cols, k, z)
    picks_other = [None] * 4
    for at in (2, 1, 3, 0):
        picks_other[at] = swap(picks[at])
    relaid = exchange(pieces, PLANE).reshape(8 * rows, 2 * own)
    relaid, *picks_other = tied(relaid, *picks_other)
    psi_other = swap(psi_rows)

    def share(at):
        return dot(relaid, jnp.concatenate([picks[at], picks_other[at]], axis=0))

    sent = []
    for at in (2, 1, 3):
        part = (NEAR * share(at)).astype(WIRE)
        sent.append(shift(part, "z", at))

    small = tied(small, relaid)[0]
    small = exchange(small, PLANE)
    co = (NEAR * dot(relaid, jnp.concatenate([psi_rows, psi_other], axis=0))).astype(WIRE)
    mine = share(0)
    co, small, mine = tied(co, small, mine)
    co = exchange(co.reshape(8, rows, -1), PLANE)
    co = jnp.sum(co.astype(jnp.float32), axis=0) * (1.0 / NEAR)

    mine, co, *sent = tied(mine, co, *sent)
    total = mine + (1.0 / NEAR) * sum(s.astype(jnp.float32) for s in sent)
    sk = (FAR * total).astype(WIRE).reshape(16, rows // 2, 2 * wide)
    sk = exchange(sk, TILE)

    omega = jnp.moveaxis(small[:, :split], 0, 1).reshape(split, -1)
    phi = jnp.moveaxis(small[:, split:], 0, 1).reshape(-1, 8 * phi_cols.shape[1])
    range_given = dot(omega, relaid[:, own:])
    range_kept = dot(omega, relaid[:, :own])
    range_sketch = range_old + range_kept + swap(range_given)

    def pick(value, at, wide):
        start = (z + at) % 4 * wide
        return jnp.concatenate(
            [lax.dynamic_slice_in_dim(value, start + half * 4 * wide, wide, 1) for half in range(2)], axis=1
        )

    narrow = co.shape[1] // 8
    others = [shift(pick(co, at, narrow), "z", at) for at in (2, 1, 3)]
    co = pick(co, 0, narrow) + others[0] + others[1] + others[2]
    co_kept = lax.dynamic_slice_in_dim(co, yl * narrow, narrow, 1)
    corange_sketch = co_kept + swap(lax.dynamic_slice_in_dim(co, (1 - yl) * narrow, narrow, 1), "yl")

    sk = (jnp.sum(sk.astype(jnp.float32), axis=0) * (1.0 / FAR)).astype(jnp.bfloat16)
    sk = jnp.stack([sk[:, :wide], sk[:, wide:]])
    sk = jnp.broadcast_to(sk[None], (8,) + sk.shape).reshape(16, rows // 2, wide)
    sk = exchange(sk, TILE)
    term = dot(phi, sk.reshape(8 * rows, wide))
    here = lax.dynamic_slice_in_dim(term, k * rows, rows, 0)
    there = lax.dynamic_slice_in_dim(term, (1 - k) * rows, rows, 0)
    core_sketch = core_old + here + swap(there)
    return (range_sketch, corange_sketch, core_sketch)


def solution(mesh):
    fine = Mesh(mesh.devices.reshape(2, 4, 2, 2, 4), ("yh", "x", "k", "yl", "z"))
    row = ("yh", "x", "k")
    col = ("yl", "z")
    placed = (
        P(row, col),
        P(None, row),
        P(col + row, None),
        P(col + row, None),
        P(None, row),
        P(None, col + row),
        P(row, col),
    )
    return jax.shard_map(
        body,
        mesh=fine,
        in_specs=placed,
        out_specs=(P(None, col + row), P(row, col), P(row, col)),
        check_vma=False,
    )
```

time: 186 us -> 354 us (1.90)
  Pallas kernels: 5.63 us -> 177 us
  other arithmetic: 15.9 us -> 11.3 us
    pallas_call x1, Pallas kernels: 5.63 us -> 177 us  [arrange(): pl.pallas_call(move, in_specs=[pl.BlockSpec(memory_space=pltpu.SMEM)] + [...]
    concatenate x7 -> x0, other arithmetic: 6.66 us -> none  [the longest x5 4.75 us: both(): jnp.concatenate([jnp.where(k == 0, mine, theirs), jnp.where(k == 0, their...]
    transpose x0 -> x4, local copies, waits for them, and re-layouts: none -> 4.76 us  [the longest x2 2.67 us: body(): omega = jnp.moveaxis(small[:, :split], 0, 1).reshape(split, -1)]
    ppermute x5 -> x8, starting transfers between devices: 8.24 us -> 10.6 us  [swap(): return lax.ppermute(value, axis, [(0, 1), (1, 0)])]
  transfers between devices with their start and end apart: 16 -> 19, of which waited for: 8 -> 11; matrix products, arithmetic and copies ran while one was open for 20% -> 10% of each run, Pallas kernels for 3% -> 0%
where the time goes in v2:
time: 354 us
  Pallas kernels  177 us (50%)
  waiting for transfers between devices  83.2 us (24%)
  starting transfers between devices  47.4 us (13%)
  matrix products  24.6 us (7%)
  other arithmetic  11.3 us (3%)
  local copies, waits for them, and re-layouts  9.41 us (3%)
    pallas_call x1, Pallas kernels, arrange(): pl.pallas_call(move, in_specs=[pl.BlockSpec(memory_space=pltpu.SMEM)] + [...  177 us
    all_to_all x5, waiting for transfers between devices, exchange(): return lax.all_to_all(value, axes, 0, 0, tiled=True)  54.1 us
    all_to_all x5, starting transfers between devices, exchange(): return lax.all_to_all(value, axes, 0, 0, tiled=True)  28.7 us
    ppermute x6, waiting for transfers between devices, shift(): return lax.ppermute(value, axis, [(i, (i + by) % n) for i in range(n)])  26.6 us
    dot_general x8, matrix products, dot(): return jnp.dot(a, b, preferred_element_type=jnp.float32)  24.6 us
    ppermute x8, starting transfers between devices, swap(): return lax.ppermute(value, axis, [(0, 1), (1, 0)])  10.6 us
    ppermute x6, starting transfers between devices, shift(): return lax.ppermute(value, axis, [(i, (i + by) % n) for i in range(n)])  8.06 us
  transfers between devices with their start and end apart: 19, of which 11 were waited for; matrix products, arithmetic and copies ran while one was open for 10% of the time, Pallas kernels for 0%

profile of v2, /device:TPU:1, one launch (start us, length us, event | category | flops | bytes accessed | tf_op | source)
XLA Modules:
  0.0 353.6 jit_solution(2168332254300137542)
XLA Ops:
  0.6 0.6 pad_add_fusion.where
  1.3 176.8 %shard_map.94 = (bf16[8,128,1024]{2,1,0:T(8,128)(2,1)}, bf16[512,512]{1,0:T(8,128)(2,1)}, bf16[512,512]{1,0:T(8,128)(2,1)}, bf16[512,512]{1,0:T(8,128)(2,1)}, bf...) custom-call(s32[2]{0:T(128)} %pad_add_fusion.where, bf16[128,8192]{1,0:T(8,128)(2,1)} %window.1, ...), custom_call_target="tpu_custom_call" | custom-call | tf_op jit(solution)/shard_map/pallas_call | solution.py:66
  178.1 0.0 copy-start.9
  178.1 7.6 %all-to-all-start = ((bf16[8,128,1024]{2,1,0:T(8,128)(2,1)}), bf16[8,128,1024]{2,1,0:T(8,128)(2,1)S(1)}, u32[]{:S(2)}, u32[]{:S(2)}) async-start(bf16[8,128,1024]{2,1,0:T(8,128)(2,1)} %get-tuple-element.23), calls=%async_computation | async-start | bytes 4194304 | tf_op jit(solution)/shard_map/all_to_all | solution.py:80
  185.7 1.0 collective-permute-start
  186.7 0.1 collective-permute-start.1
  186.8 0.4 collective-permute-start.2
  187.2 0.1 collective-permute-start.3
  187.3 0.4 collective-permute-start.4
  187.7 0.7 collective-permute-done
  188.5 0.7 collective-permute-done.1
  189.2 0.7 collective-permute-done.2
  190.0 0.1 copy-done.15
  190.0 0.8 copy-done.13
  190.8 0.0 collective-permute-done.3
  190.8 23.5 %all-to-all-done = bf16[8,128,1024]{2,1,0:T(8,128)(2,1)S(1)} async-done(((bf16[8,128,1024]{2,1,0:T(8,128)(2,1)}), bf16[8,128,1024]{2,1,0:T(8,128)(2,1)S(1)}, u32[]{:S(2)}, u32[]{:S(2)}) %all-to-all-start) | async-done | bytes 2097184 | tf_op jit(solution)/shard_map/all_to_all | solution.py:80
  214.4 1.4 copy-done.2
  215.7 4.7 %all-to-all-start.1 = ((bf16[8,768,128]{2,1,0:T(8,128)(2,1)}), bf16[8,768,128]{2,1,0:T(8,128)(2,1)S(1)}, u32[]{:S(2)}, u32[]{:S(2)}) async-start(bf16[8,768,128]{2,1,0:T(8,128)(2,1)} %get-tuple-element.30), calls=%async_computation.1 | async-start | bytes 3145728 | tf_op jit(solution)/shard_map/all_to_all | solution.py:80
  220.4 4.5 %fusion.4 = f32[1024,512]{1,0:T(8,128)} fusion(bf16[1024,1024]{1,0:T(8,128)(2,1)} %bitcast.26, bf16[512,512]{1,0:T(8,128)(2,1)} %copy-done.17, bf16[512,512]{1,0:T(8,128)(2,1)} %get-tuple-element.24), kind=kOutput, calls=%fused_computation.12 | convolution fusion | flops 1075838976 | bytes 5242880 | tf_op jit(solution)/shard_map/dot_general | solution.py:26
  225.0 0.0 collective-permute-done.4
  225.0 5.0 %multiply_convert_fusion = f16[1024,1024]{1,0:T(8,128)(2,1)} fusion(bf16[1024,1024]{1,0:T(8,128)(2,1)S(1)} %bitcast.28, bf16[512,1024]{1,0:T(8,128)(2,1)} %collective-permute-done.4, bf16[512,1024]{1,0:T(8,128)(2,1)S(1)} %copy-done.9), kind=kOutput, calls=%fused_computation.1 | convolution fusion | flops 2153775104 | bytes 6291456 | tf_op jit(solution)/shard_map/dot_general | solution.py:26
  229.9 13.5 %all-to-all-done.1 = bf16[8,768,128]{2,1,0:T(8,128)(2,1)S(1)} async-done(((bf16[8,768,128]{2,1,0:T(8,128)(2,1)}), bf16[8,768,128]{2,1,0:T(8,128)(2,1)S(1)}, u32[]{:S(2)}, u32[]{:S(2)}) %all-to-all-start.1) | async-done | bytes 1572896 | tf_op jit(solution)/shard_map/all_to_all | solution.py:80
  243.4 1.2 copy-done
  244.6 3.6 %all-to-all-start.2 = ((f16[8,128,1024]{2,1,0:T(8,128)(2,1)}), f16[8,128,1024]{2,1,0:T(8,128)(2,1)S(1)}, u32[]{:S(2)}, u32[]{:S(2)}) async-start(f16[8,128,1024]{2,1,0:T(8,128)(2,1)} %bitcast.35), calls=%async_computation.2 | async-start | bytes 4194304 | tf_op jit(solution)/shard_map/all_to_all | solution.py:80
  248.2 4.0 %multiply_convert_fusion.2 = f16[1024,512]{1,0:T(8,128)(2,1)} fusion(bf16[1024,1024]{1,0:T(8,128)(2,1)} %bitcast.27, bf16[512,512]{1,0:T(8,128)(2,1)} %collective-permute-done.3, bf16[512,512]{1,0:T(8,128)(2,1)S(1)} %copy-done.12), kind=kOutput, calls=%fused_computation.7 | convolution fusion | flops 1076887552 | bytes 4194304 | tf_op jit(solution)/shard_map/dot_general | solution.py:26
  252.3 3.8 %collective-permute-start.8 = (f16[1024,512]{1,0:T(8,128)(2,1)}, f16[1024,512]{1,0:T(8,128)(2,1)}, u32[]{:S(2)}, u32[]{:S(2)}) collective-permute-start(f16[1024,512]{1,0:T(8,128)(2,1)} %multiply_convert_fusion.2), channel_id=1, source_target_pairs={{0,3},{1,0},{2,1},{3,2},{4,7},{5,4},{6,5},{7,6},{8,11},{9,8},{10,9... | collective-permute-start | bytes 3145736 | tf_op jit(solution)/shard_map/ppermute | solution.py:18
  256.0 2.2 multiply_convert_fusion.3
  258.3 0.0 collective-permute-start.7
  258.3 2.3 multiply_convert_fusion.4
  260.6 1.3 collective-permute-start.6
  261.9 1.1 slice_bitcast_fusion.1
  263.0 1.0 copy.11
  264.0 12.7 %all-to-all-done.2 = f16[8,128,1024]{2,1,0:T(8,128)(2,1)S(1)} async-done(((f16[8,128,1024]{2,1,0:T(8,128)(2,1)}), f16[8,128,1024]{2,1,0:T(8,128)(2,1)S(1)}, u32[]{:S(2)}, u32[]{:S(2)}) %all-to-all-start.2) | async-done | bytes 2097184 | tf_op jit(solution)/shard_map/all_to_all | solution.py:80
  276.7 0.5 convert_reduce_fusion
  277.2 0.8 broadcast_multiply_fusion
  278.1 22.3 %collective-permute-done.8 = f16[1024,512]{1,0:T(8,128)(2,1)} collective-permute-done((f16[1024,512]{1,0:T(8,128)(2,1)}, f16[1024,512]{1,0:T(8,128)(2,1)}, u32[]{:S(2)}, u32[]{:S(2)}) %collective-permute-start.8) | collective-permute-done | bytes 1048608 | tf_op jit(solution)/shard_map/ppermute | solution.py:18
  300.4 0.0 collective-permute-done.7
  300.4 4.2 %collective-permute-done.6 = f16[1024,512]{1,0:T(8,128)(2,1)} collective-permute-done((f16[1024,512]{1,0:T(8,128)(2,1)}, f16[1024,512]{1,0:T(8,128)(2,1)}, u32[]{:S(2)}, u32[]{:S(2)}) %collective-permute-start.6) | collective-permute-done | bytes 1048608 | tf_op jit(solution)/shard_map/ppermute | solution.py:18
  304.6 3.6 %multiply_convert_fusion.1 = f16[1024,512]{1,0:T(8,128)(2,1)} fusion(f32[1024,512]{1,0:T(8,128)S(1)} %copy-done.6, f16[1024,512]{1,0:T(8,128)(2,1)} %collective-permute-done.8, f16[1024,512]{1,0:T(8,128)(2,1)} %collective-permute-done.7, f16[1024,512]{1,0:T(8,128)(2,1)} %collective-permute-done.6), kind=kLoop, calls=%fused_computation.6 | loop fusion | flops 4718592 | bytes 6291456 | tf_op jit(solution)/shard_map/convert_element_type | solution.py:118
  308.3 6.5 %all-to-all-start.3 = ((f16[16,64,512]{2,1,0:T(8,128)(2,1)}), f16[16,64,512]{2,1,0:T(8,128)(2,1)}, u32[]{:S(2)}, u32[]{:S(2)}) async-start(f16[16,64,512]{2,1,0:T(8,128)(2,1)} %bitcast.8), calls=%async_computation.3 | async-start | bytes 2097152 | tf_op jit(solution)/shard_map/all_to_all | solution.py:80
  314.8 1.0 slice_bitcast_fusion
  315.9 1.6 copy.10
  317.5 0.3 copy-done.5
  317.8 1.7 fusion.17
  319.5 3.8 %collective-permute-start.5 = (f32[512,512]{1,0:T(8,128)}, f32[512,512]{1,0:T(8,128)}, u32[]{:S(2)}, u32[]{:S(2)}) collective-permute-start(f32[512,512]{1,0:T(8,128)} %fusion.17), channel_id=1, source_target_pairs={{0,8},{8,0},{1,9},{9,1},{2,10},{10,2},{3,11},{11,3},{4,12},{12,4},... | collective-permute-start | bytes 3145736 | tf_op jit(solution)/shard_map/ppermute | solution.py:22
  323.3 0.1 constant_dynamic-slice_fusion.9
  323.4 0.7 pad_maximum_fusion
  324.0 0.3 collective-permute-start.9
  324.3 0.7 pad_maximum_fusion.1
  325.0 0.7 pad_maximum_fusion.2
  325.7 2.7 collective-permute-start.11
  328.3 0.7 all-to-all-done.3
  329.0 1.4 convert_reduce_fusion.1
  330.4 0.9 broadcast_in_dim.2
  331.3 6.3 %all-to-all-start.4 = ((bf16[16,64,256]{2,1,0:T(8,128)(2,1)}), bf16[16,64,256]{2,1,0:T(8,128)(2,1)}, u32[]{:S(2)}, u32[]{:S(2)}) async-start(bf16[16,64,256]{2,1,0:T(8,128)(2,1)} %bitcast.37), calls=%async_computation.4 | async-start | bytes 1048576 | tf_op jit(solution)/shard_map/all_to_all | solution.py:80
  337.6 3.2 fusion.3
  340.8 1.0 fusion.21
  341.8 1.4 collective-permute-start.12
  343.2 3.7 %all-to-all-done.4 = bf16[16,64,256]{2,1,0:T(8,128)(2,1)} async-done(((bf16[16,64,256]{2,1,0:T(8,128)(2,1)}), bf16[16,64,256]{2,1,0:T(8,128)(2,1)}, u32[]{:S(2)}, u32[]{:S(2)}) %all-to-all-start.4) | async-done | bytes 524320 | tf_op jit(solution)/shard_map/all_to_all | solution.py:80
  346.9 1.5 fusion.27
  348.5 3.4 collective-permute-start.13
  351.9 0.6 dynamic-slice_add_fusion
  352.5 0.3 collective-permute-done.13
  352.9 0.7 add_add_fusion
  (41 shorter events, 0.1 us)
Async XLA Ops:
  178.1 9.2 %copy-start.9 = (bf16[512,1024]{1,0:T(8,128)(2,1)S(1)}, bf16[512,1024]{1,0:T(8,128)(2,1)}, u32[]{:S(2)}) copy-start(bf16[512,1024]{1,0:T(8,128)(2,1)} %param.9) | copy-start | bytes 3145732
  178.1 36.2 %all-to-all-start = ((bf16[8,128,1024]{2,1,0:T(8,128)(2,1)}), bf16[8,128,1024]{2,1,0:T(8,128)(2,1)S(1)}, u32[]{:S(2)}, u32[]{:S(2)}) async-start(bf16[8,128,1024]{2,1,0:T(8,128)(2,1)} %get-tuple-element.23), calls=%async_computation | async-start | bytes 4194304 | tf_op jit(solution)/shard_map/all_to_all | solution.py:80
  185.7 2.7 collective-permute-start
  186.7 2.5 collective-permute-start.1
  186.8 3.2 collective-permute-start.2
  187.2 3.6 %collective-permute-start.3 = (bf16[512,512]{1,0:T(8,128)(2,1)}, bf16[512,512]{1,0:T(8,128)(2,1)}, u32[]{:S(2)}, u32[]{:S(2)}) collective-permute-start(bf16[512,512]{1,0:T(8,128)(2,1)} %get-tuple-element.27), channel_id=1, source_target_pairs={{0,8},{8,0},{1,9},{9,1},{2,10},{10,2},{3,11},{11,3},{4,12},{12,4},... | collective-permute-start | bytes 1572872 | tf_op jit(solution)/shard_map/ppermute | solution.py:22
  187.3 37.7 %collective-permute-start.4 = (bf16[512,1024]{1,0:T(8,128)(2,1)S(1)}, bf16[512,1024]{1,0:T(8,128)(2,1)}, u32[]{:S(2)}, u32[]{:S(2)}) collective-permute-start(bf16[512,1024]{1,0:T(8,128)(2,1)S(1)} %copy-done.9), channel_id=1, source_target_pairs={{0,8},{8,0},{1,9},{9,1},{2,10},{10,2},{3,11},{11,3},{4,12},{12,4},... | collective-permute-start | bytes 3145736 | tf_op jit(solution)/shard_map/ppermute | solution.py:22
  188.5 1.5 copy-start.17
  189.2 0.8 copy-start.15
  190.0 0.8 copy-start.13
  214.4 1.4 copy-start.2
  215.7 27.7 %all-to-all-start.1 = ((bf16[8,768,128]{2,1,0:T(8,128)(2,1)}), bf16[8,768,128]{2,1,0:T(8,128)(2,1)S(1)}, u32[]{:S(2)}, u32[]{:S(2)}) async-start(bf16[8,768,128]{2,1,0:T(8,128)(2,1)} %get-tuple-element.30), calls=%async_computation.1 | async-start | bytes 3145728 | tf_op jit(solution)/shard_map/all_to_all | solution.py:80
  220.4 4.6 %copy-start.3 = (bf16[8,128,1024]{2,1,0:T(8,128)(2,1)S(1)}, bf16[8,128,1024]{2,1,0:T(8,128)(2,1)}, u32[]{:S(2)}) copy-start(bf16[8,128,1024]{2,1,0:T(8,128)(2,1)} %copy-done.2) | copy-start | bytes 6291460
  243.4 1.2 copy-start
  243.4 4.8 %copy-start.12 = (bf16[512,512]{1,0:T(8,128)(2,1)S(1)}, bf16[512,512]{1,0:T(8,128)(2,1)}, u32[]{:S(2)}) copy-start(bf16[512,512]{1,0:T(8,128)(2,1)} %get-tuple-element.27) | copy-start | bytes 1572868
  244.6 32.2 %all-to-all-start.2 = ((f16[8,128,1024]{2,1,0:T(8,128)(2,1)}), f16[8,128,1024]{2,1,0:T(8,128)(2,1)S(1)}, u32[]{:S(2)}, u32[]{:S(2)}) async-start(f16[8,128,1024]{2,1,0:T(8,128)(2,1)} %bitcast.35), calls=%async_computation.2 | async-start | bytes 4194304 | tf_op jit(solution)/shard_map/all_to_all | solution.py:80
  248.2 7.8 %copy-start.4 = (bf16[8,128,1024]{2,1,0:T(8,128)(2,1)S(1)}, bf16[8,128,1024]{2,1,0:T(8,128)(2,1)}, u32[]{:S(2)}) copy-start(bf16[8,128,1024]{2,1,0:T(8,128)(2,1)} %copy-done.2) | copy-start | bytes 6291460
  248.2 7.8 %copy-start.11 = (bf16[512,512]{1,0:T(8,128)(2,1)S(1)}, bf16[512,512]{1,0:T(8,128)(2,1)}, u32[]{:S(2)}) copy-start(bf16[512,512]{1,0:T(8,128)(2,1)} %get-tuple-element.25) | copy-start | bytes 1572868
  248.2 7.8 %copy-start.16 = (bf16[512,512]{1,0:T(8,128)(2,1)S(1)}, bf16[512,512]{1,0:T(8,128)(2,1)}, u32[]{:S(2)}) copy-start(bf16[512,512]{1,0:T(8,128)(2,1)} %copy-done.15) | copy-start | bytes 1572868
  252.3 6.0 %copy-start.10 = (bf16[512,512]{1,0:T(8,128)(2,1)S(1)}, bf16[512,512]{1,0:T(8,128)(2,1)}, u32[]{:S(2)}) copy-start(bf16[512,512]{1,0:T(8,128)(2,1)} %get-tuple-element.26) | copy-start | bytes 1572868
  252.3 6.0 %copy-start.14 = (bf16[512,512]{1,0:T(8,128)(2,1)S(1)}, bf16[512,512]{1,0:T(8,128)(2,1)}, u32[]{:S(2)}) copy-start(bf16[512,512]{1,0:T(8,128)(2,1)} %copy-done.13) | copy-start | bytes 1572868
  252.3 48.1 %collective-permute-start.8 = (f16[1024,512]{1,0:T(8,128)(2,1)}, f16[1024,512]{1,0:T(8,128)(2,1)}, u32[]{:S(2)}, u32[]{:S(2)}) collective-permute-start(f16[1024,512]{1,0:T(8,128)(2,1)} %multiply_convert_fusion.2), channel_id=1, source_target_pairs={{0,3},{1,0},{2,1},{3,2},{4,7},{5,4},{6,5},{7,6},{8,11},{9,8},{10,9... | collective-permute-start | bytes 3145736 | tf_op jit(solution)/shard_map/ppermute | solution.py:18
  258.3 42.1 %collective-permute-start.7 = (f16[1024,512]{1,0:T(8,128)(2,1)}, f16[1024,512]{1,0:T(8,128)(2,1)}, u32[]{:S(2)}, u32[]{:S(2)}) collective-permute-start(f16[1024,512]{1,0:T(8,128)(2,1)} %multiply_convert_fusion.3), channel_id=1, source_target_pairs={{0,1},{1,2},{2,3},{3,0},{4,5},{5,6},{6,7},{7,4},{8,9},{9,10},{10,1... | collective-permute-start | bytes 3145736 | tf_op jit(solution)/shard_map/ppermute | solution.py:18
  260.6 44.1 %collective-permute-start.6 = (f16[1024,512]{1,0:T(8,128)(2,1)}, f16[1024,512]{1,0:T(8,128)(2,1)}, u32[]{:S(2)}, u32[]{:S(2)}) collective-permute-start(f16[1024,512]{1,0:T(8,128)(2,1)} %multiply_convert_fusion.4), channel_id=1, source_target_pairs={{0,2},{1,3},{2,0},{3,1},{4,6},{5,7},{6,4},{7,5},{8,10},{9,11},{10,... | collective-permute-start | bytes 3145736 | tf_op jit(solution)/shard_map/ppermute | solution.py:18
  276.7 27.9 %copy-start.6 = (f32[1024,512]{1,0:T(8,128)S(1)}, f32[1024,512]{1,0:T(8,128)}, u32[]{:S(2)}) copy-start(f32[1024,512]{1,0:T(8,128)} %fusion.4) | copy-start | bytes 6291460
  308.3 6.5 %copy-start.1 = (bf16[8,768,128]{2,1,0:T(8,128)(2,1)S(1)}, bf16[8,768,128]{2,1,0:T(8,128)(2,1)}, u32[]{:S(2)}) copy-start(bf16[8,768,128]{2,1,0:T(8,128)(2,1)} %copy-done) | copy-start | bytes 4718596
  308.3 20.7 %all-to-all-start.3 = ((f16[16,64,512]{2,1,0:T(8,128)(2,1)}), f16[16,64,512]{2,1,0:T(8,128)(2,1)}, u32[]{:S(2)}, u32[]{:S(2)}) async-start(f16[16,64,512]{2,1,0:T(8,128)(2,1)} %bitcast.8), calls=%async_computation.3 | async-start | bytes 2097152 | tf_op jit(solution)/shard_map/all_to_all | solution.py:80
  315.9 1.9 copy-start.5
  317.8 5.5 %copy-start.7 = (f32[128,1024]{1,0:T(8,128)S(1)}, f32[128,1024]{1,0:T(8,128)}, u32[]{:S(2)}) copy-start(f32[128,1024]{1,0:T(8,128)} %broadcast_multiply_fusion) | copy-start | bytes 1572868
  319.5 18.1 %collective-permute-start.5 = (f32[512,512]{1,0:T(8,128)}, f32[512,512]{1,0:T(8,128)}, u32[]{:S(2)}, u32[]{:S(2)}) collective-permute-start(f32[512,512]{1,0:T(8,128)} %fusion.17), channel_id=1, source_target_pairs={{0,8},{8,0},{1,9},{9,1},{2,10},{10,2},{3,11},{11,3},{4,12},{12,4},... | collective-permute-start | bytes 3145736 | tf_op jit(solution)/shard_map/ppermute | solution.py:22
  324.0 16.8 %collective-permute-start.9 = (f32[128,256]{1,0:T(8,128)}, f32[128,256]{1,0:T(8,128)S(1)}, u32[]{:S(2)}, u32[]{:S(2)}) collective-permute-start(f32[128,256]{1,0:T(8,128)} %pad_maximum_fusion), channel_id=1, source_target_pairs={{0,2},{1,3},{2,0},{3,1},{4,6},{5,7},{6,4},{7,5},{8,10},{9,11},{10,... | collective-permute-start | bytes 393224 | tf_op jit(solution)/shard_map/ppermute | solution.py:18
  325.0 15.8 %collective-permute-start.10 = (f32[128,256]{1,0:T(8,128)}, f32[128,256]{1,0:T(8,128)S(1)}, u32[]{:S(2)}, u32[]{:S(2)}) collective-permute-start(f32[128,256]{1,0:T(8,128)} %pad_maximum_fusion.1), channel_id=1, source_target_pairs={{0,1},{1,2},{2,3},{3,0},{4,5},{5,6},{6,7},{7,4},{8,9},{9,10},{10,1... | collective-permute-start | bytes 393224 | tf_op jit(solution)/shard_map/ppermute | solution.py:18
  325.7 15.2 %collective-permute-start.11 = (f32[128,256]{1,0:T(8,128)}, f32[128,256]{1,0:T(8,128)}, u32[]{:S(2)}, u32[]{:S(2)}) collective-permute-start(f32[128,256]{1,0:T(8,128)} %pad_maximum_fusion.2), channel_id=1, source_target_pairs={{0,3},{1,0},{2,1},{3,2},{4,7},{5,4},{6,5},{7,6},{8,11},{9,8},{10,9... | collective-permute-start | bytes 393224 | tf_op jit(solution)/shard_map/ppermute | solution.py:18
  331.3 15.6 %all-to-all-start.4 = ((bf16[16,64,256]{2,1,0:T(8,128)(2,1)}), bf16[16,64,256]{2,1,0:T(8,128)(2,1)}, u32[]{:S(2)}, u32[]{:S(2)}) async-start(bf16[16,64,256]{2,1,0:T(8,128)(2,1)} %bitcast.37), calls=%async_computation.4 | async-start | bytes 1048576 | tf_op jit(solution)/shard_map/all_to_all | solution.py:80
  340.8 12.1 %copy-start.8 = (f32[128,256]{1,0:T(8,128)S(1)}, f32[128,256]{1,0:T(8,128)}, u32[]{:S(2)}) copy-start(f32[128,256]{1,0:T(8,128)} %param.13) | copy-start | bytes 393220
  341.8 10.1 %collective-permute-start.12 = (f32[128,128]{1,0:T(8,128)S(1)}, f32[128,128]{1,0:T(8,128)S(1)}, u32[]{:S(2)}, u32[]{:S(2)}) collective-permute-start(f32[128,128]{1,0:T(8,128)S(1)} %constant_dynamic-slice_fusion.1), channel_id=1, source_target_pairs={{0,4},{4,0},{1,5},{5,1},{2,6},{6,2},{3,7},{7,3},{8,12},{12,8},{9,1... | collective-permute-start | bytes 196616 | tf_op jit(solution)/shard_map/ppermute | solution.py:22
  348.5 4.4 %collective-permute-start.13 = (f32[128,256]{1,0:T(8,128)S(1)}, f32[128,256]{1,0:T(8,128)S(1)}, u32[]{:S(2)}, u32[]{:S(2)}) collective-permute-start(f32[128,256]{1,0:T(8,128)S(1)} %constant_dynamic-slice_fusion), channel_id=1, source_target_pairs={{0,8},{8,0},{1,9},{9,1},{2,10},{10,2},{3,11},{11,3},{4,12},{12,4},... | collective-permute-start | bytes 393224 | tf_op jit(solution)/shard_map/ppermute | solution.py:22

commit v3 on v2

--- a/solution.py
+++ b/solution.py
@@ -38,42 +38,67 @@
     split, thin = omega_cols.shape
     tall = phi_cols.shape[0] // 8
 
-    def move(where, window, upsilon, omega, phi, pieces, first, second, third, fourth, small, sems):
+    def move(where, window, upsilon, omega, phi, pieces, first, second, third, fourth, small, w_buf, u_buf, s_buf, sems):
+        k, z = where[0], where[1]
         picks = (first, second, third, fourth)
-        k, z = where[0], where[1]
-        copies = []
+        count = 0
 
         def copy(src, dst):
-            copies.append(pltpu.make_async_copy(src, dst, sems.at[len(copies)]))
-            copies[-1].start()
+            nonlocal count
+            made = pltpu.make_async_copy(src, dst, sems.at[count])
+            count += 1
+            made.start()
+            return made
 
+        loads = []
         for i in range(8):
             for half in range(2):
                 start = pl.multiple_of(2 * i * own + (k + half) % 2 * own, own)
-                copy(window.at[:, pl.ds(start, own)], pieces.at[i, :, pl.ds(half * own, own)])
+                loads.append(copy(window.at[:, pl.ds(start, own)], w_buf.at[i, :, pl.ds(half * own, own)]))
         for at in range(4):
             for half in range(2):
                 start = pl.multiple_of((z + at) % 4 * wide + half * 4 * wide, wide)
-                copy(upsilon.at[:, pl.ds(start, wide)], picks[at].at[:, pl.ds(half * wide, wide)])
+                loads.append(copy(upsilon.at[:, pl.ds(start, wide)], u_buf.at[at, :, pl.ds(half * wide, wide)]))
+        turned = omega[...].T
+        stores = []
         for i in range(8):
-            copy(omega, small.at[i, pl.ds(0, split), :])
-            copy(phi.at[pl.ds(i * tall, tall), :], small.at[i, pl.ds(split, tall), :])
-        for one in copies:
+            s_buf[i, :, :split] = turned
+            s_buf[i, :, split:] = phi[i * tall : (i + 1) * tall, :].T
+            stores.append(copy(s_buf.at[i], small.at[i]))
+        for i in range(8):
+            loads[2 * i].wait()
+            loads[2 * i + 1].wait()
+            stores.append(copy(w_buf.at[i], pieces.at[i]))
+        for at in range(4):
+            loads[16 + 2 * at].wait()
+            loads[17 + 2 * at].wait()
+            stores.append(copy(u_buf.at[at], picks[at]))
+        for one in stores:
             one.wait()
 
     kind = window_rows.dtype
     anywhere = pl.BlockSpec(memory_space=pl.ANY)
+    near = pl.BlockSpec(memory_space=pltpu.VMEM)
     return pl.pallas_call(
         move,
-        in_specs=[pl.BlockSpec(memory_space=pltpu.SMEM)] + [anywhere] * 4,
+        in_specs=[pl.BlockSpec(memory_space=pltpu.SMEM), anywhere, anywhere, near, near],
         out_specs=[anywhere] * 6,
         out_shape=[
             jax.ShapeDtypeStruct((8, rows, 2 * own), kind),
             *[jax.ShapeDtypeStruct((deep, 2 * wide), kind)] * 4,
-            jax.ShapeDtypeStruct((8, split + tall, thin), kind),
+            jax.ShapeDtypeStruct((8, thin, split + tall), kind),
         ],
-        scratch_shapes=[pltpu.SemaphoreType.DMA((40,))],
+        scratch_shapes=[
+            pltpu.VMEM((8, rows, 2 * own), kind),
+            pltpu.VMEM((4, deep, 2 * wide), kind),
+            pltpu.VMEM((8, thin, split + tall), kind),
+            pltpu.SemaphoreType.DMA((44,)),
+        ],
     )(jnp.stack([k, z]).astype(jnp.int32), window_rows, upsilon_rows, omega_cols, phi_cols)
+
+
+def dot_down(a, b):
+    return lax.dot_general(a, b, (((0,), (0,)), ((), ())), preferred_element_type=jnp.float32)
 
 
 def exchange(value, axes):
@@ -93,9 +118,9 @@
     picks_other = [None] * 4
     for at in (2, 1, 3, 0):
         picks_other[at] = swap(picks[at])
+    psi_other = swap(psi_rows)
     relaid = exchange(pieces, PLANE).reshape(8 * rows, 2 * own)
-    relaid, *picks_other = tied(relaid, *picks_other)
-    psi_other = swap(psi_rows)
+    relaid, psi_other, *picks_other = tied(relaid, psi_other, *picks_other)
 
     def share(at):
         return dot(relaid, jnp.concatenate([picks[at], picks_other[at]], axis=0))
@@ -113,15 +138,15 @@
     co = exchange(co.reshape(8, rows, -1), PLANE)
     co = jnp.sum(co.astype(jnp.float32), axis=0) * (1.0 / NEAR)
 
-    mine, co, *sent = tied(mine, co, *sent)
+    mine, co, small, *sent = tied(mine, co, small, *sent)
     total = mine + (1.0 / NEAR) * sum(s.astype(jnp.float32) for s in sent)
     sk = (FAR * total).astype(WIRE).reshape(16, rows // 2, 2 * wide)
     sk = exchange(sk, TILE)
 
-    omega = jnp.moveaxis(small[:, :split], 0, 1).reshape(split, -1)
-    phi = jnp.moveaxis(small[:, split:], 0, 1).reshape(-1, 8 * phi_cols.shape[1])
-    range_given = dot(omega, relaid[:, own:])
-    range_kept = dot(omega, relaid[:, :own])
+    small = small.reshape(8 * rows, -1)
+    omega, phi = small[:, :split], small[:, split:]
+    range_given = dot_down(omega, relaid[:, own:])
+    range_kept = dot_down(omega, relaid[:, :own])
     range_sketch = range_old + range_kept + swap(range_given)
 
     def pick(value, at, wide):
@@ -140,7 +165,7 @@
     sk = jnp.stack([sk[:, :wide], sk[:, wide:]])
     sk = jnp.broadcast_to(sk[None], (8,) + sk.shape).reshape(16, rows // 2, wide)
     sk = exchange(sk, TILE)
-    term = dot(phi, sk.reshape(8 * rows, wide))
+    term = dot_down(phi, sk.reshape(8 * rows, wide))
     here = lax.dynamic_slice_in_dim(term, k * rows, rows, 0)
     there = lax.dynamic_slice_in_dim(term, (1 - k) * rows, rows, 0)
     core_sketch = core_old + here + swap(there)

time: 354 us -> 182 us (0.51)
  Pallas kernels: 177 us -> 6.28 us
  local copies, waits for them, and re-layouts: 9.41 us -> 2.93 us
  waiting for transfers between devices: 83.2 us -> 88.1 us
    pallas_call x1, Pallas kernels: 177 us -> 6.28 us  [arrange(): pl.pallas_call(move, in_specs=[pl.BlockSpec(memory_space=pltpu.SMEM), any...]
    dot_general x0 -> x3, matrix products: none -> 7.71 us  [dot_down(): lax.dot_general(a, b, (((0,), (0,)), ((), ())), preferred_element_type=jn...]
    dot_general x8 -> x5, matrix products: 24.6 us -> 17.1 us  [dot(): return jnp.dot(a, b, preferred_element_type=jnp.float32)]
    transpose x4 -> x0, local copies, waits for them, and re-layouts: 4.76 us -> none  [the longest x2 2.67 us: body(): omega = jnp.moveaxis(small[:, :split], 0, 1).reshape(split, -1)]
    ppermute x8, waiting for transfers between devices: 2.59 us -> 6.42 us  [swap(): return lax.ppermute(value, axis, [(0, 1), (1, 0)])]
  transfers between devices with their start and end apart: 19 -> 19, of which waited for: 11 -> 12; matrix products, arithmetic and copies ran while one was open for 10% -> 18% of each run, Pallas kernels for 0% -> 0%
where the time goes in v3:
time: 182 us; the launch traced here: 181 us
  waiting for transfers between devices  88.1 us (48%)
  starting transfers between devices  48.5 us (27%)
  matrix products  24.8 us (14%)
  other arithmetic  9.69 us (5%)
  Pallas kernels  6.28 us (3%)
  local copies, waits for them, and re-layouts  2.93 us (2%)
    all_to_all x5, waiting for transfers between devices, exchange(): return lax.all_to_all(value, axes, 0, 0, tiled=True)  55.2 us
    all_to_all x5, starting transfers between devices, exchange(): return lax.all_to_all(value, axes, 0, 0, tiled=True)  29.1 us
    ppermute x6, waiting for transfers between devices, shift(): return lax.ppermute(value, axis, [(i, (i + by) % n) for i in range(n)])  26.4 us
    dot_general x5, matrix products, dot(): return jnp.dot(a, b, preferred_element_type=jnp.float32)  17.1 us
    ppermute x8, starting transfers between devices, swap(): return lax.ppermute(value, axis, [(0, 1), (1, 0)])  9.78 us
    ppermute x6, starting transfers between devices, shift(): return lax.ppermute(value, axis, [(i, (i + by) % n) for i in range(n)])  9.65 us
    dot_general x3, matrix products, dot_down(): lax.dot_general(a, b, (((0,), (0,)), ((), ())), preferred_element_type=jn...  7.71 us
    ppermute x8, waiting for transfers between devices, swap(): return lax.ppermute(value, axis, [(0, 1), (1, 0)])  6.42 us
  transfers between devices with their start and end apart: 19, of which 12 were waited for; matrix products, arithmetic and copies ran while one was open for 18% of the time, Pallas kernels for 0%

profile of v3, /device:TPU:1, one launch (start us, length us, event | category | flops | bytes accessed | tf_op | source)
XLA Modules:
  0.0 181.3 jit_solution(6151758882232115902)
XLA Ops:
  0.6 0.6 pad_add_fusion.where
  1.2 6.3 %shard_map.94 = (bf16[8,128,1024]{2,1,0:T(8,128)(2,1)}, bf16[512,512]{1,0:T(8,128)(2,1)}, bf16[512,512]{1,0:T(8,128)(2,1)}, bf16[512,512]{1,0:T(8,128)(2,1)}, bf...) custom-call(s32[2]{0:T(128)} %pad_add_fusion.where, bf16[128,8192]{1,0:T(8,128)(2,1)} %window.1, ...), custom_call_target="tpu_custom_call" | custom-call | tf_op jit(solution)/shard_map/pallas_call | solution.py:82
  7.5 0.0 copy-start.6
  7.5 7.6 %all-to-all-start = ((bf16[8,128,1024]{2,1,0:T(8,128)(2,1)}), bf16[8,128,1024]{2,1,0:T(8,128)(2,1)S(1)}, u32[]{:S(2)}, u32[]{:S(2)}) async-start(bf16[8,128,1024]{2,1,0:T(8,128)(2,1)} %get-tuple-element.25), calls=%async_computation | async-start | bytes 4194304 | tf_op jit(solution)/shard_map/all_to_all | solution.py:105
  15.1 1.0 collective-permute-start
  16.2 0.1 collective-permute-start.1
  16.3 0.4 collective-permute-start.2
  16.7 0.1 collective-permute-start.3
  16.8 0.4 collective-permute-start.4
  17.2 2.0 %collective-permute-done.1 = bf16[512,512]{1,0:T(8,128)(2,1)S(1)} collective-permute-done((bf16[512,512]{1,0:T(8,128)(2,1)}, bf16[512,512]{1,0:T(8,128)(2,1)S(1)}, u32[]{:S(2)}, u32[]{:S(2)}) %collective-permute-start.1) | collective-permute-done | bytes 524320 | tf_op jit(solution)/shard_map/ppermute | solution.py:22
  19.2 0.7 collective-permute-done.2
  20.0 0.7 collective-permute-done.3
  20.7 0.7 collective-permute-done.4
  21.5 0.1 copy-done.10
  21.5 0.8 copy-done.14
  22.3 0.0 collective-permute-done
  22.3 21.4 %all-to-all-done = bf16[8,128,1024]{2,1,0:T(8,128)(2,1)S(1)} async-done(((bf16[8,128,1024]{2,1,0:T(8,128)(2,1)}), bf16[8,128,1024]{2,1,0:T(8,128)(2,1)S(1)}, u32[]{:S(2)}, u32[]{:S(2)}) %all-to-all-start) | async-done | bytes 2097184 | tf_op jit(solution)/shard_map/all_to_all | solution.py:105
  43.7 4.7 %all-to-all-start.1 = ((bf16[8,128,768]{2,1,0:T(8,128)(2,1)}), bf16[8,128,768]{2,1,0:T(8,128)(2,1)}, u32[]{:S(2)}, u32[]{:S(2)}) async-start(bf16[8,128,768]{2,1,0:T(8,128)(2,1)} %get-tuple-element.33), calls=%async_computation.1 | async-start | bytes 3145728 | tf_op jit(solution)/shard_map/all_to_all | solution.py:105
  48.4 3.8 %fusion.4 = f32[1024,512]{1,0:T(8,128)} fusion(bf16[1024,1024]{1,0:T(8,128)(2,1)S(1)} %bitcast.18, bf16[512,512]{1,0:T(8,128)(2,1)} %copy-done.16, bf16[512,512]{1,0:T(8,128)(2,1)} %get-tuple-element.26), kind=kOutput, calls=%fused_computation.12 | convolution fusion | flops 1075838976 | bytes 5242880 | tf_op jit(solution)/shard_map/dot_general | solution.py:26
  52.2 4.9 %multiply_convert_fusion = f16[1024,1024]{1,0:T(8,128)(2,1)} fusion(bf16[1024,1024]{1,0:T(8,128)(2,1)S(1)} %bitcast.19, bf16[512,1024]{1,0:T(8,128)(2,1)} %collective-permute-done, bf16[512,1024]{1,0:T(8,128)(2,1)S(1)} %copy-done.6), kind=kOutput, calls=%fused_computation.1 | convolution fusion | flops 2153775104 | bytes 6291456 | tf_op jit(solution)/shard_map/dot_general | solution.py:26
  57.2 14.4 %all-to-all-done.1 = bf16[8,128,768]{2,1,0:T(8,128)(2,1)} async-done(((bf16[8,128,768]{2,1,0:T(8,128)(2,1)}), bf16[8,128,768]{2,1,0:T(8,128)(2,1)}, u32[]{:S(2)}, u32[]{:S(2)}) %all-to-all-start.1) | async-done | bytes 1572896 | tf_op jit(solution)/shard_map/all_to_all | solution.py:105
  71.5 3.7 %all-to-all-start.2 = ((f16[8,128,1024]{2,1,0:T(8,128)(2,1)}), f16[8,128,1024]{2,1,0:T(8,128)(2,1)S(1)}, u32[]{:S(2)}, u32[]{:S(2)}) async-start(f16[8,128,1024]{2,1,0:T(8,128)(2,1)} %bitcast.26), calls=%async_computation.2 | async-start | bytes 4194304 | tf_op jit(solution)/shard_map/all_to_all | solution.py:105
  75.3 4.0 %multiply_convert_fusion.2 = f16[1024,512]{1,0:T(8,128)(2,1)} fusion(bf16[1024,1024]{1,0:T(8,128)(2,1)} %bitcast.20, bf16[512,512]{1,0:T(8,128)(2,1)S(1)} %copy-done.15, bf16[512,512]{1,0:T(8,128)(2,1)S(1)} %copy-done.9), kind=kOutput, calls=%fused_computation.7 | convolution fusion | flops 1076887552 | bytes 4194304 | tf_op jit(solution)/shard_map/dot_general | solution.py:26
  79.3 3.8 %collective-permute-start.7 = (f16[1024,512]{1,0:T(8,128)(2,1)}, f16[1024,512]{1,0:T(8,128)(2,1)S(1)}, u32[]{:S(2)}, u32[]{:S(2)}) collective-permute-start(f16[1024,512]{1,0:T(8,128)(2,1)} %multiply_convert_fusion.2), channel_id=1, source_target_pairs={{0,3},{1,0},{2,1},{3,2},{4,7},{5,4},{6,5},{7,6},{8,11},{9,8},{10,9... | collective-permute-start | bytes 3145736 | tf_op jit(solution)/shard_map/ppermute | solution.py:18
  83.1 2.2 %multiply_convert_fusion.3 = f16[1024,512]{1,0:T(8,128)(2,1)} fusion(bf16[1024,1024]{1,0:T(8,128)(2,1)S(1)} %bitcast.21, bf16[512,512]{1,0:T(8,128)(2,1)S(1)} %copy-done.13, bf16[512,512]{1,0:T(8,128)(2,1)S(1)} %copy-done.8), kind=kOutput, calls=%fused_computation.8 | convolution fusion | flops 1076887552 | bytes 4194304 | tf_op jit(solution)/shard_map/dot_general | solution.py:26
  85.3 0.0 collective-permute-start.6
  85.3 2.2 %multiply_convert_fusion.4 = f16[1024,512]{1,0:T(8,128)(2,1)} fusion(bf16[1024,1024]{1,0:T(8,128)(2,1)S(1)} %bitcast.22, bf16[512,512]{1,0:T(8,128)(2,1)S(1)} %copy-done.11, bf16[512,512]{1,0:T(8,128)(2,1)S(1)} %copy-done.7), kind=kOutput, calls=%fused_computation.9 | convolution fusion | flops 1076887552 | bytes 4194304 | tf_op jit(solution)/shard_map/dot_general | solution.py:26
  87.5 1.3 collective-permute-start.5
  88.8 15.0 %all-to-all-done.2 = f16[8,128,1024]{2,1,0:T(8,128)(2,1)S(1)} async-done(((f16[8,128,1024]{2,1,0:T(8,128)(2,1)}), f16[8,128,1024]{2,1,0:T(8,128)(2,1)S(1)}, u32[]{:S(2)}, u32[]{:S(2)}) %all-to-all-start.2) | async-done | bytes 2097184 | tf_op jit(solution)/shard_map/all_to_all | solution.py:105
  103.8 0.5 convert_reduce_fusion
  104.3 0.8 broadcast_multiply_fusion
  105.2 22.2 %collective-permute-done.7 = f16[1024,512]{1,0:T(8,128)(2,1)S(1)} collective-permute-done((f16[1024,512]{1,0:T(8,128)(2,1)}, f16[1024,512]{1,0:T(8,128)(2,1)S(1)}, u32[]{:S(2)}, u32[]{:S(2)}) %collective-permute-start.7) | collective-permute-done | bytes 1048608 | tf_op jit(solution)/shard_map/ppermute | solution.py:18
  127.4 0.0 collective-permute-done.6
  127.4 4.2 %collective-permute-done.5 = f16[1024,512]{1,0:T(8,128)(2,1)} collective-permute-done((f16[1024,512]{1,0:T(8,128)(2,1)}, f16[1024,512]{1,0:T(8,128)(2,1)}, u32[]{:S(2)}, u32[]{:S(2)}) %collective-permute-start.5) | collective-permute-done | bytes 1048608 | tf_op jit(solution)/shard_map/ppermute | solution.py:18
  131.6 3.3 %multiply_convert_fusion.1 = f16[1024,512]{1,0:T(8,128)(2,1)} fusion(f32[1024,512]{1,0:T(8,128)S(1)} %copy-done.3, f16[1024,512]{1,0:T(8,128)(2,1)S(1)} %collective-permute-done.7, f16[1024,512]{1,0:T(8,128)(2,1)} %collective-permute-done.6, f16[1024,512]{1,0:T(8,128)(2,1)} %collective-permute-done.5), kind=kLoop, calls=%fused_computation.6 | loop fusion | flops 4718592 | bytes 6291456 | tf_op jit(solution)/shard_map/convert_element_type | solution.py:143
  134.9 6.5 %all-to-all-start.3 = ((f16[16,64,512]{2,1,0:T(8,128)(2,1)}), f16[16,64,512]{2,1,0:T(8,128)(2,1)S(1)}, u32[]{:S(2)}, u32[]{:S(2)}) async-start(f16[16,64,512]{2,1,0:T(8,128)(2,1)} %bitcast.25), calls=%async_computation.3 | async-start | bytes 2097152 | tf_op jit(solution)/shard_map/all_to_all | solution.py:105
  141.5 1.1 constant_dynamic-slice_fusion.9
  142.7 0.7 pad_maximum_fusion
  143.3 1.9 %collective-permute-start.9 = (f32[128,256]{1,0:T(8,128)}, f32[128,256]{1,0:T(8,128)S(1)}, u32[]{:S(2)}, u32[]{:S(2)}) collective-permute-start(f32[128,256]{1,0:T(8,128)} %pad_maximum_fusion), channel_id=1, source_target_pairs={{0,2},{1,3},{2,0},{3,1},{4,6},{5,7},{6,4},{7,5},{8,10},{9,11},{10,... | collective-permute-start | bytes 393224 | tf_op jit(solution)/shard_map/ppermute | solution.py:18
  145.2 0.7 pad_maximum_fusion.1
  145.9 0.0 collective-permute-start.10
  145.9 0.7 pad_maximum_fusion.2
  146.5 2.7 %collective-permute-start.11 = (f32[128,256]{1,0:T(8,128)}, f32[128,256]{1,0:T(8,128)}, u32[]{:S(2)}, u32[]{:S(2)}) collective-permute-start(f32[128,256]{1,0:T(8,128)} %pad_maximum_fusion.2), channel_id=1, source_target_pairs={{0,3},{1,0},{2,1},{3,2},{4,7},{5,4},{6,5},{7,6},{8,11},{9,8},{10,9... | collective-permute-start | bytes 393224 | tf_op jit(solution)/shard_map/ppermute | solution.py:18
  149.2 2.9 %fusion.17 = f32[512,512]{1,0:T(8,128)} fusion(bf16[1024,1024]{1,0:T(8,128)(2,1)S(1)} %bitcast.23, bf16[1024,768]{1,0:T(8,128)(2,1)} %bitcast.4), kind=kOutput, calls=%fused_computation.25 | convolution fusion | flops 536870912 | bytes 3145728 | tf_op jit(solution)/shard_map/dot_general | solution.py:101
  152.1 3.0 %collective-permute-start.8 = (f32[512,512]{1,0:T(8,128)}, f32[512,512]{1,0:T(8,128)}, u32[]{:S(2)}, u32[]{:S(2)}) collective-permute-start(f32[512,512]{1,0:T(8,128)} %fusion.17), channel_id=1, source_target_pairs={{0,8},{8,0},{1,9},{9,1},{2,10},{10,2},{3,11},{11,3},{4,12},{12,4},... | collective-permute-start | bytes 3145736 | tf_op jit(solution)/shard_map/ppermute | solution.py:22
  155.2 0.4 all-to-all-done.3
  155.6 0.1 convert_reduce_fusion.1
  155.8 0.0 copy-start.4
  155.8 0.9 broadcast_in_dim.2
  156.6 6.5 %all-to-all-start.4 = ((bf16[16,64,256]{2,1,0:T(8,128)(2,1)}), bf16[16,64,256]{2,1,0:T(8,128)(2,1)}, u32[]{:S(2)}, u32[]{:S(2)}) async-start(bf16[16,64,256]{2,1,0:T(8,128)(2,1)} %bitcast.8), calls=%async_computation.4 | async-start | bytes 1048576 | tf_op jit(solution)/shard_map/all_to_all | solution.py:105
  163.2 0.0 collective-permute-done.9
  163.2 0.0 collective-permute-done.10
  163.2 1.0 fusion.25
  164.2 1.4 collective-permute-start.12
  165.6 2.2 %collective-permute-done.12 = f32[128,128]{1,0:T(8,128)S(1)} collective-permute-done((f32[128,128]{1,0:T(8,128)S(1)}, f32[128,128]{1,0:T(8,128)S(1)}, u32[]{:S(2)}, u32[]{:S(2)}) %collective-permute-start.12) | collective-permute-done | bytes 65568 | tf_op jit(solution)/shard_map/ppermute | solution.py:22
  167.8 0.6 dynamic-slice_add_fusion
  168.4 4.1 %all-to-all-done.4 = bf16[16,64,256]{2,1,0:T(8,128)(2,1)} async-done(((bf16[16,64,256]{2,1,0:T(8,128)(2,1)}), bf16[16,64,256]{2,1,0:T(8,128)(2,1)}, u32[]{:S(2)}, u32[]{:S(2)}) %all-to-all-start.4) | async-done | bytes 524320 | tf_op jit(solution)/shard_map/all_to_all | solution.py:105
  172.5 1.5 fusion.22
  174.0 0.0 copy-start.5
  174.0 3.3 %collective-permute-start.13 = (f32[128,256]{1,0:T(8,128)S(1)}, f32[128,256]{1,0:T(8,128)S(1)}, u32[]{:S(2)}, u32[]{:S(2)}) collective-permute-start(f32[128,256]{1,0:T(8,128)S(1)} %constant_dynamic-slice_fusion), channel_id=1, source_target_pairs={{0,8},{8,0},{1,9},{9,1},{2,10},{10,2},{3,11},{11,3},{4,12},{12,4},... | collective-permute-start | bytes 393224 | tf_op jit(solution)/shard_map/ppermute | solution.py:22
  177.3 0.0 collective-permute-done.8
  177.3 3.2 %fusion.3 = f32[512,512]{1,0:T(8,128)} fusion(f32[512,512]{1,0:T(8,128)} %collective-permute-done.8, f32[512,512]{1,0:T(8,128)S(1)} %copy-done.4, bf16[1024,1024]{1,0:T(8,128)(2,1)S(1)} %bitcast.24, bf16[1024,768]{1,0:T(8,128)(2,1)} %bitcast.4), kind=kOutput, calls=%fused_computation.11 | convolution fusion | flops 537395200 | bytes 5242880 | tf_op jit(solution)/shard_map/dot_general | solution.py:101
  180.6 0.0 collective-permute-done.13
  180.6 0.7 add_add_fusion
  (35 shorter events, 0.1 us)
Async XLA Ops:
  7.5 7.6 %copy-start.6 = (bf16[512,1024]{1,0:T(8,128)(2,1)S(1)}, bf16[512,1024]{1,0:T(8,128)(2,1)}, u32[]{:S(2)}) copy-start(bf16[512,1024]{1,0:T(8,128)(2,1)} %param.9) | copy-start | bytes 3145732
  7.5 36.2 %all-to-all-start = ((bf16[8,128,1024]{2,1,0:T(8,128)(2,1)}), bf16[8,128,1024]{2,1,0:T(8,128)(2,1)S(1)}, u32[]{:S(2)}, u32[]{:S(2)}) async-start(bf16[8,128,1024]{2,1,0:T(8,128)(2,1)} %get-tuple-element.25), calls=%async_computation | async-start | bytes 4194304 | tf_op jit(solution)/shard_map/all_to_all | solution.py:105
  15.1 7.2 %collective-permute-start = (bf16[512,1024]{1,0:T(8,128)(2,1)S(1)}, bf16[512,1024]{1,0:T(8,128)(2,1)}, u32[]{:S(2)}, u32[]{:S(2)}) collective-permute-start(bf16[512,1024]{1,0:T(8,128)(2,1)S(1)} %copy-done.6), channel_id=1, source_target_pairs={{0,8},{8,0},{1,9},{9,1},{2,10},{10,2},{3,11},{11,3},{4,12},{12,4},... | collective-permute-start | bytes 3145736 | tf_op jit(solution)/shard_map/ppermute | solution.py:22
  16.2 3.0 %collective-permute-start.1 = (bf16[512,512]{1,0:T(8,128)(2,1)}, bf16[512,512]{1,0:T(8,128)(2,1)S(1)}, u32[]{:S(2)}, u32[]{:S(2)}) collective-permute-start(bf16[512,512]{1,0:T(8,128)(2,1)} %get-tuple-element.26), channel_id=1, source_target_pairs={{0,8},{8,0},{1,9},{9,1},{2,10},{10,2},{3,11},{11,3},{4,12},{12,4},... | collective-permute-start | bytes 1572872 | tf_op jit(solution)/shard_map/ppermute | solution.py:22
  16.3 3.7 %collective-permute-start.2 = (bf16[512,512]{1,0:T(8,128)(2,1)}, bf16[512,512]{1,0:T(8,128)(2,1)S(1)}, u32[]{:S(2)}, u32[]{:S(2)}) collective-permute-start(bf16[512,512]{1,0:T(8,128)(2,1)} %get-tuple-element.27), channel_id=1, source_target_pairs={{0,8},{8,0},{1,9},{9,1},{2,10},{10,2},{3,11},{11,3},{4,12},{12,4},... | collective-permute-start | bytes 1572872 | tf_op jit(solution)/shard_map/ppermute | solution.py:22
  16.7 4.0 %collective-permute-start.3 = (bf16[512,512]{1,0:T(8,128)(2,1)}, bf16[512,512]{1,0:T(8,128)(2,1)S(1)}, u32[]{:S(2)}, u32[]{:S(2)}) collective-permute-start(bf16[512,512]{1,0:T(8,128)(2,1)} %get-tuple-element.28), channel_id=1, source_target_pairs={{0,8},{8,0},{1,9},{9,1},{2,10},{10,2},{3,11},{11,3},{4,12},{12,4},... | collective-permute-start | bytes 1572872 | tf_op jit(solution)/shard_map/ppermute | solution.py:22
  16.8 4.7 %collective-permute-start.4 = (bf16[512,512]{1,0:T(8,128)(2,1)}, bf16[512,512]{1,0:T(8,128)(2,1)S(1)}, u32[]{:S(2)}, u32[]{:S(2)}) collective-permute-start(bf16[512,512]{1,0:T(8,128)(2,1)} %get-tuple-element.29), channel_id=1, source_target_pairs={{0,8},{8,0},{1,9},{9,1},{2,10},{10,2},{3,11},{11,3},{4,12},{12,4},... | collective-permute-start | bytes 1572872 | tf_op jit(solution)/shard_map/ppermute | solution.py:22
  19.2 2.3 %copy-start.16 = (bf16[512,512]{1,0:T(8,128)(2,1)}, bf16[512,512]{1,0:T(8,128)(2,1)S(1)}, u32[]{:S(2)}) copy-start(bf16[512,512]{1,0:T(8,128)(2,1)S(1)} %collective-permute-done.1) | copy-start | bytes 1572868
  20.0 1.5 copy-start.12
  20.7 0.8 copy-start.10
  21.5 0.8 copy-start.14
  43.7 8.5 %copy-start = (bf16[8,128,1024]{2,1,0:T(8,128)(2,1)}, bf16[8,128,1024]{2,1,0:T(8,128)(2,1)S(1)}, u32[]{:S(2)}) copy-start(bf16[8,128,1024]{2,1,0:T(8,128)(2,1)S(1)} %all-to-all-done) | copy-start | bytes 6291460
  43.7 27.8 %all-to-all-start.1 = ((bf16[8,128,768]{2,1,0:T(8,128)(2,1)}), bf16[8,128,768]{2,1,0:T(8,128)(2,1)}, u32[]{:S(2)}, u32[]{:S(2)}) async-start(bf16[8,128,768]{2,1,0:T(8,128)(2,1)} %get-tuple-element.33), calls=%async_computation.1 | async-start | bytes 3145728 | tf_op jit(solution)/shard_map/all_to_all | solution.py:105
  71.5 3.7 %copy-start.9 = (bf16[512,512]{1,0:T(8,128)(2,1)S(1)}, bf16[512,512]{1,0:T(8,128)(2,1)}, u32[]{:S(2)}) copy-start(bf16[512,512]{1,0:T(8,128)(2,1)} %get-tuple-element.29) | copy-start | bytes 1572868
  71.5 3.8 %copy-start.15 = (bf16[512,512]{1,0:T(8,128)(2,1)S(1)}, bf16[512,512]{1,0:T(8,128)(2,1)}, u32[]{:S(2)}) copy-start(bf16[512,512]{1,0:T(8,128)(2,1)} %copy-done.14) | copy-start | bytes 1572868
  71.5 32.3 %all-to-all-start.2 = ((f16[8,128,1024]{2,1,0:T(8,128)(2,1)}), f16[8,128,1024]{2,1,0:T(8,128)(2,1)S(1)}, u32[]{:S(2)}, u32[]{:S(2)}) async-start(f16[8,128,1024]{2,1,0:T(8,128)(2,1)} %bitcast.26), calls=%async_computation.2 | async-start | bytes 4194304 | tf_op jit(solution)/shard_map/all_to_all | solution.py:105
  75.3 7.8 %copy-start.1 = (bf16[8,128,1024]{2,1,0:T(8,128)(2,1)S(1)}, bf16[8,128,1024]{2,1,0:T(8,128)(2,1)}, u32[]{:S(2)}) copy-start(bf16[8,128,1024]{2,1,0:T(8,128)(2,1)} %copy-done) | copy-start | bytes 6291460
  75.3 7.7 %copy-start.8 = (bf16[512,512]{1,0:T(8,128)(2,1)S(1)}, bf16[512,512]{1,0:T(8,128)(2,1)}, u32[]{:S(2)}) copy-start(bf16[512,512]{1,0:T(8,128)(2,1)} %get-tuple-element.27) | copy-start | bytes 1572868
  75.3 7.7 %copy-start.13 = (bf16[512,512]{1,0:T(8,128)(2,1)S(1)}, bf16[512,512]{1,0:T(8,128)(2,1)}, u32[]{:S(2)}) copy-start(bf16[512,512]{1,0:T(8,128)(2,1)} %copy-done.12) | copy-start | bytes 1572868
  79.3 6.0 %copy-start.7 = (bf16[512,512]{1,0:T(8,128)(2,1)S(1)}, bf16[512,512]{1,0:T(8,128)(2,1)}, u32[]{:S(2)}) copy-start(bf16[512,512]{1,0:T(8,128)(2,1)} %get-tuple-element.28) | copy-start | bytes 1572868
  79.3 6.0 %copy-start.11 = (bf16[512,512]{1,0:T(8,128)(2,1)S(1)}, bf16[512,512]{1,0:T(8,128)(2,1)}, u32[]{:S(2)}) copy-start(bf16[512,512]{1,0:T(8,128)(2,1)} %copy-done.10) | copy-start | bytes 1572868
  79.3 48.1 %collective-permute-start.7 = (f16[1024,512]{1,0:T(8,128)(2,1)}, f16[1024,512]{1,0:T(8,128)(2,1)S(1)}, u32[]{:S(2)}, u32[]{:S(2)}) collective-permute-start(f16[1024,512]{1,0:T(8,128)(2,1)} %multiply_convert_fusion.2), channel_id=1, source_target_pairs={{0,3},{1,0},{2,1},{3,2},{4,7},{5,4},{6,5},{7,6},{8,11},{9,8},{10,9... | collective-permute-start | bytes 3145736 | tf_op jit(solution)/shard_map/ppermute | solution.py:18
  85.3 42.2 %collective-permute-start.6 = (f16[1024,512]{1,0:T(8,128)(2,1)}, f16[1024,512]{1,0:T(8,128)(2,1)}, u32[]{:S(2)}, u32[]{:S(2)}) collective-permute-start(f16[1024,512]{1,0:T(8,128)(2,1)} %multiply_convert_fusion.3), channel_id=1, source_target_pairs={{0,1},{1,2},{2,3},{3,0},{4,5},{5,6},{6,7},{7,4},{8,9},{9,10},{10,1... | collective-permute-start | bytes 3145736 | tf_op jit(solution)/shard_map/ppermute | solution.py:18
  87.5 44.1 %collective-permute-start.5 = (f16[1024,512]{1,0:T(8,128)(2,1)}, f16[1024,512]{1,0:T(8,128)(2,1)}, u32[]{:S(2)}, u32[]{:S(2)}) collective-permute-start(f16[1024,512]{1,0:T(8,128)(2,1)} %multiply_convert_fusion.4), channel_id=1, source_target_pairs={{0,2},{1,3},{2,0},{3,1},{4,6},{5,7},{6,4},{7,5},{8,10},{9,11},{10,... | collective-permute-start | bytes 3145736 | tf_op jit(solution)/shard_map/ppermute | solution.py:18
  103.8 27.8 %copy-start.3 = (f32[1024,512]{1,0:T(8,128)S(1)}, f32[1024,512]{1,0:T(8,128)}, u32[]{:S(2)}) copy-start(f32[1024,512]{1,0:T(8,128)} %fusion.4) | copy-start | bytes 6291460
  134.9 14.3 %copy-start.2 = (bf16[8,128,1024]{2,1,0:T(8,128)(2,1)S(1)}, bf16[8,128,1024]{2,1,0:T(8,128)(2,1)}, u32[]{:S(2)}) copy-start(bf16[8,128,1024]{2,1,0:T(8,128)(2,1)} %copy-done) | copy-start | bytes 6291460
  134.9 20.6 %all-to-all-start.3 = ((f16[16,64,512]{2,1,0:T(8,128)(2,1)}), f16[16,64,512]{2,1,0:T(8,128)(2,1)S(1)}, u32[]{:S(2)}, u32[]{:S(2)}) async-start(f16[16,64,512]{2,1,0:T(8,128)(2,1)} %bitcast.25), calls=%async_computation.3 | async-start | bytes 2097152 | tf_op jit(solution)/shard_map/all_to_all | solution.py:105
  143.3 19.8 %collective-permute-start.9 = (f32[128,256]{1,0:T(8,128)}, f32[128,256]{1,0:T(8,128)S(1)}, u32[]{:S(2)}, u32[]{:S(2)}) collective-permute-start(f32[128,256]{1,0:T(8,128)} %pad_maximum_fusion), channel_id=1, source_target_pairs={{0,2},{1,3},{2,0},{3,1},{4,6},{5,7},{6,4},{7,5},{8,10},{9,11},{10,... | collective-permute-start | bytes 393224 | tf_op jit(solution)/shard_map/ppermute | solution.py:18
  145.9 17.3 %collective-permute-start.10 = (f32[128,256]{1,0:T(8,128)}, f32[128,256]{1,0:T(8,128)}, u32[]{:S(2)}, u32[]{:S(2)}) collective-permute-start(f32[128,256]{1,0:T(8,128)} %pad_maximum_fusion.1), channel_id=1, source_target_pairs={{0,1},{1,2},{2,3},{3,0},{4,5},{5,6},{6,7},{7,4},{8,9},{9,10},{10,1... | collective-permute-start | bytes 393224 | tf_op jit(solution)/shard_map/ppermute | solution.py:18
  146.5 16.6 %collective-permute-start.11 = (f32[128,256]{1,0:T(8,128)}, f32[128,256]{1,0:T(8,128)}, u32[]{:S(2)}, u32[]{:S(2)}) collective-permute-start(f32[128,256]{1,0:T(8,128)} %pad_maximum_fusion.2), channel_id=1, source_target_pairs={{0,3},{1,0},{2,1},{3,2},{4,7},{5,4},{6,5},{7,6},{8,11},{9,8},{10,9... | collective-permute-start | bytes 393224 | tf_op jit(solution)/shard_map/ppermute | solution.py:18
  152.1 25.2 %collective-permute-start.8 = (f32[512,512]{1,0:T(8,128)}, f32[512,512]{1,0:T(8,128)}, u32[]{:S(2)}, u32[]{:S(2)}) collective-permute-start(f32[512,512]{1,0:T(8,128)} %fusion.17), channel_id=1, source_target_pairs={{0,8},{8,0},{1,9},{9,1},{2,10},{10,2},{3,11},{11,3},{4,12},{12,4},... | collective-permute-start | bytes 3145736 | tf_op jit(solution)/shard_map/ppermute | solution.py:22
  155.8 21.6 %copy-start.4 = (f32[512,512]{1,0:T(8,128)S(1)}, f32[512,512]{1,0:T(8,128)}, u32[]{:S(2)}) copy-start(f32[512,512]{1,0:T(8,128)} %param.12) | copy-start | bytes 3145732
  156.6 15.8 %all-to-all-start.4 = ((bf16[16,64,256]{2,1,0:T(8,128)(2,1)}), bf16[16,64,256]{2,1,0:T(8,128)(2,1)}, u32[]{:S(2)}, u32[]{:S(2)}) async-start(bf16[16,64,256]{2,1,0:T(8,128)(2,1)} %bitcast.8), calls=%async_computation.4 | async-start | bytes 1048576 | tf_op jit(solution)/shard_map/all_to_all | solution.py:105
  164.2 3.5 %collective-permute-start.12 = (f32[128,128]{1,0:T(8,128)S(1)}, f32[128,128]{1,0:T(8,128)S(1)}, u32[]{:S(2)}, u32[]{:S(2)}) collective-permute-start(f32[128,128]{1,0:T(8,128)S(1)} %constant_dynamic-slice_fusion.1), channel_id=1, source_target_pairs={{0,4},{4,0},{1,5},{5,1},{2,6},{6,2},{3,7},{7,3},{8,12},{12,8},{9,1... | collective-permute-start | bytes 196616 | tf_op jit(solution)/shard_map/ppermute | solution.py:22
  174.0 6.6 %copy-start.5 = (f32[128,256]{1,0:T(8,128)S(1)}, f32[128,256]{1,0:T(8,128)}, u32[]{:S(2)}) copy-start(f32[128,256]{1,0:T(8,128)} %param.13) | copy-start | bytes 393220
  174.0 6.5 %collective-permute-start.13 = (f32[128,256]{1,0:T(8,128)S(1)}, f32[128,256]{1,0:T(8,128)S(1)}, u32[]{:S(2)}, u32[]{:S(2)}) collective-permute-start(f32[128,256]{1,0:T(8,128)S(1)} %constant_dynamic-slice_fusion), channel_id=1, source_target_pairs={{0,8},{8,0},{1,9},{9,1},{2,10},{10,2},{3,11},{11,3},{4,12},{12,4},... | collective-permute-start | bytes 393224 | tf_op jit(solution)/shard_map/ppermute | solution.py:22

commit v4 on v3

v4 whole, which is shorter than its diff:
```python
import jax
import jax.numpy as jnp
from jax import lax
from jax.experimental import pallas as pl
from jax.experimental.pallas import tpu as pltpu
from jax.sharding import Mesh, PartitionSpec as P


PLANE = ("yh", "x")
TILE = ("yh", "x", "yl")
WIRE = jnp.float16
NEAR = 64.0
FAR = 16.0


def shift(value, axis, by):
    n = lax.axis_size(axis)
    return lax.ppermute(value, axis, [(i, (i + by) % n) for i in range(n)])


def swap(value, axis="k"):
    return lax.ppermute(value, axis, [(0, 1), (1, 0)])


def dot(a, b):
    return jnp.dot(a, b, preferred_element_type=jnp.float32)


def tied(*values):
    return lax.optimization_barrier(values)


def launcher(sems):
    started = []

    def copy(src, dst):
        made = pltpu.make_async_copy(src, dst, sems.at[len(started)])
        started.append(made)
        made.start()
        return made

    return copy


ANYWHERE = pl.BlockSpec(memory_space=pl.ANY)
NEARBY = pl.BlockSpec(memory_space=pltpu.VMEM)
SCALARS = pl.BlockSpec(memory_space=pltpu.SMEM)


def cut_window(where, window_rows):
    rows, cols = window_rows.shape
    own = cols // 16

    def move(where, window, pieces, buf, sems):
        k = where[0]
        copy = launcher(sems)
        loads = []
        for i in range(8):
            for half in range(2):
                start = pl.multiple_of(2 * i * own + (k + half) % 2 * own, own)
                loads.append(copy(window.at[:, pl.ds(start, own)], buf.at[i, :, pl.ds(half * own, own)]))
        stores = []
        for i in range(8):
            loads[2 * i].wait()
            loads[2 * i + 1].wait()
            stores.append(copy(buf.at[i], pieces.at[i]))
        for one in stores:
            one.wait()

    shape = (8, rows, 2 * own)
    return pl.pallas_call(
        move,
        in_specs=[SCALARS, ANYWHERE],
        out_specs=ANYWHERE,
        out_shape=jax.ShapeDtypeStruct(shape, window_rows.dtype),
        scratch_shapes=[pltpu.VMEM(shape, window_rows.dtype), pltpu.SemaphoreType.DMA((24,))],
    )(where, window_rows)


def arrange(where, upsilon_rows, omega_cols, phi_cols):
    deep, width = upsilon_rows.shape
    wide = width // 8
    split, thin = omega_cols.shape
    tall = phi_cols.shape[0] // 8

    def move(where, upsilon, omega, phi, first, second, third, fourth, small, u_buf, s_buf, sems):
        z = where[1]
        picks = (first, second, third, fourth)
        copy = launcher(sems)
        loads = []
        for at in (2, 1, 3, 0):
            for half in range(2):
                start = pl.multiple_of((z + at) % 4 * wide + half * 4 * wide, wide)
                loads.append(copy(upsilon.at[:, pl.ds(start, wide)], u_buf.at[at, :, pl.ds(half * wide, wide)]))
        turned = omega[...].T
        stores = []
        for i in range(8):
            s_buf[i, :, :split] = turned
            s_buf[i, :, split:] = phi[i * tall : (i + 1) * tall, :].T
            stores.append(copy(s_buf.at[i], small.at[i]))
        for place, at in enumerate((2, 1, 3, 0)):
            loads[2 * place].wait()
            loads[2 * place + 1].wait()
            stores.append(copy(u_buf.at[at], picks[at]))
        for one in stores:
            one.wait()

    kind = upsilon_rows.dtype
    return pl.pallas_call(
        move,
        in_specs=[SCALARS, ANYWHERE, NEARBY, NEARBY],
        out_specs=[ANYWHERE] * 5,
        out_shape=[
            *[jax.ShapeDtypeStruct((deep, 2 * wide), kind)] * 4,
            jax.ShapeDtypeStruct((8, thin, split + tall), kind),
        ],
        scratch_shapes=[
            pltpu.VMEM((4, deep, 2 * wide), kind),
            pltpu.VMEM((8, thin, split + tall), kind),
            pltpu.SemaphoreType.DMA((20,)),
        ],
    )(where, upsilon_rows, omega_cols, phi_cols)


def dot_down(a, b):
    return lax.dot_general(a, b, (((0,), (0,)), ((), ())), preferred_element_type=jnp.float32)


def exchange(value, axes):
    return lax.all_to_all(value, axes, 0, 0, tiled=True)


def body(window_rows, omega_cols, psi_rows, upsilon_rows, phi_cols, range_old, core_old):
    k = lax.axis_index("k")
    z = lax.axis_index("z")
    yl = lax.axis_index("yl")
    rows, cols = window_rows.shape
    own = cols // 16
    wide = upsilon_rows.shape[1] // 8
    split = omega_cols.shape[0]

    where = jnp.stack([k, z]).astype(jnp.int32)
    pieces = cut_window(where, window_rows)
    relaid = exchange(pieces, PLANE).reshape(8 * rows, 2 * own)
    *picks, small = arrange(where, upsilon_rows, omega_cols, phi_cols)
    psi_other = swap(psi_rows)
    picks_other = [None] * 4
    for at in (2, 1, 3, 0):
        picks_other[at] = swap(picks[at])
    relaid, psi_other, *picks_other = tied(relaid, psi_other, *picks_other)

    def share(at):
        return dot(relaid, jnp.concatenate([picks[at], picks_other[at]], axis=0))

    co = (NEAR * dot(relaid, jnp.concatenate([psi_rows, psi_other], axis=0))).astype(WIRE)
    co = exchange(co.reshape(8, rows, -1), PLANE)

    sent = []
    for at in (2, 1, 3):
        part = (NEAR * share(at)).astype(WIRE)
        sent.append(shift(part, "z", at))
    mine = share(0)

    co, small = tied(co, small)
    small = exchange(small, PLANE)
    co = jnp.sum(co.astype(jnp.float32), axis=0) * (1.0 / NEAR)

    def pick(value, at, wide):
        start = (z + at) % 4 * wide
        return jnp.concatenate(
            [lax.dynamic_slice_in_dim(value, start + half * 4 * wide, wide, 1) for half in range(2)], axis=1
        )

    narrow = co.shape[1] // 8
    others = [shift(pick(co, at, narrow), "z", at) for at in (2, 1, 3)]

    mine, small, *sent = tied(mine, small, *sent)
    total = mine + (1.0 / NEAR) * sum(s.astype(jnp.float32) for s in sent)
    sk = (FAR * total).astype(WIRE).reshape(16, rows // 2, 2 * wide)
    sk = exchange(sk, TILE)

    small = small.reshape(8 * rows, -1)
    omega, phi = small[:, :split], small[:, split:]
    range_given = dot_down(omega, relaid[:, own:])
    range_kept = dot_down(omega, relaid[:, :own])
    range_sketch = range_old + range_kept + swap(range_given)

    co = pick(co, 0, narrow) + others[0] + others[1] + others[2]
    co_kept = lax.dynamic_slice_in_dim(co, yl * narrow, narrow, 1)
    corange_sketch = co_kept + swap(lax.dynamic_slice_in_dim(co, (1 - yl) * narrow, narrow, 1), "yl")

    sk = (jnp.sum(sk.astype(jnp.float32), axis=0) * (1.0 / FAR)).astype(jnp.bfloat16)
    sk = jnp.stack([sk[:, :wide], sk[:, wide:]])
    sk = jnp.broadcast_to(sk[None], (8,) + sk.shape).reshape(16, rows // 2, wide)
    sk = exchange(sk, TILE)
    term = dot_down(phi, sk.reshape(8 * rows, wide))
    here = lax.dynamic_slice_in_dim(term, k * rows, rows, 0)
    there = lax.dynamic_slice_in_dim(term, (1 - k) * rows, rows, 0)
    core_sketch = core_old + here + swap(there)
    return (range_sketch, corange_sketch, core_sketch)


def solution(mesh):
    fine = Mesh(mesh.devices.reshape(2, 4, 2, 2, 4), ("yh", "x", "k", "yl", "z"))
    row = ("yh", "x", "k")
    col = ("yl", "z")
    placed = (
        P(row, col),
        P(None, row),
        P(col + row, None),
        P(col + row, None),
        P(None, row),
        P(None, col + row),
        P(row, col),
    )
    return jax.shard_map(
        body,
        mesh=fine,
        in_specs=placed,
        out_specs=(P(None, col + row), P(row, col), P(row, col)),
        check_vma=False,
    )
```

time: 182 us -> 167 us (0.918)
  waiting for transfers between devices: 88.1 us -> 65.5 us
  matrix products: 24.8 us -> 28.1 us
  starting transfers between devices: 48.5 us -> 50.8 us
    all_to_all x5, waiting for transfers between devices: 55.2 us -> 41.4 us  [exchange(): return lax.all_to_all(value, axes, 0, 0, tiled=True)]
    ppermute x6, waiting for transfers between devices: 26.4 us -> 17.4 us  [shift(): return lax.ppermute(value, axis, [(i, (i + by) % n) for i in range(n)])]
    dot_general x5, matrix products: 17.1 us -> 20.3 us  [dot(): return jnp.dot(a, b, preferred_element_type=jnp.float32)]
    ppermute x6, starting transfers between devices: 9.65 us -> 12.7 us  [shift(): return lax.ppermute(value, axis, [(i, (i + by) % n) for i in range(n)])]
    pallas_call x1 -> x2, Pallas kernels: 6.28 us -> 7.56 us  [the longest x1 4.29 us: arrange(): pl.pallas_call(move, in_specs=[SCALARS, ANYWHERE, NEARBY, NEARBY], out_sp...]
  transfers between devices with their start and end apart: 19 -> 19, of which waited for: 12 -> 10; matrix products, arithmetic and copies ran while one was open for 18% -> 18% of each run, Pallas kernels for 0% -> 3%
where the time goes in v4:
time: 167 us; the launch traced here: 166 us
  waiting for transfers between devices  65.5 us (39%)
  starting transfers between devices  50.8 us (30%)
  matrix products  28.1 us (17%)
  other arithmetic  11.3 us (7%)
  Pallas kernels  7.56 us (5%)
  local copies, waits for them, and re-layouts  1.87 us (1%)
    all_to_all x5, waiting for transfers between devices, exchange(): return lax.all_to_all(value, axes, 0, 0, tiled=True)  41.4 us
    all_to_all x5, starting transfers between devices, exchange(): return lax.all_to_all(value, axes, 0, 0, tiled=True)  28.9 us
    dot_general x5, matrix products, dot(): return jnp.dot(a, b, preferred_element_type=jnp.float32)  20.3 us
    ppermute x6, waiting for transfers between devices, shift(): return lax.ppermute(value, axis, [(i, (i + by) % n) for i in range(n)])  17.4 us
    ppermute x6, starting transfers between devices, shift(): return lax.ppermute(value, axis, [(i, (i + by) % n) for i in range(n)])  12.7 us
    ppermute x8, starting transfers between devices, swap(): return lax.ppermute(value, axis, [(0, 1), (1, 0)])  9.13 us
    dot_general x3, matrix products, dot_down(): lax.dot_general(a, b, (((0,), (0,)), ((), ())), preferred_element_type=jn...  7.72 us
    ppermute x8, waiting for transfers between devices, swap(): return lax.ppermute(value, axis, [(0, 1), (1, 0)])  6.67 us
  transfers between devices with their start and end apart: 19, of which 10 were waited for; matrix products, arithmetic and copies ran while one was open for 18% of the time, Pallas kernels for 3%

profile of v4, /device:TPU:1, one launch (start us, length us, event | category | flops | bytes accessed | tf_op | source)
XLA Modules:
  0.0 165.9 jit_solution(12622516400922787112)
XLA Ops:
  0.6 0.6 pad_add_fusion.where
  1.2 3.3 %shard_map.94 = bf16[8,128,1024]{2,1,0:T(8,128)(2,1)} custom-call(s32[2]{0:T(128)} %pad_add_fusion.where, bf16[128,8192]{1,0:T(8,128)(2,1)} %window.1), custom_call_target="tpu_custom_call" | custom-call | tf_op jit(solution)/shard_map/pallas_call | solution.py:71
  4.5 0.0 copy-start.5
  4.5 7.6 %all-to-all-start = ((bf16[8,128,1024]{2,1,0:T(8,128)(2,1)}), bf16[8,128,1024]{2,1,0:T(8,128)(2,1)S(1)}, u32[]{:S(2)}, u32[]{:S(2)}) async-start(bf16[8,128,1024]{2,1,0:T(8,128)(2,1)} %shard_map.94), calls=%async_computation | async-start | bytes 4194304 | tf_op jit(solution)/shard_map/all_to_all | solution.py:130
  12.1 1.0 collective-permute-start
  13.2 4.3 %shard_map.95 = (bf16[512,512]{1,0:T(8,128)(2,1)}, bf16[512,512]{1,0:T(8,128)(2,1)}, bf16[512,512]{1,0:T(8,128)(2,1)}, bf16[512,512]{1,0:T(8,128)(2,1)}, bf16[8,128,768]{2,1,0:T(8,128)(2,1)}) custom-call(s32[2]{0:T(128)} %pad_add_fusion.where, bf16[512,2048]{1,0:T(8,128)(2,1)} %upsilon.1, bf16[512,128]{1,0:T(8,128)(2,1)} %omega.1, bf16[2048,128]{1,0:T(8,128)(2,1)} %phi.1), custom_call_target="tpu_custom_call" | custom-call | tf_op jit(solution)/shard_map/pallas_call | solution.py:109
  17.5 0.1 collective-permute-start.1
  17.6 0.5 collective-permute-start.2
  18.0 0.1 collective-permute-start.3
  18.1 0.4 collective-permute-start.4
  18.6 1.1 collective-permute-done.1
  19.7 0.7 collective-permute-done.2
  20.4 0.7 collective-permute-done.3
  21.2 0.7 collective-permute-done.4
  21.9 0.1 copy-done.7
  22.0 0.8 copy-done.12
  22.8 0.0 collective-permute-done
  22.8 18.0 %all-to-all-done = bf16[8,128,1024]{2,1,0:T(8,128)(2,1)S(1)} async-done(((bf16[8,128,1024]{2,1,0:T(8,128)(2,1)}), bf16[8,128,1024]{2,1,0:T(8,128)(2,1)S(1)}, u32[]{:S(2)}, u32[]{:S(2)}) %all-to-all-start) | async-done | bytes 2097184 | tf_op jit(solution)/shard_map/all_to_all | solution.py:130
  40.7 5.6 %multiply_convert_fusion = f16[1024,1024]{1,0:T(8,128)(2,1)} fusion(bf16[1024,1024]{1,0:T(8,128)(2,1)S(1)} %bitcast.18, bf16[512,1024]{1,0:T(8,128)(2,1)} %collective-permute-done, bf16[512,1024]{1,0:T(8,128)(2,1)S(1)} %copy-done.5), kind=kOutput, calls=%fused_computation.1 | convolution fusion | flops 2153775104 | bytes 6291456 | tf_op jit(solution)/shard_map/dot_general | solution.py:26
  46.4 4.8 %all-to-all-start.1 = ((f16[8,128,1024]{2,1,0:T(8,128)(2,1)}), f16[8,128,1024]{2,1,0:T(8,128)(2,1)S(1)}, u32[]{:S(2)}, u32[]{:S(2)}) async-start(f16[8,128,1024]{2,1,0:T(8,128)(2,1)} %bitcast.26), calls=%async_computation.1 | async-start | bytes 4194304 | tf_op jit(solution)/shard_map/all_to_all | solution.py:130
  51.3 4.0 %multiply_convert_fusion.2 = f16[1024,512]{1,0:T(8,128)(2,1)} fusion(bf16[1024,1024]{1,0:T(8,128)(2,1)} %bitcast.19, bf16[512,512]{1,0:T(8,128)(2,1)S(1)} %copy-done.13, bf16[512,512]{1,0:T(8,128)(2,1)S(1)} %copy-done.9), kind=kOutput, calls=%fused_computation.7 | convolution fusion | flops 1076887552 | bytes 4194304 | tf_op jit(solution)/shard_map/dot_general | solution.py:26
  55.2 3.8 %collective-permute-start.7 = (f16[1024,512]{1,0:T(8,128)(2,1)}, f16[1024,512]{1,0:T(8,128)(2,1)S(1)}, u32[]{:S(2)}, u32[]{:S(2)}) collective-permute-start(f16[1024,512]{1,0:T(8,128)(2,1)} %multiply_convert_fusion.2), channel_id=1, source_target_pairs={{0,3},{1,0},{2,1},{3,2},{4,7},{5,4},{6,5},{7,6},{8,11},{9,8},{10,9... | collective-permute-start | bytes 3145736 | tf_op jit(solution)/shard_map/ppermute | solution.py:18
  59.0 2.3 %multiply_convert_fusion.3 = f16[1024,512]{1,0:T(8,128)(2,1)} fusion(bf16[1024,1024]{1,0:T(8,128)(2,1)S(1)} %bitcast.22, bf16[512,512]{1,0:T(8,128)(2,1)S(1)} %copy-done.11, bf16[512,512]{1,0:T(8,128)(2,1)S(1)} %copy-done.8), kind=kOutput, calls=%fused_computation.8 | convolution fusion | flops 1076887552 | bytes 4194304 | tf_op jit(solution)/shard_map/dot_general | solution.py:26
  61.3 0.0 collective-permute-start.6
  61.3 18.6 %all-to-all-done.1 = f16[8,128,1024]{2,1,0:T(8,128)(2,1)S(1)} async-done(((f16[8,128,1024]{2,1,0:T(8,128)(2,1)}), f16[8,128,1024]{2,1,0:T(8,128)(2,1)S(1)}, u32[]{:S(2)}, u32[]{:S(2)}) %all-to-all-start.1) | async-done | bytes 2097184 | tf_op jit(solution)/shard_map/all_to_all | solution.py:130
  79.8 4.3 %all-to-all-start.2 = ((bf16[8,128,768]{2,1,0:T(8,128)(2,1)}), bf16[8,128,768]{2,1,0:T(8,128)(2,1)}, u32[]{:S(2)}, u32[]{:S(2)}) async-start(bf16[8,128,768]{2,1,0:T(8,128)(2,1)} %get-tuple-element.29), calls=%async_computation.2 | async-start | bytes 3145728 | tf_op jit(solution)/shard_map/all_to_all | solution.py:130
  84.1 4.0 %multiply_convert_fusion.4 = f16[1024,512]{1,0:T(8,128)(2,1)} fusion(bf16[1024,1024]{1,0:T(8,128)(2,1)} %bitcast.20, bf16[512,512]{1,0:T(8,128)(2,1)} %copy-done.7, bf16[512,512]{1,0:T(8,128)(2,1)} %get-tuple-element.23), kind=kOutput, calls=%fused_computation.9 | convolution fusion | flops 1076887552 | bytes 4194304 | tf_op jit(solution)/shard_map/dot_general | solution.py:26
  88.2 3.6 %collective-permute-start.5 = (f16[1024,512]{1,0:T(8,128)(2,1)}, f16[1024,512]{1,0:T(8,128)(2,1)}, u32[]{:S(2)}, u32[]{:S(2)}) collective-permute-start(f16[1024,512]{1,0:T(8,128)(2,1)} %multiply_convert_fusion.4), channel_id=1, source_target_pairs={{0,2},{1,3},{2,0},{3,1},{4,6},{5,7},{6,4},{7,5},{8,10},{9,11},{10,... | collective-permute-start | bytes 3145736 | tf_op jit(solution)/shard_map/ppermute | solution.py:18
  91.8 4.4 %fusion.4 = f32[1024,512]{1,0:T(8,128)} fusion(bf16[1024,1024]{1,0:T(8,128)(2,1)} %bitcast.21, bf16[512,512]{1,0:T(8,128)(2,1)} %copy-done.6, bf16[512,512]{1,0:T(8,128)(2,1)} %get-tuple-element.21), kind=kOutput, calls=%fused_computation.12 | convolution fusion | flops 1075838976 | bytes 5242880 | tf_op jit(solution)/shard_map/dot_general | solution.py:26
  96.2 1.3 convert_reduce_fusion
  97.5 0.0 collective-permute-done.7
  97.5 0.0 collective-permute-done.6
  97.5 17.4 %collective-permute-done.5 = f16[1024,512]{1,0:T(8,128)(2,1)} collective-permute-done((f16[1024,512]{1,0:T(8,128)(2,1)}, f16[1024,512]{1,0:T(8,128)(2,1)}, u32[]{:S(2)}, u32[]{:S(2)}) %collective-permute-start.5) | collective-permute-done | bytes 1048608 | tf_op jit(solution)/shard_map/ppermute | solution.py:18
  114.8 0.0 all-to-all-done.2
  114.8 3.9 %multiply_convert_fusion.1 = f16[1024,512]{1,0:T(8,128)(2,1)} fusion(f32[1024,512]{1,0:T(8,128)} %fusion.4, f16[1024,512]{1,0:T(8,128)(2,1)S(1)} %collective-permute-done.7, f16[1024,512]{1,0:T(8,128)(2,1)} %collective-permute-done.6, f16[1024,512]{1,0:T(8,128)(2,1)} %collective-permute-done.5), kind=kLoop, calls=%fused_computation.6 | loop fusion | flops 4718592 | bytes 6291456 | tf_op jit(solution)/shard_map/convert_element_type | solution.py:179
  118.7 6.5 %all-to-all-start.3 = ((f16[16,64,512]{2,1,0:T(8,128)(2,1)}), f16[16,64,512]{2,1,0:T(8,128)(2,1)S(1)}, u32[]{:S(2)}, u32[]{:S(2)}) async-start(f16[16,64,512]{2,1,0:T(8,128)(2,1)} %bitcast.25), calls=%async_computation.3 | async-start | bytes 2097152 | tf_op jit(solution)/shard_map/all_to_all | solution.py:130
  125.2 1.1 broadcast_multiply_fusion
  126.3 0.1 constant_dynamic-slice_fusion.9
  126.4 0.7 pad_maximum_fusion
  127.1 2.7 %collective-permute-start.9 = (f32[128,256]{1,0:T(8,128)}, f32[128,256]{1,0:T(8,128)S(1)}, u32[]{:S(2)}, u32[]{:S(2)}) collective-permute-start(f32[128,256]{1,0:T(8,128)} %pad_maximum_fusion), channel_id=1, source_target_pairs={{0,2},{1,3},{2,0},{3,1},{4,6},{5,7},{6,4},{7,5},{8,10},{9,11},{10,... | collective-permute-start | bytes 393224 | tf_op jit(solution)/shard_map/ppermute | solution.py:18
  129.7 0.7 pad_maximum_fusion.1
  130.4 0.7 collective-permute-start.10
  131.1 0.7 pad_maximum_fusion.2
  131.8 1.9 %collective-permute-start.11 = (f32[128,256]{1,0:T(8,128)}, f32[128,256]{1,0:T(8,128)}, u32[]{:S(2)}, u32[]{:S(2)}) collective-permute-start(f32[128,256]{1,0:T(8,128)} %pad_maximum_fusion.2), channel_id=1, source_target_pairs={{0,3},{1,0},{2,1},{3,2},{4,7},{5,4},{6,5},{7,6},{8,11},{9,8},{10,9... | collective-permute-start | bytes 393224 | tf_op jit(solution)/shard_map/ppermute | solution.py:18
  133.8 2.9 %fusion.17 = f32[512,512]{1,0:T(8,128)} fusion(bf16[1024,1024]{1,0:T(8,128)(2,1)S(1)} %bitcast.23, bf16[1024,768]{1,0:T(8,128)(2,1)} %bitcast.4), kind=kOutput, calls=%fused_computation.25 | convolution fusion | flops 536870912 | bytes 3145728 | tf_op jit(solution)/shard_map/dot_general | solution.py:126
  136.7 3.0 %collective-permute-start.8 = (f32[512,512]{1,0:T(8,128)}, f32[512,512]{1,0:T(8,128)}, u32[]{:S(2)}, u32[]{:S(2)}) collective-permute-start(f32[512,512]{1,0:T(8,128)} %fusion.17), channel_id=1, source_target_pairs={{0,8},{8,0},{1,9},{9,1},{2,10},{10,2},{3,11},{11,3},{4,12},{12,4},... | collective-permute-start | bytes 3145736 | tf_op jit(solution)/shard_map/ppermute | solution.py:22
  139.7 1.3 all-to-all-done.3
  141.0 0.1 convert_reduce_fusion.1
  141.2 0.0 copy-start.3
  141.3 0.8 broadcast_in_dim.2
  142.1 5.7 %all-to-all-start.4 = ((bf16[16,64,256]{2,1,0:T(8,128)(2,1)}), bf16[16,64,256]{2,1,0:T(8,128)(2,1)}, u32[]{:S(2)}, u32[]{:S(2)}) async-start(bf16[16,64,256]{2,1,0:T(8,128)(2,1)} %bitcast.8), calls=%async_computation.4 | async-start | bytes 1048576 | tf_op jit(solution)/shard_map/all_to_all | solution.py:130
  147.8 0.0 collective-permute-done.9
  147.8 0.0 collective-permute-done.10
  147.8 1.0 fusion.25
  148.8 1.4 collective-permute-start.12
  150.2 3.3 %collective-permute-done.12 = f32[128,128]{1,0:T(8,128)S(1)} collective-permute-done((f32[128,128]{1,0:T(8,128)S(1)}, f32[128,128]{1,0:T(8,128)S(1)}, u32[]{:S(2)}, u32[]{:S(2)}) %collective-permute-start.12) | collective-permute-done | bytes 65568 | tf_op jit(solution)/shard_map/ppermute | solution.py:22
  153.6 0.6 dynamic-slice_add_fusion
  154.2 3.6 %all-to-all-done.4 = bf16[16,64,256]{2,1,0:T(8,128)(2,1)} async-done(((bf16[16,64,256]{2,1,0:T(8,128)(2,1)}), bf16[16,64,256]{2,1,0:T(8,128)(2,1)}, u32[]{:S(2)}, u32[]{:S(2)}) %all-to-all-start.4) | async-done | bytes 524320 | tf_op jit(solution)/shard_map/all_to_all | solution.py:130
  157.8 1.5 fusion.22
  159.4 0.0 copy-start.4
  159.4 2.6 %collective-permute-start.13 = (f32[128,256]{1,0:T(8,128)S(1)}, f32[128,256]{1,0:T(8,128)S(1)}, u32[]{:S(2)}, u32[]{:S(2)}) collective-permute-start(f32[128,256]{1,0:T(8,128)S(1)} %constant_dynamic-slice_fusion), channel_id=1, source_target_pairs={{0,8},{8,0},{1,9},{9,1},{2,10},{10,2},{3,11},{11,3},{4,12},{12,4},... | collective-permute-start | bytes 393224 | tf_op jit(solution)/shard_map/ppermute | solution.py:22
  162.0 3.2 %fusion.3 = f32[512,512]{1,0:T(8,128)} fusion(f32[512,512]{1,0:T(8,128)} %collective-permute-done.8, f32[512,512]{1,0:T(8,128)S(1)} %copy-done.3, bf16[1024,1024]{1,0:T(8,128)(2,1)S(1)} %bitcast.24, bf16[1024,768]{1,0:T(8,128)(2,1)} %bitcast.4), kind=kOutput, calls=%fused_computation.11 | convolution fusion | flops 537395200 | bytes 5242880 | tf_op jit(solution)/shard_map/dot_general | solution.py:126
  165.2 0.0 collective-permute-done.13
  165.2 0.7 add_add_fusion
  (30 shorter events, 0.1 us)
Async XLA Ops:
  4.5 7.6 %copy-start.5 = (bf16[512,1024]{1,0:T(8,128)(2,1)S(1)}, bf16[512,1024]{1,0:T(8,128)(2,1)}, u32[]{:S(2)}) copy-start(bf16[512,1024]{1,0:T(8,128)(2,1)} %param.9) | copy-start | bytes 3145732
  4.5 36.2 %all-to-all-start = ((bf16[8,128,1024]{2,1,0:T(8,128)(2,1)}), bf16[8,128,1024]{2,1,0:T(8,128)(2,1)S(1)}, u32[]{:S(2)}, u32[]{:S(2)}) async-start(bf16[8,128,1024]{2,1,0:T(8,128)(2,1)} %shard_map.94), calls=%async_computation | async-start | bytes 4194304 | tf_op jit(solution)/shard_map/all_to_all | solution.py:130
  12.1 10.6 %collective-permute-start = (bf16[512,1024]{1,0:T(8,128)(2,1)S(1)}, bf16[512,1024]{1,0:T(8,128)(2,1)}, u32[]{:S(2)}, u32[]{:S(2)}) collective-permute-start(bf16[512,1024]{1,0:T(8,128)(2,1)S(1)} %copy-done.5), channel_id=1, source_target_pairs={{0,8},{8,0},{1,9},{9,1},{2,10},{10,2},{3,11},{11,3},{4,12},{12,4},... | collective-permute-start | bytes 3145736 | tf_op jit(solution)/shard_map/ppermute | solution.py:22
  17.5 2.2 %collective-permute-start.1 = (bf16[512,512]{1,0:T(8,128)(2,1)}, bf16[512,512]{1,0:T(8,128)(2,1)S(1)}, u32[]{:S(2)}, u32[]{:S(2)}) collective-permute-start(bf16[512,512]{1,0:T(8,128)(2,1)} %get-tuple-element.21), channel_id=1, source_target_pairs={{0,8},{8,0},{1,9},{9,1},{2,10},{10,2},{3,11},{11,3},{4,12},{12,4},... | collective-permute-start | bytes 1572872 | tf_op jit(solution)/shard_map/ppermute | solution.py:22
  17.6 2.9 %collective-permute-start.2 = (bf16[512,512]{1,0:T(8,128)(2,1)}, bf16[512,512]{1,0:T(8,128)(2,1)S(1)}, u32[]{:S(2)}, u32[]{:S(2)}) collective-permute-start(bf16[512,512]{1,0:T(8,128)(2,1)} %get-tuple-element.22), channel_id=1, source_target_pairs={{0,8},{8,0},{1,9},{9,1},{2,10},{10,2},{3,11},{11,3},{4,12},{12,4},... | collective-permute-start | bytes 1572872 | tf_op jit(solution)/shard_map/ppermute | solution.py:22
  18.0 3.1 %collective-permute-start.3 = (bf16[512,512]{1,0:T(8,128)(2,1)}, bf16[512,512]{1,0:T(8,128)(2,1)S(1)}, u32[]{:S(2)}, u32[]{:S(2)}) collective-permute-start(bf16[512,512]{1,0:T(8,128)(2,1)} %get-tuple-element.23), channel_id=1, source_target_pairs={{0,8},{8,0},{1,9},{9,1},{2,10},{10,2},{3,11},{11,3},{4,12},{12,4},... | collective-permute-start | bytes 1572872 | tf_op jit(solution)/shard_map/ppermute | solution.py:22
  18.1 3.8 %collective-permute-start.4 = (bf16[512,512]{1,0:T(8,128)(2,1)}, bf16[512,512]{1,0:T(8,128)(2,1)S(1)}, u32[]{:S(2)}, u32[]{:S(2)}) collective-permute-start(bf16[512,512]{1,0:T(8,128)(2,1)} %get-tuple-element.24), channel_id=1, source_target_pairs={{0,8},{8,0},{1,9},{9,1},{2,10},{10,2},{3,11},{11,3},{4,12},{12,4},... | collective-permute-start | bytes 1572872 | tf_op jit(solution)/shard_map/ppermute | solution.py:22
  19.7 2.3 %copy-start.6 = (bf16[512,512]{1,0:T(8,128)(2,1)}, bf16[512,512]{1,0:T(8,128)(2,1)S(1)}, u32[]{:S(2)}) copy-start(bf16[512,512]{1,0:T(8,128)(2,1)S(1)} %collective-permute-done.1) | copy-start | bytes 1572868
  20.4 1.5 copy-start.10
  21.2 0.8 copy-start.7
  22.0 0.8 copy-start.12
  40.7 5.6 %copy-start = (bf16[8,128,1024]{2,1,0:T(8,128)(2,1)}, bf16[8,128,1024]{2,1,0:T(8,128)(2,1)S(1)}, u32[]{:S(2)}) copy-start(bf16[8,128,1024]{2,1,0:T(8,128)(2,1)S(1)} %all-to-all-done) | copy-start | bytes 6291460
  46.4 4.8 %copy-start.9 = (bf16[512,512]{1,0:T(8,128)(2,1)S(1)}, bf16[512,512]{1,0:T(8,128)(2,1)}, u32[]{:S(2)}) copy-start(bf16[512,512]{1,0:T(8,128)(2,1)} %get-tuple-element.24) | copy-start | bytes 1572868
  46.4 4.8 %copy-start.13 = (bf16[512,512]{1,0:T(8,128)(2,1)S(1)}, bf16[512,512]{1,0:T(8,128)(2,1)}, u32[]{:S(2)}) copy-start(bf16[512,512]{1,0:T(8,128)(2,1)} %copy-done.12) | copy-start | bytes 1572868
  46.4 33.4 %all-to-all-start.1 = ((f16[8,128,1024]{2,1,0:T(8,128)(2,1)}), f16[8,128,1024]{2,1,0:T(8,128)(2,1)S(1)}, u32[]{:S(2)}, u32[]{:S(2)}) async-start(f16[8,128,1024]{2,1,0:T(8,128)(2,1)} %bitcast.26), calls=%async_computation.1 | async-start | bytes 4194304 | tf_op jit(solution)/shard_map/all_to_all | solution.py:130
  51.2 7.7 %copy-start.1 = (bf16[8,128,1024]{2,1,0:T(8,128)(2,1)S(1)}, bf16[8,128,1024]{2,1,0:T(8,128)(2,1)}, u32[]{:S(2)}) copy-start(bf16[8,128,1024]{2,1,0:T(8,128)(2,1)} %copy-done) | copy-start | bytes 6291460
  51.2 7.7 %copy-start.8 = (bf16[512,512]{1,0:T(8,128)(2,1)S(1)}, bf16[512,512]{1,0:T(8,128)(2,1)}, u32[]{:S(2)}) copy-start(bf16[512,512]{1,0:T(8,128)(2,1)} %get-tuple-element.22) | copy-start | bytes 1572868
  51.2 7.7 %copy-start.11 = (bf16[512,512]{1,0:T(8,128)(2,1)S(1)}, bf16[512,512]{1,0:T(8,128)(2,1)}, u32[]{:S(2)}) copy-start(bf16[512,512]{1,0:T(8,128)(2,1)} %copy-done.10) | copy-start | bytes 1572868
  55.2 42.2 %collective-permute-start.7 = (f16[1024,512]{1,0:T(8,128)(2,1)}, f16[1024,512]{1,0:T(8,128)(2,1)S(1)}, u32[]{:S(2)}, u32[]{:S(2)}) collective-permute-start(f16[1024,512]{1,0:T(8,128)(2,1)} %multiply_convert_fusion.2), channel_id=1, source_target_pairs={{0,3},{1,0},{2,1},{3,2},{4,7},{5,4},{6,5},{7,6},{8,11},{9,8},{10,9... | collective-permute-start | bytes 3145736 | tf_op jit(solution)/shard_map/ppermute | solution.py:18
  61.3 36.2 %collective-permute-start.6 = (f16[1024,512]{1,0:T(8,128)(2,1)}, f16[1024,512]{1,0:T(8,128)(2,1)}, u32[]{:S(2)}, u32[]{:S(2)}) collective-permute-start(f16[1024,512]{1,0:T(8,128)(2,1)} %multiply_convert_fusion.3), channel_id=1, source_target_pairs={{0,1},{1,2},{2,3},{3,0},{4,5},{5,6},{6,7},{7,4},{8,9},{9,10},{10,1... | collective-permute-start | bytes 3145736 | tf_op jit(solution)/shard_map/ppermute | solution.py:18
  79.8 35.0 %all-to-all-start.2 = ((bf16[8,128,768]{2,1,0:T(8,128)(2,1)}), bf16[8,128,768]{2,1,0:T(8,128)(2,1)}, u32[]{:S(2)}, u32[]{:S(2)}) async-start(bf16[8,128,768]{2,1,0:T(8,128)(2,1)} %get-tuple-element.29), calls=%async_computation.2 | async-start | bytes 3145728 | tf_op jit(solution)/shard_map/all_to_all | solution.py:130
  88.2 26.7 %collective-permute-start.5 = (f16[1024,512]{1,0:T(8,128)(2,1)}, f16[1024,512]{1,0:T(8,128)(2,1)}, u32[]{:S(2)}, u32[]{:S(2)}) collective-permute-start(f16[1024,512]{1,0:T(8,128)(2,1)} %multiply_convert_fusion.4), channel_id=1, source_target_pairs={{0,2},{1,3},{2,0},{3,1},{4,6},{5,7},{6,4},{7,5},{8,10},{9,11},{10,... | collective-permute-start | bytes 3145736 | tf_op jit(solution)/shard_map/ppermute | solution.py:18
  118.7 15.1 %copy-start.2 = (bf16[8,128,1024]{2,1,0:T(8,128)(2,1)S(1)}, bf16[8,128,1024]{2,1,0:T(8,128)(2,1)}, u32[]{:S(2)}) copy-start(bf16[8,128,1024]{2,1,0:T(8,128)(2,1)} %copy-done) | copy-start | bytes 6291460
  118.7 22.3 %all-to-all-start.3 = ((f16[16,64,512]{2,1,0:T(8,128)(2,1)}), f16[16,64,512]{2,1,0:T(8,128)(2,1)S(1)}, u32[]{:S(2)}, u32[]{:S(2)}) async-start(f16[16,64,512]{2,1,0:T(8,128)(2,1)} %bitcast.25), calls=%async_computation.3 | async-start | bytes 2097152 | tf_op jit(solution)/shard_map/all_to_all | solution.py:130
  127.1 20.7 %collective-permute-start.9 = (f32[128,256]{1,0:T(8,128)}, f32[128,256]{1,0:T(8,128)S(1)}, u32[]{:S(2)}, u32[]{:S(2)}) collective-permute-start(f32[128,256]{1,0:T(8,128)} %pad_maximum_fusion), channel_id=1, source_target_pairs={{0,2},{1,3},{2,0},{3,1},{4,6},{5,7},{6,4},{7,5},{8,10},{9,11},{10,... | collective-permute-start | bytes 393224 | tf_op jit(solution)/shard_map/ppermute | solution.py:18
  130.4 17.4 %collective-permute-start.10 = (f32[128,256]{1,0:T(8,128)}, f32[128,256]{1,0:T(8,128)}, u32[]{:S(2)}, u32[]{:S(2)}) collective-permute-start(f32[128,256]{1,0:T(8,128)} %pad_maximum_fusion.1), channel_id=1, source_target_pairs={{0,1},{1,2},{2,3},{3,0},{4,5},{5,6},{6,7},{7,4},{8,9},{9,10},{10,1... | collective-permute-start | bytes 393224 | tf_op jit(solution)/shard_map/ppermute | solution.py:18
  131.8 16.0 %collective-permute-start.11 = (f32[128,256]{1,0:T(8,128)}, f32[128,256]{1,0:T(8,128)}, u32[]{:S(2)}, u32[]{:S(2)}) collective-permute-start(f32[128,256]{1,0:T(8,128)} %pad_maximum_fusion.2), channel_id=1, source_target_pairs={{0,3},{1,0},{2,1},{3,2},{4,7},{5,4},{6,5},{7,6},{8,11},{9,8},{10,9... | collective-permute-start | bytes 393224 | tf_op jit(solution)/shard_map/ppermute | solution.py:18
  136.7 25.3 %collective-permute-start.8 = (f32[512,512]{1,0:T(8,128)}, f32[512,512]{1,0:T(8,128)}, u32[]{:S(2)}, u32[]{:S(2)}) collective-permute-start(f32[512,512]{1,0:T(8,128)} %fusion.17), channel_id=1, source_target_pairs={{0,8},{8,0},{1,9},{9,1},{2,10},{10,2},{3,11},{11,3},{4,12},{12,4},... | collective-permute-start | bytes 3145736 | tf_op jit(solution)/shard_map/ppermute | solution.py:22
  141.2 20.7 %copy-start.3 = (f32[512,512]{1,0:T(8,128)S(1)}, f32[512,512]{1,0:T(8,128)}, u32[]{:S(2)}) copy-start(f32[512,512]{1,0:T(8,128)} %param.12) | copy-start | bytes 3145732
  142.1 15.7 %all-to-all-start.4 = ((bf16[16,64,256]{2,1,0:T(8,128)(2,1)}), bf16[16,64,256]{2,1,0:T(8,128)(2,1)}, u32[]{:S(2)}, u32[]{:S(2)}) async-start(bf16[16,64,256]{2,1,0:T(8,128)(2,1)} %bitcast.8), calls=%async_computation.4 | async-start | bytes 1048576 | tf_op jit(solution)/shard_map/all_to_all | solution.py:130
  148.8 4.7 %collective-permute-start.12 = (f32[128,128]{1,0:T(8,128)S(1)}, f32[128,128]{1,0:T(8,128)S(1)}, u32[]{:S(2)}, u32[]{:S(2)}) collective-permute-start(f32[128,128]{1,0:T(8,128)S(1)} %constant_dynamic-slice_fusion.1), channel_id=1, source_target_pairs={{0,4},{4,0},{1,5},{5,1},{2,6},{6,2},{3,7},{7,3},{8,12},{12,8},{9,1... | collective-permute-start | bytes 196616 | tf_op jit(solution)/shard_map/ppermute | solution.py:22
  159.4 5.8 %copy-start.4 = (f32[128,256]{1,0:T(8,128)S(1)}, f32[128,256]{1,0:T(8,128)}, u32[]{:S(2)}) copy-start(f32[128,256]{1,0:T(8,128)} %param.13) | copy-start | bytes 393220
  159.4 5.8 %collective-permute-start.13 = (f32[128,256]{1,0:T(8,128)S(1)}, f32[128,256]{1,0:T(8,128)S(1)}, u32[]{:S(2)}, u32[]{:S(2)}) collective-permute-start(f32[128,256]{1,0:T(8,128)S(1)} %constant_dynamic-slice_fusion), channel_id=1, source_target_pairs={{0,8},{8,0},{1,9},{9,1},{2,10},{10,2},{3,11},{11,3},{4,12},{12,4},... | collective-permute-start | bytes 393224 | tf_op jit(solution)/shard_map/ppermute | solution.py:22

commit v5 on v4

--- a/solution.py
+++ b/solution.py
@@ -14,7 +14,7 @@
 
 
 def shift(value, axis, by):
-    n = lax.axis_size(axis)
+    n = lax.psum(1, axis)
     return lax.ppermute(value, axis, [(i, (i + by) % n) for i in range(n)])
 
 
@@ -83,8 +83,9 @@
     split, thin = omega_cols.shape
     tall = phi_cols.shape[0] // 8
 
-    def move(where, upsilon, omega, phi, first, second, third, fourth, small, u_buf, s_buf, sems):
-        z = where[1]
+    def move(where, upsilon, omega, phi, first, second, third, fourth, *rest):
+        *small, u_buf, s_buf, sems = rest
+        z, place_here = where[1], where[2]
         picks = (first, second, third, fourth)
         copy = launcher(sems)
         loads = []
@@ -95,9 +96,10 @@
         turned = omega[...].T
         stores = []
         for i in range(8):
+            start = pl.multiple_of((place_here + i) % 8 * tall, tall)
             s_buf[i, :, :split] = turned
-            s_buf[i, :, split:] = phi[i * tall : (i + 1) * tall, :].T
-            stores.append(copy(s_buf.at[i], small.at[i]))
+            s_buf[i, :, split:] = phi[pl.ds(start, tall), :].T
+            stores.append(copy(s_buf.at[i], small[i]))
         for place, at in enumerate((2, 1, 3, 0)):
             loads[2 * place].wait()
             loads[2 * place + 1].wait()
@@ -109,10 +111,10 @@
     return pl.pallas_call(
         move,
         in_specs=[SCALARS, ANYWHERE, NEARBY, NEARBY],
-        out_specs=[ANYWHERE] * 5,
+        out_specs=[ANYWHERE] * 12,
         out_shape=[
             *[jax.ShapeDtypeStruct((deep, 2 * wide), kind)] * 4,
-            jax.ShapeDtypeStruct((8, thin, split + tall), kind),
+            *[jax.ShapeDtypeStruct((thin, split + tall), kind)] * 8,
         ],
         scratch_shapes=[
             pltpu.VMEM((4, deep, 2 * wide), kind),
@@ -120,6 +122,26 @@
             pltpu.SemaphoreType.DMA((20,)),
         ],
     )(where, upsilon_rows, omega_cols, phi_cols)
+
+
+def assemble(where, blocks):
+    shape = (8,) + blocks[0].shape
+
+    def move(where, *refs):
+        *parts, whole, buf, sems = refs
+        copy = launcher(sems)
+        loads = [copy(parts[i], buf.at[(where[2] + 8 - i) % 8]) for i in range(8)]
+        for one in loads:
+            one.wait()
+        copy(buf, whole).wait()
+
+    return pl.pallas_call(
+        move,
+        in_specs=[SCALARS] + [ANYWHERE] * 8,
+        out_specs=ANYWHERE,
+        out_shape=jax.ShapeDtypeStruct(shape, blocks[0].dtype),
+        scratch_shapes=[pltpu.VMEM(shape, blocks[0].dtype), pltpu.SemaphoreType.DMA((9,))],
+    )(where, *blocks)
 
 
 def dot_down(a, b):
@@ -139,10 +161,11 @@
     wide = upsilon_rows.shape[1] // 8
     split = omega_cols.shape[0]
 
-    where = jnp.stack([k, z]).astype(jnp.int32)
+    where = jnp.stack([k, z, lax.axis_index(PLANE)]).astype(jnp.int32)
     pieces = cut_window(where, window_rows)
     relaid = exchange(pieces, PLANE).reshape(8 * rows, 2 * own)
-    *picks, small = arrange(where, upsilon_rows, omega_cols, phi_cols)
+    arranged = arrange(where, upsilon_rows, omega_cols, phi_cols)
+    picks, small = arranged[:4], arranged[4:]
     psi_other = swap(psi_rows)
     picks_other = [None] * 4
     for at in (2, 1, 3, 0):
@@ -152,17 +175,14 @@
     def share(at):
         return dot(relaid, jnp.concatenate([picks[at], picks_other[at]], axis=0))
 
-    co = (NEAR * dot(relaid, jnp.concatenate([psi_rows, psi_other], axis=0))).astype(WIRE)
-    co = exchange(co.reshape(8, rows, -1), PLANE)
-
     sent = []
     for at in (2, 1, 3):
         part = (NEAR * share(at)).astype(WIRE)
         sent.append(shift(part, "z", at))
+    co = (NEAR * dot(relaid, jnp.concatenate([psi_rows, psi_other], axis=0))).astype(WIRE)
+    co = exchange(co.reshape(8, rows, -1), PLANE)
     mine = share(0)
-
-    co, small = tied(co, small)
-    small = exchange(small, PLANE)
+    small = [small[0]] + [shift(small[by], PLANE, by) for by in range(1, 8)]
     co = jnp.sum(co.astype(jnp.float32), axis=0) * (1.0 / NEAR)
 
     def pick(value, at, wide):
@@ -174,12 +194,12 @@
     narrow = co.shape[1] // 8
     others = [shift(pick(co, at, narrow), "z", at) for at in (2, 1, 3)]
 
-    mine, small, *sent = tied(mine, small, *sent)
+    mine, co, *sent = tied(mine, co, *sent)
     total = mine + (1.0 / NEAR) * sum(s.astype(jnp.float32) for s in sent)
     sk = (FAR * total).astype(WIRE).reshape(16, rows // 2, 2 * wide)
     sk = exchange(sk, TILE)
 
-    small = small.reshape(8 * rows, -1)
+    small = assemble(where, small).reshape(8 * rows, -1)
     omega, phi = small[:, :split], small[:, split:]
     range_given = dot_down(omega, relaid[:, own:])
     range_kept = dot_down(omega, relaid[:, :own])

time: 167 us -> 186 us (1.11)
  starting transfers between devices: 50.8 us -> 62.5 us
  waiting for transfers between devices: 65.5 us -> 74.6 us
  matrix products: 28.1 us -> 24.6 us
  Pallas kernels: 7.56 us -> 10.9 us
  other arithmetic: 11.3 us -> 9.18 us
    ppermute x6 -> x13, waiting for transfers between devices: 17.4 us -> 39.9 us  [shift(): return lax.ppermute(value, axis, [(i, (i + by) % n) for i in range(n)])]
    all_to_all x5 -> x4, waiting for transfers between devices: 41.4 us -> 31 us  [exchange(): return lax.all_to_all(value, axes, 0, 0, tiled=True)]
    ppermute x6 -> x13, starting transfers between devices: 12.7 us -> 22 us  [shift(): return lax.ppermute(value, axis, [(i, (i + by) % n) for i in range(n)])]
    dot_general x5, matrix products: 20.3 us -> 16.8 us  [dot(): return jnp.dot(a, b, preferred_element_type=jnp.float32)]
    pallas_call x0 -> x1, Pallas kernels: none -> 3.38 us  [assemble(): pl.pallas_call(move, in_specs=[SCALARS] + [ANYWHERE] * 8, out_specs=ANYWH...]
    ppermute x8, starting transfers between devices: 9.13 us -> 12.2 us  [swap(): return lax.ppermute(value, axis, [(0, 1), (1, 0)])]
    ppermute x8, waiting for transfers between devices: 6.67 us -> 3.69 us  [swap(): return lax.ppermute(value, axis, [(0, 1), (1, 0)])]
    all_to_all x5 -> x4, starting transfers between devices: 28.9 us -> 28.2 us  [exchange(): return lax.all_to_all(value, axes, 0, 0, tiled=True)]
  transfers between devices with their start and end apart: 19 -> 25, of which waited for: 10 -> 15; matrix products, arithmetic and copies ran while one was open for 18% -> 15% of each run, Pallas kernels for 3% -> 4%
where the time goes in v5:
time: 186 us; the launch traced here: 185 us
  waiting for transfers between devices  74.6 us (40%)
  starting transfers between devices  62.5 us (34%)
  matrix products  24.6 us (13%)
  Pallas kernels  10.9 us (6%)
  other arithmetic  9.18 us (5%)
  local copies, waits for them, and re-layouts  2.88 us (2%)
    ppermute x13, waiting for transfers between devices, shift(): return lax.ppermute(value, axis, [(i, (i + by) % n) for i in range(n)])  39.9 us
    all_to_all x4, waiting for transfers between devices, exchange(): return lax.all_to_all(value, axes, 0, 0, tiled=True)  31 us
    all_to_all x4, starting transfers between devices, exchange(): return lax.all_to_all(value, axes, 0, 0, tiled=True)  28.2 us
    ppermute x13, starting transfers between devices, shift(): return lax.ppermute(value, axis, [(i, (i + by) % n) for i in range(n)])  22 us
    dot_general x5, matrix products, dot(): return jnp.dot(a, b, preferred_element_type=jnp.float32)  16.8 us
    ppermute x8, starting transfers between devices, swap(): return lax.ppermute(value, axis, [(0, 1), (1, 0)])  12.2 us
    dot_general x3, matrix products, dot_down(): lax.dot_general(a, b, (((0,), (0,)), ((), ())), preferred_element_type=jn...  7.77 us
    pallas_call x1, Pallas kernels, arrange(): pl.pallas_call(move, in_specs=[SCALARS, ANYWHERE, NEARBY, NEARBY], out_sp...  4.26 us
  transfers between devices with their start and end apart: 25, of which 15 were waited for; matrix products, arithmetic and copies ran while one was open for 15% of the time, Pallas kernels for 4%

profile of v5, /device:TPU:1, one launch (start us, length us, event | category | flops | bytes accessed | tf_op | source)
XLA Modules:
  0.0 185.5 jit_solution(13174511665006067074)
XLA Ops:
  0.6 0.7 pad_add_fusion.where
  1.3 3.3 %shard_map.96 = bf16[8,128,1024]{2,1,0:T(8,128)(2,1)} custom-call(s32[3]{0:T(128)} %pad_add_fusion.where, bf16[128,8192]{1,0:T(8,128)(2,1)} %window.1), custom_call_target="tpu_custom_call" | custom-call | tf_op jit(solution)/shard_map/pallas_call | solution.py:71
  4.6 7.6 %all-to-all-start = ((bf16[8,128,1024]{2,1,0:T(8,128)(2,1)}), bf16[8,128,1024]{2,1,0:T(8,128)(2,1)S(1)}, u32[]{:S(2)}, u32[]{:S(2)}) async-start(bf16[8,128,1024]{2,1,0:T(8,128)(2,1)} %shard_map.96), calls=%async_computation | async-start | bytes 4194304 | tf_op jit(solution)/shard_map/all_to_all | solution.py:152
  12.2 1.0 collective-permute-start.7
  13.2 4.3 %shard_map.94 = (bf16[512,512]{1,0:T(8,128)(2,1)}, bf16[512,512]{1,0:T(8,128)(2,1)}, bf16[512,512]{1,0:T(8,128)(2,1)}, bf16[512,512]{1,0:T(8,128)(2,1)}, bf16[12...) custom-call(s32[3]{0:T(128)} %pad_add_fusion.where, ...), custom_call_target="tpu_custom_call" | custom-call | tf_op jit(solution)/shard_map/pallas_call | solution.py:111
  17.5 0.1 collective-permute-start.8
  17.6 0.5 collective-permute-start.9
  18.1 0.1 collective-permute-start.10
  18.2 0.4 collective-permute-start.11
  18.6 1.1 collective-permute-done.8
  19.7 0.7 collective-permute-done.9
  20.5 0.7 collective-permute-done.10
  21.2 0.7 collective-permute-done.11
  22.0 0.1 copy-done.20
  22.0 0.8 copy-done.18
  22.9 17.9 %all-to-all-done = bf16[8,128,1024]{2,1,0:T(8,128)(2,1)S(1)} async-done(((bf16[8,128,1024]{2,1,0:T(8,128)(2,1)}), bf16[8,128,1024]{2,1,0:T(8,128)(2,1)S(1)}, u32[]{:S(2)}, u32[]{:S(2)}) %all-to-all-start) | async-done | bytes 2097184 | tf_op jit(solution)/shard_map/all_to_all | solution.py:152
  40.8 5.7 %multiply_convert_fusion = f16[1024,1024]{1,0:T(8,128)(2,1)} fusion(bf16[1024,1024]{1,0:T(8,128)(2,1)S(1)} %bitcast.19, bf16[512,1024]{1,0:T(8,128)(2,1)} %collective-permute-done.7, bf16[512,1024]{1,0:T(8,128)(2,1)S(1)} %copy-done.9), kind=kOutput, calls=%fused_computation.1 | convolution fusion | flops 2153775104 | bytes 6291456 | tf_op jit(solution)/shard_map/dot_general | solution.py:26
  46.5 4.8 %all-to-all-start.1 = ((f16[8,128,1024]{2,1,0:T(8,128)(2,1)}), f16[8,128,1024]{2,1,0:T(8,128)(2,1)S(1)}, u32[]{:S(2)}, u32[]{:S(2)}) async-start(f16[8,128,1024]{2,1,0:T(8,128)(2,1)} %bitcast.29), calls=%async_computation.1 | async-start | bytes 4194304 | tf_op jit(solution)/shard_map/all_to_all | solution.py:152
  51.3 4.1 %multiply_convert_fusion.4 = f16[1024,512]{1,0:T(8,128)(2,1)} fusion(bf16[1024,1024]{1,0:T(8,128)(2,1)} %bitcast.20, bf16[512,512]{1,0:T(8,128)(2,1)} %copy-done.20, bf16[512,512]{1,0:T(8,128)(2,1)S(1)} %copy-done.15), kind=kOutput, calls=%fused_computation.9 | convolution fusion | flops 1076887552 | bytes 4194304 | tf_op jit(solution)/shard_map/dot_general | solution.py:26
  55.4 2.2 %multiply_convert_fusion.3 = f16[1024,512]{1,0:T(8,128)(2,1)} fusion(bf16[1024,1024]{1,0:T(8,128)(2,1)S(1)} %bitcast.21, bf16[512,512]{1,0:T(8,128)(2,1)S(1)} %copy-done.17, bf16[512,512]{1,0:T(8,128)(2,1)S(1)} %copy-done.14), kind=kOutput, calls=%fused_computation.8 | convolution fusion | flops 1076887552 | bytes 4194304 | tf_op jit(solution)/shard_map/dot_general | solution.py:26
  57.7 2.2 %multiply_convert_fusion.2 = f16[1024,512]{1,0:T(8,128)(2,1)} fusion(bf16[1024,1024]{1,0:T(8,128)(2,1)S(1)} %bitcast.22, bf16[512,512]{1,0:T(8,128)(2,1)S(1)} %copy-done.19, bf16[512,512]{1,0:T(8,128)(2,1)S(1)} %copy-done.13), kind=kOutput, calls=%fused_computation.7 | convolution fusion | flops 1076887552 | bytes 4194304 | tf_op jit(solution)/shard_map/dot_general | solution.py:26
  59.9 3.8 %collective-permute-start.15 = (f16[1024,512]{1,0:T(8,128)(2,1)}, f16[1024,512]{1,0:T(8,128)(2,1)}, u32[]{:S(2)}, u32[]{:S(2)}) collective-permute-start(f16[1024,512]{1,0:T(8,128)(2,1)} %multiply_convert_fusion.2), channel_id=1, source_target_pairs={{0,3},{1,0},{2,1},{3,2},{4,7},{5,4},{6,5},{7,6},{8,11},{9,8},{10,9... | collective-permute-start | bytes 3145736 | tf_op jit(solution)/shard_map/ppermute | solution.py:18
  63.7 1.3 collective-permute-start.13
  64.9 1.4 collective-permute-start
  66.4 2.4 %collective-permute-start.1 = (bf16[128,768]{1,0:T(8,128)(2,1)}, bf16[128,768]{1,0:T(8,128)(2,1)S(1)}, u32[]{:S(2)}, u32[]{:S(2)}) collective-permute-start(bf16[128,768]{1,0:T(8,128)(2,1)} %get-tuple-element.28), channel_id=1, source_target_pairs={{0,32},{16,48},{32,64},{48,80},{64,96},{80,112},{96,0},{112,16},{1... | collective-permute-start | bytes 589832 | tf_op jit(solution)/shard_map/ppermute | solution.py:18
  68.8 2.6 %fusion.4 = f32[1024,512]{1,0:T(8,128)} fusion(bf16[1024,1024]{1,0:T(8,128)(2,1)S(1)} %bitcast.23, bf16[512,512]{1,0:T(8,128)(2,1)S(1)} %copy-done.12, bf16[512,512]{1,0:T(8,128)(2,1)S(1)} %copy-done.10), kind=kOutput, calls=%fused_computation.12 | convolution fusion | flops 1075838976 | bytes 5242880 | tf_op jit(solution)/shard_map/dot_general | solution.py:26
  71.4 8.5 %all-to-all-done.1 = f16[8,128,1024]{2,1,0:T(8,128)(2,1)S(1)} async-done(((f16[8,128,1024]{2,1,0:T(8,128)(2,1)}), f16[8,128,1024]{2,1,0:T(8,128)(2,1)S(1)}, u32[]{:S(2)}, u32[]{:S(2)}) %all-to-all-start.1) | async-done | bytes 2097184 | tf_op jit(solution)/shard_map/all_to_all | solution.py:152
  79.9 0.5 convert_reduce_fusion
  80.4 0.8 broadcast_multiply_fusion
  81.3 4.9 %collective-permute-done.15 = f16[1024,512]{1,0:T(8,128)(2,1)} collective-permute-done((f16[1024,512]{1,0:T(8,128)(2,1)}, f16[1024,512]{1,0:T(8,128)(2,1)}, u32[]{:S(2)}, u32[]{:S(2)}) %collective-permute-start.15) | collective-permute-done | bytes 1048608 | tf_op jit(solution)/shard_map/ppermute | solution.py:18
  86.1 2.8 %collective-permute-done.14 = f16[1024,512]{1,0:T(8,128)(2,1)} collective-permute-done((f16[1024,512]{1,0:T(8,128)(2,1)}, f16[1024,512]{1,0:T(8,128)(2,1)}, u32[]{:S(2)}, u32[]{:S(2)}) %collective-permute-start.14) | collective-permute-done | bytes 1048608 | tf_op jit(solution)/shard_map/ppermute | solution.py:18
  88.9 19.7 %collective-permute-done.13 = f16[1024,512]{1,0:T(8,128)(2,1)} collective-permute-done((f16[1024,512]{1,0:T(8,128)(2,1)}, f16[1024,512]{1,0:T(8,128)(2,1)}, u32[]{:S(2)}, u32[]{:S(2)}) %collective-permute-start.13) | collective-permute-done | bytes 1048608 | tf_op jit(solution)/shard_map/ppermute | solution.py:18
  108.6 3.6 %multiply_convert_fusion.1 = f16[1024,512]{1,0:T(8,128)(2,1)} fusion(f32[1024,512]{1,0:T(8,128)S(1)} %copy-done.3, f16[1024,512]{1,0:T(8,128)(2,1)} %collective-permute-done.15, f16[1024,512]{1,0:T(8,128)(2,1)} %collective-permute-done.14, f16[1024,512]{1,0:T(8,128)(2,1)} %collective-permute-done.13), kind=kLoop, calls=%fused_computation.6 | loop fusion | flops 4718592 | bytes 6291456 | tf_op jit(solution)/shard_map/convert_element_type | solution.py:199
  112.2 6.5 %all-to-all-start.2 = ((f16[16,64,512]{2,1,0:T(8,128)(2,1)}), f16[16,64,512]{2,1,0:T(8,128)(2,1)S(1)}, u32[]{:S(2)}, u32[]{:S(2)}) async-start(f16[16,64,512]{2,1,0:T(8,128)(2,1)} %bitcast.6), calls=%async_computation.2 | async-start | bytes 2097152 | tf_op jit(solution)/shard_map/all_to_all | solution.py:152
  118.7 2.6 %collective-permute-start.2 = (bf16[128,768]{1,0:T(8,128)(2,1)}, bf16[128,768]{1,0:T(8,128)(2,1)}, u32[]{:S(2)}, u32[]{:S(2)}) collective-permute-start(bf16[128,768]{1,0:T(8,128)(2,1)} %get-tuple-element.29), channel_id=1, source_target_pairs={{0,48},{16,64},{32,80},{48,96},{64,112},{80,0},{96,16},{112,32},{1... | collective-permute-start | bytes 589832 | tf_op jit(solution)/shard_map/ppermute | solution.py:18
  121.4 2.7 %collective-permute-start.3 = (bf16[128,768]{1,0:T(8,128)(2,1)}, bf16[128,768]{1,0:T(8,128)(2,1)}, u32[]{:S(2)}, u32[]{:S(2)}) collective-permute-start(bf16[128,768]{1,0:T(8,128)(2,1)} %get-tuple-element.30), channel_id=1, source_target_pairs={{0,64},{16,80},{32,96},{48,112},{64,0},{80,16},{96,32},{112,48},{1... | collective-permute-start | bytes 589832 | tf_op jit(solution)/shard_map/ppermute | solution.py:18
  124.0 1.5 collective-permute-start.4
  125.5 2.7 %collective-permute-start.5 = (bf16[128,768]{1,0:T(8,128)(2,1)}, bf16[128,768]{1,0:T(8,128)(2,1)}, u32[]{:S(2)}, u32[]{:S(2)}) collective-permute-start(bf16[128,768]{1,0:T(8,128)(2,1)} %get-tuple-element.32), channel_id=1, source_target_pairs={{0,96},{16,112},{32,0},{48,16},{64,32},{80,48},{96,64},{112,80},{1... | collective-permute-start | bytes 589832 | tf_op jit(solution)/shard_map/ppermute | solution.py:18
  128.2 0.9 collective-permute-start.6
  129.1 6.4 %collective-permute-done.2.refs_3_ = bf16[128,768]{1,0:T(8,128)(2,1)} collective-permute-done((bf16[128,768]{1,0:T(8,128)(2,1)}, bf16[128,768]{1,0:T(8,128)(2,1)}, u32[]{:S(2)}, u32[]{:S(2)}) %collective-permute-start.2) | collective-permute-done | bytes 196640 | tf_op jit(solution)/shard_map/ppermute | solution.py:18
  135.5 1.9 %collective-permute-done.3.refs_4_ = bf16[128,768]{1,0:T(8,128)(2,1)} collective-permute-done((bf16[128,768]{1,0:T(8,128)(2,1)}, bf16[128,768]{1,0:T(8,128)(2,1)}, u32[]{:S(2)}, u32[]{:S(2)}) %collective-permute-start.3) | collective-permute-done | bytes 196640 | tf_op jit(solution)/shard_map/ppermute | solution.py:18
  137.3 1.3 collective-permute-done.5.refs_6_
  138.7 3.0 %collective-permute-done.6.refs_7_ = bf16[128,768]{1,0:T(8,128)(2,1)} collective-permute-done((bf16[128,768]{1,0:T(8,128)(2,1)}, bf16[128,768]{1,0:T(8,128)(2,1)}, u32[]{:S(2)}, u32[]{:S(2)}) %collective-permute-start.6) | collective-permute-done | bytes 196640 | tf_op jit(solution)/shard_map/ppermute | solution.py:18
  141.7 3.4 %shard_map.95 = bf16[8,128,768]{2,1,0:T(8,128)(2,1)} custom-call(s32[3]{0:T(128)} %pad_add_fusion.where, bf16[128,768]{1,0:T(8,128)(2,1)} %get-tuple-element.26.refs_0_, bf16[128,768]{1,0:T(8,128)(2,1)} %copy-done.6, bf16[128,768]{1,0:T(8,128)(2,1)} %copy-done.7, bf16[128,768]{1,0:T(8,128)(2,1)} %collective-permute-done.2.refs_3_, ...), custom_call_target="tpu_custom_call" | custom-call | tf_op jit(solution)/shard_map/pallas_call | solution.py:138
  145.1 3.0 %fusion.17 = f32[512,512]{1,0:T(8,128)} fusion(bf16[1024,1024]{1,0:T(8,128)(2,1)S(1)} %bitcast.24, bf16[1024,768]{1,0:T(8,128)(2,1)} %bitcast.26), kind=kOutput, calls=%fused_computation.25 | convolution fusion | flops 536870912 | bytes 3145728 | tf_op jit(solution)/shard_map/dot_general | solution.py:148
  148.1 6.3 %collective-permute-start.12 = (f32[512,512]{1,0:T(8,128)}, f32[512,512]{1,0:T(8,128)}, u32[]{:S(2)}, u32[]{:S(2)}) collective-permute-start(f32[512,512]{1,0:T(8,128)} %fusion.17), channel_id=1, source_target_pairs={{0,8},{8,0},{1,9},{9,1},{2,10},{10,2},{3,11},{11,3},{4,12},{12,4},... | collective-permute-start | bytes 3145736 | tf_op jit(solution)/shard_map/ppermute | solution.py:22
  154.4 0.1 constant_dynamic-slice_fusion.7
  154.5 0.7 pad_maximum_fusion.1
  155.2 0.7 pad_maximum_fusion.2
  155.8 2.7 %collective-permute-start.18 = (f32[128,256]{1,0:T(8,128)}, f32[128,256]{1,0:T(8,128)S(1)}, u32[]{:S(2)}, u32[]{:S(2)}) collective-permute-start(f32[128,256]{1,0:T(8,128)} %pad_maximum_fusion.2), channel_id=1, source_target_pairs={{0,3},{1,0},{2,1},{3,2},{4,7},{5,4},{6,5},{7,6},{8,11},{9,8},{10,9... | collective-permute-start | bytes 393224 | tf_op jit(solution)/shard_map/ppermute | solution.py:18
  158.5 0.7 pad_maximum_fusion
  159.2 0.1 collective-permute-start.16
  159.3 0.1 convert_reduce_fusion.1
  159.5 0.9 broadcast_in_dim.2
  160.3 9.3 %all-to-all-start.3 = ((bf16[16,64,256]{2,1,0:T(8,128)(2,1)}), bf16[16,64,256]{2,1,0:T(8,128)(2,1)}, u32[]{:S(2)}, u32[]{:S(2)}) async-start(bf16[16,64,256]{2,1,0:T(8,128)(2,1)} %bitcast.9), calls=%async_computation.3 | async-start | bytes 1048576 | tf_op jit(solution)/shard_map/all_to_all | solution.py:152
  169.7 3.2 %fusion.3 = f32[512,512]{1,0:T(8,128)} fusion(f32[512,512]{1,0:T(8,128)} %collective-permute-done.12, f32[512,512]{1,0:T(8,128)S(1)} %copy-done.5, bf16[1024,1024]{1,0:T(8,128)(2,1)S(1)} %bitcast.25, bf16[1024,768]{1,0:T(8,128)(2,1)} %bitcast.27), kind=kOutput, calls=%fused_computation.11 | convolution fusion | flops 537395200 | bytes 5242880 | tf_op jit(solution)/shard_map/dot_general | solution.py:148
  172.9 0.9 constant_dynamic-slice_fusion.9
  173.9 1.4 collective-permute-start.19
  175.3 4.6 %all-to-all-done.3 = bf16[16,64,256]{2,1,0:T(8,128)(2,1)} async-done(((bf16[16,64,256]{2,1,0:T(8,128)(2,1)}), bf16[16,64,256]{2,1,0:T(8,128)(2,1)}, u32[]{:S(2)}, u32[]{:S(2)}) %all-to-all-start.3) | async-done | bytes 524320 | tf_op jit(solution)/shard_map/all_to_all | solution.py:152
  179.9 1.5 fusion.22
  181.5 2.4 %collective-permute-start.20 = (f32[128,256]{1,0:T(8,128)S(1)}, f32[128,256]{1,0:T(8,128)S(1)}, u32[]{:S(2)}, u32[]{:S(2)}) collective-permute-start(f32[128,256]{1,0:T(8,128)S(1)} %constant_dynamic-slice_fusion), channel_id=1, source_target_pairs={{0,8},{8,0},{1,9},{9,1},{2,10},{10,2},{3,11},{11,3},{4,12},{12,4},... | collective-permute-start | bytes 393224 | tf_op jit(solution)/shard_map/ppermute | solution.py:22
  183.8 0.6 dynamic-slice_add_fusion
  184.5 0.3 collective-permute-done.20
  184.8 0.7 add_add_fusion
  (58 shorter events, 0.2 us)
Async XLA Ops:
  4.6 7.6 %copy-start.9 = (bf16[512,1024]{1,0:T(8,128)(2,1)S(1)}, bf16[512,1024]{1,0:T(8,128)(2,1)}, u32[]{:S(2)}) copy-start(bf16[512,1024]{1,0:T(8,128)(2,1)} %param.9) | copy-start | bytes 3145732
  4.6 36.2 %all-to-all-start = ((bf16[8,128,1024]{2,1,0:T(8,128)(2,1)}), bf16[8,128,1024]{2,1,0:T(8,128)(2,1)S(1)}, u32[]{:S(2)}, u32[]{:S(2)}) async-start(bf16[8,128,1024]{2,1,0:T(8,128)(2,1)} %shard_map.96), calls=%async_computation | async-start | bytes 4194304 | tf_op jit(solution)/shard_map/all_to_all | solution.py:152
  12.2 10.7 %collective-permute-start.7 = (bf16[512,1024]{1,0:T(8,128)(2,1)S(1)}, bf16[512,1024]{1,0:T(8,128)(2,1)}, u32[]{:S(2)}, u32[]{:S(2)}) collective-permute-start(bf16[512,1024]{1,0:T(8,128)(2,1)S(1)} %copy-done.9), channel_id=1, source_target_pairs={{0,8},{8,0},{1,9},{9,1},{2,10},{10,2},{3,11},{11,3},{4,12},{12,4},... | collective-permute-start | bytes 3145736 | tf_op jit(solution)/shard_map/ppermute | solution.py:22
  17.5 2.2 %collective-permute-start.8 = (bf16[512,512]{1,0:T(8,128)(2,1)}, bf16[512,512]{1,0:T(8,128)(2,1)S(1)}, u32[]{:S(2)}, u32[]{:S(2)}) collective-permute-start(bf16[512,512]{1,0:T(8,128)(2,1)} %get-tuple-element.34), channel_id=1, source_target_pairs={{0,8},{8,0},{1,9},{9,1},{2,10},{10,2},{3,11},{11,3},{4,12},{12,4},... | collective-permute-start | bytes 1572872 | tf_op jit(solution)/shard_map/ppermute | solution.py:22
  17.6 2.8 %collective-permute-start.9 = (bf16[512,512]{1,0:T(8,128)(2,1)}, bf16[512,512]{1,0:T(8,128)(2,1)S(1)}, u32[]{:S(2)}, u32[]{:S(2)}) collective-permute-start(bf16[512,512]{1,0:T(8,128)(2,1)} %get-tuple-element.35), channel_id=1, source_target_pairs={{0,8},{8,0},{1,9},{9,1},{2,10},{10,2},{3,11},{11,3},{4,12},{12,4},... | collective-permute-start | bytes 1572872 | tf_op jit(solution)/shard_map/ppermute | solution.py:22
  18.1 3.1 %collective-permute-start.10 = (bf16[512,512]{1,0:T(8,128)(2,1)}, bf16[512,512]{1,0:T(8,128)(2,1)S(1)}, u32[]{:S(2)}, u32[]{:S(2)}) collective-permute-start(bf16[512,512]{1,0:T(8,128)(2,1)} %get-tuple-element.36), channel_id=1, source_target_pairs={{0,8},{8,0},{1,9},{9,1},{2,10},{10,2},{3,11},{11,3},{4,12},{12,4},... | collective-permute-start | bytes 1572872 | tf_op jit(solution)/shard_map/ppermute | solution.py:22
  18.2 3.8 %collective-permute-start.11 = (bf16[512,512]{1,0:T(8,128)(2,1)}, bf16[512,512]{1,0:T(8,128)(2,1)S(1)}, u32[]{:S(2)}, u32[]{:S(2)}) collective-permute-start(bf16[512,512]{1,0:T(8,128)(2,1)} %get-tuple-element.37), channel_id=1, source_target_pairs={{0,8},{8,0},{1,9},{9,1},{2,10},{10,2},{3,11},{11,3},{4,12},{12,4},... | collective-permute-start | bytes 1572872 | tf_op jit(solution)/shard_map/ppermute | solution.py:22
  19.7 2.3 %copy-start.11 = (bf16[512,512]{1,0:T(8,128)(2,1)}, bf16[512,512]{1,0:T(8,128)(2,1)S(1)}, u32[]{:S(2)}) copy-start(bf16[512,512]{1,0:T(8,128)(2,1)S(1)} %collective-permute-done.8) | copy-start | bytes 1572868
  20.5 1.5 copy-start.16
  21.2 0.8 copy-start.20
  22.0 0.9 copy-start.18
  40.8 5.7 %copy-start = (bf16[8,128,1024]{2,1,0:T(8,128)(2,1)}, bf16[8,128,1024]{2,1,0:T(8,128)(2,1)S(1)}, u32[]{:S(2)}) copy-start(bf16[8,128,1024]{2,1,0:T(8,128)(2,1)S(1)} %all-to-all-done) | copy-start | bytes 6291460
  46.5 4.8 %copy-start.15 = (bf16[512,512]{1,0:T(8,128)(2,1)S(1)}, bf16[512,512]{1,0:T(8,128)(2,1)}, u32[]{:S(2)}) copy-start(bf16[512,512]{1,0:T(8,128)(2,1)} %get-tuple-element.36) | copy-start | bytes 1572868
  46.5 33.4 %all-to-all-start.1 = ((f16[8,128,1024]{2,1,0:T(8,128)(2,1)}), f16[8,128,1024]{2,1,0:T(8,128)(2,1)S(1)}, u32[]{:S(2)}, u32[]{:S(2)}) async-start(f16[8,128,1024]{2,1,0:T(8,128)(2,1)} %bitcast.29), calls=%async_computation.1 | async-start | bytes 4194304 | tf_op jit(solution)/shard_map/all_to_all | solution.py:152
  51.3 4.1 %copy-start.1 = (bf16[8,128,1024]{2,1,0:T(8,128)(2,1)S(1)}, bf16[8,128,1024]{2,1,0:T(8,128)(2,1)}, u32[]{:S(2)}) copy-start(bf16[8,128,1024]{2,1,0:T(8,128)(2,1)} %copy-done) | copy-start | bytes 6291460
  51.3 4.1 %copy-start.14 = (bf16[512,512]{1,0:T(8,128)(2,1)S(1)}, bf16[512,512]{1,0:T(8,128)(2,1)}, u32[]{:S(2)}) copy-start(bf16[512,512]{1,0:T(8,128)(2,1)} %get-tuple-element.35) | copy-start | bytes 1572868
  51.3 4.1 %copy-start.17 = (bf16[512,512]{1,0:T(8,128)(2,1)S(1)}, bf16[512,512]{1,0:T(8,128)(2,1)}, u32[]{:S(2)}) copy-start(bf16[512,512]{1,0:T(8,128)(2,1)} %copy-done.16) | copy-start | bytes 1572868
  55.4 2.3 %copy-start.13 = (bf16[512,512]{1,0:T(8,128)(2,1)S(1)}, bf16[512,512]{1,0:T(8,128)(2,1)}, u32[]{:S(2)}) copy-start(bf16[512,512]{1,0:T(8,128)(2,1)} %get-tuple-element.37) | copy-start | bytes 1572868
  55.4 2.3 %copy-start.19 = (bf16[512,512]{1,0:T(8,128)(2,1)S(1)}, bf16[512,512]{1,0:T(8,128)(2,1)}, u32[]{:S(2)}) copy-start(bf16[512,512]{1,0:T(8,128)(2,1)} %copy-done.18) | copy-start | bytes 1572868
  57.7 11.1 %copy-start.10 = (bf16[512,512]{1,0:T(8,128)(2,1)S(1)}, bf16[512,512]{1,0:T(8,128)(2,1)}, u32[]{:S(2)}) copy-start(bf16[512,512]{1,0:T(8,128)(2,1)} %get-tuple-element.34) | copy-start | bytes 1572868
  57.7 11.1 %copy-start.12 = (bf16[512,512]{1,0:T(8,128)(2,1)S(1)}, bf16[512,512]{1,0:T(8,128)(2,1)}, u32[]{:S(2)}) copy-start(bf16[512,512]{1,0:T(8,128)(2,1)} %copy-done.11) | copy-start | bytes 1572868
  59.9 26.2 %collective-permute-start.15 = (f16[1024,512]{1,0:T(8,128)(2,1)}, f16[1024,512]{1,0:T(8,128)(2,1)}, u32[]{:S(2)}, u32[]{:S(2)}) collective-permute-start(f16[1024,512]{1,0:T(8,128)(2,1)} %multiply_convert_fusion.2), channel_id=1, source_target_pairs={{0,3},{1,0},{2,1},{3,2},{4,7},{5,4},{6,5},{7,6},{8,11},{9,8},{10,9... | collective-permute-start | bytes 3145736 | tf_op jit(solution)/shard_map/ppermute | solution.py:18
  63.7 25.3 %collective-permute-start.14 = (f16[1024,512]{1,0:T(8,128)(2,1)}, f16[1024,512]{1,0:T(8,128)(2,1)}, u32[]{:S(2)}, u32[]{:S(2)}) collective-permute-start(f16[1024,512]{1,0:T(8,128)(2,1)} %multiply_convert_fusion.3), channel_id=1, source_target_pairs={{0,1},{1,2},{2,3},{3,0},{4,5},{5,6},{6,7},{7,4},{8,9},{9,10},{10,1... | collective-permute-start | bytes 3145736 | tf_op jit(solution)/shard_map/ppermute | solution.py:18
  63.7 44.9 %collective-permute-start.13 = (f16[1024,512]{1,0:T(8,128)(2,1)}, f16[1024,512]{1,0:T(8,128)(2,1)}, u32[]{:S(2)}, u32[]{:S(2)}) collective-permute-start(f16[1024,512]{1,0:T(8,128)(2,1)} %multiply_convert_fusion.4), channel_id=1, source_target_pairs={{0,2},{1,3},{2,0},{3,1},{4,6},{5,7},{6,4},{7,5},{8,10},{9,11},{10,... | collective-permute-start | bytes 3145736 | tf_op jit(solution)/shard_map/ppermute | solution.py:18
  64.9 60.6 %collective-permute-start = (bf16[128,768]{1,0:T(8,128)(2,1)}, bf16[128,768]{1,0:T(8,128)(2,1)S(1)}, u32[]{:S(2)}, u32[]{:S(2)}) collective-permute-start(bf16[128,768]{1,0:T(8,128)(2,1)} %get-tuple-element.27), channel_id=1, source_target_pairs={{0,16},{16,32},{32,48},{48,64},{64,80},{80,96},{96,112},{112,0},{1... | collective-permute-start | bytes 589832 | tf_op jit(solution)/shard_map/ppermute | solution.py:18
  66.4 61.8 %collective-permute-start.1 = (bf16[128,768]{1,0:T(8,128)(2,1)}, bf16[128,768]{1,0:T(8,128)(2,1)S(1)}, u32[]{:S(2)}, u32[]{:S(2)}) collective-permute-start(bf16[128,768]{1,0:T(8,128)(2,1)} %get-tuple-element.28), channel_id=1, source_target_pairs={{0,32},{16,48},{32,64},{48,80},{64,96},{80,112},{96,0},{112,16},{1... | collective-permute-start | bytes 589832 | tf_op jit(solution)/shard_map/ppermute | solution.py:18
  79.9 28.7 %copy-start.3 = (f32[1024,512]{1,0:T(8,128)S(1)}, f32[1024,512]{1,0:T(8,128)}, u32[]{:S(2)}) copy-start(f32[1024,512]{1,0:T(8,128)} %fusion.4) | copy-start | bytes 6291460
  112.2 47.0 %all-to-all-start.2 = ((f16[16,64,512]{2,1,0:T(8,128)(2,1)}), f16[16,64,512]{2,1,0:T(8,128)(2,1)S(1)}, u32[]{:S(2)}, u32[]{:S(2)}) async-start(f16[16,64,512]{2,1,0:T(8,128)(2,1)} %bitcast.6), calls=%async_computation.2 | async-start | bytes 2097152 | tf_op jit(solution)/shard_map/all_to_all | solution.py:152
  118.7 26.4 %copy-start.2 = (bf16[8,128,1024]{2,1,0:T(8,128)(2,1)S(1)}, bf16[8,128,1024]{2,1,0:T(8,128)(2,1)}, u32[]{:S(2)}) copy-start(bf16[8,128,1024]{2,1,0:T(8,128)(2,1)} %copy-done) | copy-start | bytes 6291460
  118.7 16.8 %collective-permute-start.2 = (bf16[128,768]{1,0:T(8,128)(2,1)}, bf16[128,768]{1,0:T(8,128)(2,1)}, u32[]{:S(2)}, u32[]{:S(2)}) collective-permute-start(bf16[128,768]{1,0:T(8,128)(2,1)} %get-tuple-element.29), channel_id=1, source_target_pairs={{0,48},{16,64},{32,80},{48,96},{64,112},{80,0},{96,16},{112,32},{1... | collective-permute-start | bytes 589832 | tf_op jit(solution)/shard_map/ppermute | solution.py:18
  121.4 16.0 %collective-permute-start.3 = (bf16[128,768]{1,0:T(8,128)(2,1)}, bf16[128,768]{1,0:T(8,128)(2,1)}, u32[]{:S(2)}, u32[]{:S(2)}) collective-permute-start(bf16[128,768]{1,0:T(8,128)(2,1)} %get-tuple-element.30), channel_id=1, source_target_pairs={{0,64},{16,80},{32,96},{48,112},{64,0},{80,16},{96,32},{112,48},{1... | collective-permute-start | bytes 589832 | tf_op jit(solution)/shard_map/ppermute | solution.py:18
  124.0 13.3 %collective-permute-start.4 = (bf16[128,768]{1,0:T(8,128)(2,1)}, bf16[128,768]{1,0:T(8,128)(2,1)}, u32[]{:S(2)}, u32[]{:S(2)}) collective-permute-start(bf16[128,768]{1,0:T(8,128)(2,1)} %get-tuple-element.31), channel_id=1, source_target_pairs={{0,80},{16,96},{32,112},{48,0},{64,16},{80,32},{96,48},{112,64},{1... | collective-permute-start | bytes 589832 | tf_op jit(solution)/shard_map/ppermute | solution.py:18
  125.5 16.2 %copy-start.6 = (bf16[128,768]{1,0:T(8,128)(2,1)}, bf16[128,768]{1,0:T(8,128)(2,1)S(1)}, u32[]{:S(2)}) copy-start(bf16[128,768]{1,0:T(8,128)(2,1)S(1)} %collective-permute-done.refs_1_) | copy-start | bytes 589828
  125.5 13.1 %collective-permute-start.5 = (bf16[128,768]{1,0:T(8,128)(2,1)}, bf16[128,768]{1,0:T(8,128)(2,1)}, u32[]{:S(2)}, u32[]{:S(2)}) collective-permute-start(bf16[128,768]{1,0:T(8,128)(2,1)} %get-tuple-element.32), channel_id=1, source_target_pairs={{0,96},{16,112},{32,0},{48,16},{64,32},{80,48},{96,64},{112,80},{1... | collective-permute-start | bytes 589832 | tf_op jit(solution)/shard_map/ppermute | solution.py:18
  128.2 13.5 %copy-start.7 = (bf16[128,768]{1,0:T(8,128)(2,1)}, bf16[128,768]{1,0:T(8,128)(2,1)S(1)}, u32[]{:S(2)}) copy-start(bf16[128,768]{1,0:T(8,128)(2,1)S(1)} %collective-permute-done.1.refs_2_) | copy-start | bytes 589828
  128.2 13.5 %collective-permute-start.6 = (bf16[128,768]{1,0:T(8,128)(2,1)}, bf16[128,768]{1,0:T(8,128)(2,1)}, u32[]{:S(2)}, u32[]{:S(2)}) collective-permute-start(bf16[128,768]{1,0:T(8,128)(2,1)} %get-tuple-element.33), channel_id=1, source_target_pairs={{0,112},{16,0},{32,16},{48,32},{64,48},{80,64},{96,80},{112,96},{1... | collective-permute-start | bytes 589832 | tf_op jit(solution)/shard_map/ppermute | solution.py:18
  145.1 9.3 %copy-start.4 = (f32[128,1024]{1,0:T(8,128)S(1)}, f32[128,1024]{1,0:T(8,128)}, u32[]{:S(2)}) copy-start(f32[128,1024]{1,0:T(8,128)} %broadcast_multiply_fusion) | copy-start | bytes 1572868
  148.1 21.6 %collective-permute-start.12 = (f32[512,512]{1,0:T(8,128)}, f32[512,512]{1,0:T(8,128)}, u32[]{:S(2)}, u32[]{:S(2)}) collective-permute-start(f32[512,512]{1,0:T(8,128)} %fusion.17), channel_id=1, source_target_pairs={{0,8},{8,0},{1,9},{9,1},{2,10},{10,2},{3,11},{11,3},{4,12},{12,4},... | collective-permute-start | bytes 3145736 | tf_op jit(solution)/shard_map/ppermute | solution.py:22
  155.2 18.7 %collective-permute-start.17 = (f32[128,256]{1,0:T(8,128)}, f32[128,256]{1,0:T(8,128)S(1)}, u32[]{:S(2)}, u32[]{:S(2)}) collective-permute-start(f32[128,256]{1,0:T(8,128)} %pad_maximum_fusion.1), channel_id=1, source_target_pairs={{0,1},{1,2},{2,3},{3,0},{4,5},{5,6},{6,7},{7,4},{8,9},{9,10},{10,1... | collective-permute-start | bytes 393224 | tf_op jit(solution)/shard_map/ppermute | solution.py:18
  155.8 18.0 %collective-permute-start.18 = (f32[128,256]{1,0:T(8,128)}, f32[128,256]{1,0:T(8,128)S(1)}, u32[]{:S(2)}, u32[]{:S(2)}) collective-permute-start(f32[128,256]{1,0:T(8,128)} %pad_maximum_fusion.2), channel_id=1, source_target_pairs={{0,3},{1,0},{2,1},{3,2},{4,7},{5,4},{6,5},{7,6},{8,11},{9,8},{10,9... | collective-permute-start | bytes 393224 | tf_op jit(solution)/shard_map/ppermute | solution.py:18
  159.2 14.7 %collective-permute-start.16 = (f32[128,256]{1,0:T(8,128)}, f32[128,256]{1,0:T(8,128)S(1)}, u32[]{:S(2)}, u32[]{:S(2)}) collective-permute-start(f32[128,256]{1,0:T(8,128)} %pad_maximum_fusion), channel_id=1, source_target_pairs={{0,2},{1,3},{2,0},{3,1},{4,6},{5,7},{6,4},{7,5},{8,10},{9,11},{10,... | collective-permute-start | bytes 393224 | tf_op jit(solution)/shard_map/ppermute | solution.py:18
  159.4 10.3 %copy-start.5 = (f32[512,512]{1,0:T(8,128)S(1)}, f32[512,512]{1,0:T(8,128)}, u32[]{:S(2)}) copy-start(f32[512,512]{1,0:T(8,128)} %param.12) | copy-start | bytes 3145732
  160.3 19.5 %all-to-all-start.3 = ((bf16[16,64,256]{2,1,0:T(8,128)(2,1)}), bf16[16,64,256]{2,1,0:T(8,128)(2,1)}, u32[]{:S(2)}, u32[]{:S(2)}) async-start(bf16[16,64,256]{2,1,0:T(8,128)(2,1)} %bitcast.9), calls=%async_computation.3 | async-start | bytes 1048576 | tf_op jit(solution)/shard_map/all_to_all | solution.py:152
  172.9 11.9 %copy-start.8 = (f32[128,256]{1,0:T(8,128)S(1)}, f32[128,256]{1,0:T(8,128)}, u32[]{:S(2)}) copy-start(f32[128,256]{1,0:T(8,128)} %param.13) | copy-start | bytes 393220
  173.9 9.9 %collective-permute-start.19 = (f32[128,128]{1,0:T(8,128)S(1)}, f32[128,128]{1,0:T(8,128)S(1)}, u32[]{:S(2)}, u32[]{:S(2)}) collective-permute-start(f32[128,128]{1,0:T(8,128)S(1)} %constant_dynamic-slice_fusion.1), channel_id=1, source_target_pairs={{0,4},{4,0},{1,5},{5,1},{2,6},{6,2},{3,7},{7,3},{8,12},{12,8},{9,1... | collective-permute-start | bytes 196616 | tf_op jit(solution)/shard_map/ppermute | solution.py:22
  181.5 3.3 %collective-permute-start.20 = (f32[128,256]{1,0:T(8,128)S(1)}, f32[128,256]{1,0:T(8,128)S(1)}, u32[]{:S(2)}, u32[]{:S(2)}) collective-permute-start(f32[128,256]{1,0:T(8,128)S(1)} %constant_dynamic-slice_fusion), channel_id=1, source_target_pairs={{0,8},{8,0},{1,9},{9,1},{2,10},{10,2},{3,11},{11,3},{4,12},{12,4},... | collective-permute-start | bytes 393224 | tf_op jit(solution)/shard_map/ppermute | solution.py:22
